TPU v7x, 256 devices: a whole 4x4x8 slice. The times are simulated.
256 devices in a mesh: seq: 32 (over z, x), heads: 8 (over y, core).
Axes of the slice: x: 4, y: 4, z: 8, core: 2. Of those that a mesh axis runs over, the one named last changes fastest.
Arguments:
- lin_q: bfloat16 [8192, 8192], P('seq', 'heads'), may hold values from -4 to 4
- lin_k: bfloat16 [8192, 8192], P('seq', 'heads'), may hold values from -4 to 4
- lin_v: bfloat16 [8192, 8192], P('seq', 'heads'), may hold values from -6 to 6
- decay_rates: float32 [64], P('heads'), may hold values from 3.0517578e-05 to 0.03125
- norm_gain: float32 [8192], P('heads'), may hold values from 0.25 to 1.75
- soft_q: bfloat16 [8192, 8192], P('seq', 'heads'), may hold values from -8 to 8
- soft_k: bfloat16 [8192, 1024], P('seq', 'heads'), may hold values from -8 to 8
- soft_v: bfloat16 [8192, 1024], P('seq', 'heads'), may hold values from -6 to 6
- segment_ids: int32 [8192], P('seq'), may hold values from 0 to 3, never falling along the last dimension, each value on 1 to 6144 neighbouring positions
Outputs:
- lin_out: bfloat16 [8192, 8192], P('seq', 'heads')
- soft_out: bfloat16 [8192, 8192], P('seq', 'heads')
Inputs may be any that keep to these rules, and one draw needn't show every extreme that they name: `segment_ids`: never falling along the sequence; each document has 1 to 6144 tokens, one exactly that many.
All inputs are finite; a program needn't handle non-finite values.
Results may differ from a plain program's by a relative error of at most 0.0049.
Values may be sent and summed in bfloat16 or wider, within the bound.
A program may use at most 128 MiB of HBM per device.

v0:
```python
from functools import partial
import math

import jax
import jax.numpy as jnp
from jax import lax
from jax.sharding import PartitionSpec as P

BLOCK = 256


def carried_in(part, axis, combine, identity):
    place = lax.axis_index(axis)
    gathered = jax.tree.map(lambda a: lax.all_gather(a, axis), part)
    state = jax.tree.map(lambda a, e: jnp.zeros_like(a) + jnp.asarray(e, a.dtype), part, identity)

    def carried_one(step, state):
        return combine(
            state, jax.tree.map(lambda a: lax.dynamic_index_in_dim(a, step, 0, False), gathered)
        )

    return lax.fori_loop(0, place, carried_one, state)


def light_block(carry, inputs, rates):
    state, last_prev = carry
    q_blk, k_blk, v_blk, seg_blk = inputs
    size = q_blk.shape[0]
    seg_f = seg_blk.astype(jnp.float32)
    pos = jnp.arange(size).astype(jnp.float32)
    diff = pos[:, None] - pos[None, :]
    linked = (diff >= 0.0) & (seg_f[:, None] == seg_f[None, :])
    decay = jnp.exp(-rates[:, None, None] * jnp.maximum(diff, 0.0)[None])
    scores = jnp.einsum("thd,shd->hts", q_blk, k_blk, preferred_element_type=jnp.float32)
    weights = jnp.where(linked[None], scores * decay, 0.0).astype(jnp.bfloat16)
    intra = jnp.einsum("hts,shd->thd", weights, v_blk, preferred_element_type=jnp.float32)
    use = (seg_f == last_prev).astype(jnp.float32)
    coef = jnp.exp(-rates[None, :] * (pos[:, None] + 1.0)) * use[:, None]
    q_state = jnp.einsum(
        "thd,hde->the", q_blk.astype(jnp.float32), state, precision=lax.Precision.HIGHEST
    )
    out = intra + coef[:, :, None] * q_state
    last = seg_f[-1]
    k_weight = (
        jnp.exp(-rates[None, :] * (size - 1.0 - pos[:, None]))
        * (seg_f == last).astype(jnp.float32)[:, None]
    )
    k_dec = (k_blk.astype(jnp.float32) * k_weight[:, :, None]).astype(jnp.bfloat16)
    local = jnp.einsum("shd,she->hde", k_dec, v_blk, preferred_element_type=jnp.float32)
    keep = jnp.where(last == last_prev, 1.0, 0.0) * jnp.exp(-rates * size)
    return ((keep[:, None, None] * state + local, last), out)


def combine_states(earlier, later):
    state_e, dec_e, last_e = earlier
    state_l, dec_l, last_l = later
    match = (last_e == last_l) | (last_l < 0.0)
    factor = jnp.where(match, dec_l, 0.0)
    return (factor[:, None, None] * state_e + state_l, dec_e * dec_l, jnp.maximum(last_e, last_l))


def block_update(inner, queries, qpos, seg_rows, k_blk, v_blk, s_blk, kpos, scale):
    mx, den, acc = inner
    shared_heads = k_blk.shape[1]
    group = queries.shape[2]
    query_count = queries.shape[0]
    key_count = k_blk.shape[0]
    heads = shared_heads * group
    s = (
        jnp.einsum("tgjd,sgd->gjts", queries, k_blk, preferred_element_type=jnp.float32).reshape(
            heads, query_count, key_count
        )
        * scale
    )
    mask = (kpos[None, :] <= qpos[:, None]) & (s_blk[None, :] == seg_rows[:, None])
    top = jnp.max(jnp.where(mask[None], s, -1e30), axis=2)
    new_mx = jnp.maximum(mx, top)
    corr = jnp.exp(mx - new_mx)
    p = jnp.where(mask[None], jnp.exp(s - new_mx[:, :, None]), 0.0)
    den = den * corr + jnp.sum(p, axis=2)
    weights = p.astype(jnp.bfloat16).reshape(shared_heads, group, query_count, key_count)
    mixed = jnp.einsum(
        "gjts,sgd->gjtd", weights, v_blk, preferred_element_type=jnp.float32
    ).reshape(heads, query_count, -1)
    acc = acc * corr[:, :, None] + mixed
    return (new_mx, den, acc)


def body(lin_q, lin_k, lin_v, decay_rates, norm_gain, soft_q, soft_k, soft_v, segment_ids):
    tok = lin_q.shape[0]
    heads = decay_rates.shape[0]
    width = lin_q.shape[1] // heads
    blocks = tok // BLOCK
    shape4 = (blocks, BLOCK, heads, width)
    init = (jnp.zeros((heads, width, width), jnp.float32), jnp.float32(-1.0))
    step_fn = lambda c, x: light_block(c, x, decay_rates)
    (state_loc, last_loc), outs = lax.scan(
        step_fn,
        init,
        (
            lin_q.reshape(shape4),
            lin_k.reshape(shape4),
            lin_v.reshape(shape4),
            segment_ids.reshape(blocks, BLOCK),
        ),
    )
    local_out = outs.reshape(tok, heads, width)
    summary = (state_loc, jnp.exp(-decay_rates * tok), last_loc.reshape(1))
    identity = (
        jnp.zeros((heads, width, width), jnp.float32),
        jnp.ones((heads,), jnp.float32),
        jnp.full((1,), -1.0, jnp.float32),
    )
    state_in, dec_in, last_in = carried_in(summary, "seq", combine_states, identity)
    seg_f = segment_ids.astype(jnp.float32)
    pos = jnp.arange(tok).astype(jnp.float32)
    coef = (
        jnp.exp(-decay_rates[None, :] * (pos[:, None] + 1.0))
        * (seg_f == last_in[0]).astype(jnp.float32)[:, None]
    )
    q_three = lin_q.reshape(tok, heads, width)
    q_state = jnp.einsum(
        "thd,hde->the", q_three.astype(jnp.float32), state_in, precision=lax.Precision.HIGHEST
    )
    raw = (local_out + coef[:, :, None] * q_state).reshape(tok, heads * width)
    sums = jnp.sum(raw * raw, axis=1)
    total_sq = lax.psum(sums, "heads")
    count = lax.axis_size("heads") * heads * width
    lin_out = (raw * lax.rsqrt(total_sq / count + 1e-06)[:, None] * norm_gain[None, :]).astype(
        jnp.bfloat16
    )
    scale = 1.0 / math.sqrt(width)
    shared_heads = soft_k.shape[1] // width
    group = heads // shared_heads
    mine = lax.axis_index("seq")
    plans = (soft_q, segment_ids, mine * tok)
    query_sets = []
    query_rows, seg_rows, first = plans
    count_rows = query_rows.shape[0]
    query_sets.append(
        (
            query_rows.reshape(count_rows, shared_heads, group, width),
            first + jnp.arange(count_rows),
            seg_rows,
            first + count_rows - 1,
        )
    )
    start_carry = tuple(
        (
            (
                jnp.full((heads, qs[0].shape[0]), -1e30, jnp.float32),
                jnp.zeros((heads, qs[0].shape[0]), jnp.float32),
                jnp.zeros((heads, qs[0].shape[0], width), jnp.float32),
            )
            for qs in query_sets
        )
    )
    carry = start_carry
    keys = lax.all_gather(soft_k, "seq", axis=0, tiled=True)
    values = lax.all_gather(soft_v, "seq", axis=0, tiled=True)
    seg_keys = lax.all_gather(segment_ids, "seq", axis=0, tiled=True)
    length = keys.shape[0]
    rows = math.gcd(length, 1024)
    count_blk = length // rows
    k_blocks = keys.reshape(count_blk, rows, shared_heads, width)
    v_blocks = values.reshape(count_blk, rows, shared_heads, width)
    s_blocks = seg_keys.reshape(count_blk, rows)

    def attend_one(state, item):
        k_blk, v_blk, s_blk, index = item
        blk_start = index * rows
        kpos = blk_start + jnp.arange(rows)
        fresh = []
        for query_set, inner in zip(query_sets, state):
            queries, qpos, seg_rows, last_pos = query_set
            update = partial(
                block_update,
                queries=queries,
                qpos=qpos,
                seg_rows=seg_rows,
                k_blk=k_blk,
                v_blk=v_blk,
                s_blk=s_blk,
                kpos=kpos,
                scale=scale,
            )
            inner = update(inner)
            fresh.append(inner)
        return (tuple(fresh), None)

    carry, _ = lax.scan(attend_one, carry, (k_blocks, v_blocks, s_blocks, jnp.arange(count_blk)))
    outputs = []
    for mx, den, acc in carry:
        outputs.append(
            (acc / den[:, :, None])
            .transpose(1, 0, 2)
            .reshape(acc.shape[1], heads * width)
            .astype(jnp.bfloat16)
        )
    soft_out = outputs[0]
    return (lin_out, soft_out)


def solution(mesh):
    placed = (
        P("seq", "heads"),
        P("seq", "heads"),
        P("seq", "heads"),
        P("heads"),
        P("heads"),
        P("seq", "heads"),
        P("seq", "heads"),
        P("seq", "heads"),
        P("seq"),
    )
    return jax.shard_map(
        body,
        mesh=mesh,
        in_specs=placed,
        out_specs=(P("seq", "heads"), P("seq", "heads")),
        check_vma=False,
    )
```

profile of v0, /device:TPU:230, one launch (start us, length us, event | category | flops | bytes accessed | tf_op | source)
XLA Modules:
  0.0 448.4 jit_solution(15058796765951390284)
XLA Ops:
  9.4 1.2 copy.50
  10.7 1.3 dynamic-slice.1
  12.6 1.2 fusion.61
  14.5 1.3 compare_convert_fusion.1
  16.6 2.1 convolution_add_fusion
  18.8 69.7 %all-reduce.2 = (f32[32]{0:T(128)S(1)}, f32[256]{0:T(256)S(1)}) all-reduce(f32[32]{0:T(128)S(1)} %get-tuple-element.258, f32[256]{0:T(256)S(1)} %get-tuple-element.260), channel_id=2, replica_groups=mesh['seq'=32,'heads'=8] {'seq'}, use_global_device_ids=true, to_apply=%add | all-reduce | flops 288 | bytes 2304
  88.6 1.3 copy.44
  90.2 43.2 %all-gather.3 = s32[32,1,256]{2,1,0:T(1,128)S(1)} all-gather(s32[1,1,256]{2,1,0:T(1,128)} %bitcast.157), channel_id=1, replica_groups=mesh['seq'=32,'heads'=8] {'seq'}, dimensions={0}, use_global_device_ids=true | all-gather | bytes 33792 | tf_op jit(solution)/shard_map/all_gather | solution.py:161
  133.8 29.7 %all-gather.10.cloned.1.call-done = bf16[8192,128]{1,0:T(8,128)(2,1)} async-done(((bf16[256,128]{1,0:T(8,128)(2,1)}), bf16[8192,128]{1,0:T(8,128)(2,1)}) %all-gather.10.cloned.1.call-update) | async-done | bytes 2097168 | tf_op jit(solution)/shard_map/all_gather | solution.py:160
  163.5 139.9 %while.36 = (s32[]{:T(128)}, f32[8,256]{1,0:T(8,128)S(1)}, f32[8,256]{1,0:T(8,128)S(1)}, f32[8,256,128]{2,1,0:T(8,128)S(1)}, s32[8]{0:T(128)S(1)}, /*index=5*/s3...) while((s32[]{:T(128)}, f32[8,256]{1,0:T(8,128)S(1)}, ...), condition=%wide.region_7.8_spmd.clone, body=%wide.region_4.7_spmd.clone.sunk | while | flops 1098394880 | bytes 63070416 | solution.py:191
  165.9 5.6 %fusion.80 = (f32[8,256]{1,0:T(8,128)S(1)}, f32[1024,256,8]{1,0,2:T(8,128)}) fusion(pred[256,1024]{0,1:T(8,128)(4,1)S(1)} %compare_and_fusion.2, bf16[256,1,8,128]{3,0,2,1:T(8,128)(2,1)S(1)} %get-tuple-element.452, bf16[8,1024,1,128]{3,1,2,0:T(8,128)(2,1)} %get-tuple-element.451, s32[]{:T(128)} %get-tuple-element.430), kind=kOutput, calls=%fused_computation.8.clone.1 | convolution fusion | flops 543160320 | bytes 9445888 | tf_op jit(solution)/shard_map/while/body/eval_jaxpr/tgjd,sgd->gjts/dot_general | solution.py:70
  171.5 5.2 %fusion.81 = f32[8,256]{1,0:T(8,128)S(1)} fusion(f32[1024,256,8]{1,0,2:T(8,128)} %get-tuple-element.380, f32[8,256]{1,0:T(8,128)S(1)} %select_maximum_fusion.2, pred[256,1024]{0,1:T(8,128)(4,1)S(1)} %compare_and_fusion.2), kind=kLoop, calls=%fused_computation.11.clone.1 | loop fusion | flops 8386560 | bytes 8667136 | tf_op jit(solution)/shard_map/while/body/eval_jaxpr/reduce_sum | solution.py:80
  177.3 3.4 fusion.83
  183.2 5.6 %fusion.80 = (f32[8,256]{1,0:T(8,128)S(1)}, f32[1024,256,8]{1,0,2:T(8,128)}) fusion(pred[256,1024]{0,1:T(8,128)(4,1)S(1)} %compare_and_fusion.2, bf16[256,1,8,128]{3,0,2,1:T(8,128)(2,1)S(1)} %get-tuple-element.452, bf16[8,1024,1,128]{3,1,2,0:T(8,128)(2,1)} %get-tuple-element.451, s32[]{:T(128)} %get-tuple-element.430), kind=kOutput, calls=%fused_computation.8.clone.1 | convolution fusion | flops 543160320 | bytes 9445888 | tf_op jit(solution)/shard_map/while/body/eval_jaxpr/tgjd,sgd->gjts/dot_general | solution.py:70
  188.8 5.3 %fusion.81 = f32[8,256]{1,0:T(8,128)S(1)} fusion(f32[1024,256,8]{1,0,2:T(8,128)} %get-tuple-element.380, f32[8,256]{1,0:T(8,128)S(1)} %select_maximum_fusion.2, pred[256,1024]{0,1:T(8,128)(4,1)S(1)} %compare_and_fusion.2), kind=kLoop, calls=%fused_computation.11.clone.1 | loop fusion | flops 8386560 | bytes 8667136 | tf_op jit(solution)/shard_map/while/body/eval_jaxpr/reduce_sum | solution.py:80
  194.8 3.4 fusion.83
  200.7 5.6 %fusion.80 = (f32[8,256]{1,0:T(8,128)S(1)}, f32[1024,256,8]{1,0,2:T(8,128)}) fusion(pred[256,1024]{0,1:T(8,128)(4,1)S(1)} %compare_and_fusion.2, bf16[256,1,8,128]{3,0,2,1:T(8,128)(2,1)S(1)} %get-tuple-element.452, bf16[8,1024,1,128]{3,1,2,0:T(8,128)(2,1)} %get-tuple-element.451, s32[]{:T(128)} %get-tuple-element.430), kind=kOutput, calls=%fused_computation.8.clone.1 | convolution fusion | flops 543160320 | bytes 9445888 | tf_op jit(solution)/shard_map/while/body/eval_jaxpr/tgjd,sgd->gjts/dot_general | solution.py:70
  206.3 5.2 %fusion.81 = f32[8,256]{1,0:T(8,128)S(1)} fusion(f32[1024,256,8]{1,0,2:T(8,128)} %get-tuple-element.380, f32[8,256]{1,0:T(8,128)S(1)} %select_maximum_fusion.2, pred[256,1024]{0,1:T(8,128)(4,1)S(1)} %compare_and_fusion.2), kind=kLoop, calls=%fused_computation.11.clone.1 | loop fusion | flops 8386560 | bytes 8667136 | tf_op jit(solution)/shard_map/while/body/eval_jaxpr/reduce_sum | solution.py:80
  212.1 3.4 fusion.83
  218.0 6.0 %fusion.80 = (f32[8,256]{1,0:T(8,128)S(1)}, f32[1024,256,8]{1,0,2:T(8,128)}) fusion(pred[256,1024]{0,1:T(8,128)(4,1)S(1)} %compare_and_fusion.2, bf16[256,1,8,128]{3,0,2,1:T(8,128)(2,1)S(1)} %get-tuple-element.452, bf16[8,1024,1,128]{3,1,2,0:T(8,128)(2,1)} %get-tuple-element.451, s32[]{:T(128)} %get-tuple-element.430), kind=kOutput, calls=%fused_computation.8.clone.1 | convolution fusion | flops 543160320 | bytes 9445888 | tf_op jit(solution)/shard_map/while/body/eval_jaxpr/tgjd,sgd->gjts/dot_general | solution.py:70
  223.9 5.3 %fusion.81 = f32[8,256]{1,0:T(8,128)S(1)} fusion(f32[1024,256,8]{1,0,2:T(8,128)} %get-tuple-element.380, f32[8,256]{1,0:T(8,128)S(1)} %select_maximum_fusion.2, pred[256,1024]{0,1:T(8,128)(4,1)S(1)} %compare_and_fusion.2), kind=kLoop, calls=%fused_computation.11.clone.1 | loop fusion | flops 8386560 | bytes 8667136 | tf_op jit(solution)/shard_map/while/body/eval_jaxpr/reduce_sum | solution.py:80
  229.9 3.5 fusion.83
  235.8 5.6 %fusion.80 = (f32[8,256]{1,0:T(8,128)S(1)}, f32[1024,256,8]{1,0,2:T(8,128)}) fusion(pred[256,1024]{0,1:T(8,128)(4,1)S(1)} %compare_and_fusion.2, bf16[256,1,8,128]{3,0,2,1:T(8,128)(2,1)S(1)} %get-tuple-element.452, bf16[8,1024,1,128]{3,1,2,0:T(8,128)(2,1)} %get-tuple-element.451, s32[]{:T(128)} %get-tuple-element.430), kind=kOutput, calls=%fused_computation.8.clone.1 | convolution fusion | flops 543160320 | bytes 9445888 | tf_op jit(solution)/shard_map/while/body/eval_jaxpr/tgjd,sgd->gjts/dot_general | solution.py:70
  241.4 5.3 %fusion.81 = f32[8,256]{1,0:T(8,128)S(1)} fusion(f32[1024,256,8]{1,0,2:T(8,128)} %get-tuple-element.380, f32[8,256]{1,0:T(8,128)S(1)} %select_maximum_fusion.2, pred[256,1024]{0,1:T(8,128)(4,1)S(1)} %compare_and_fusion.2), kind=kLoop, calls=%fused_computation.11.clone.1 | loop fusion | flops 8386560 | bytes 8667136 | tf_op jit(solution)/shard_map/while/body/eval_jaxpr/reduce_sum | solution.py:80
  247.7 3.4 fusion.83
  253.6 5.6 %fusion.80 = (f32[8,256]{1,0:T(8,128)S(1)}, f32[1024,256,8]{1,0,2:T(8,128)}) fusion(pred[256,1024]{0,1:T(8,128)(4,1)S(1)} %compare_and_fusion.2, bf16[256,1,8,128]{3,0,2,1:T(8,128)(2,1)S(1)} %get-tuple-element.452, bf16[8,1024,1,128]{3,1,2,0:T(8,128)(2,1)} %get-tuple-element.451, s32[]{:T(128)} %get-tuple-element.430), kind=kOutput, calls=%fused_computation.8.clone.1 | convolution fusion | flops 543160320 | bytes 9445888 | tf_op jit(solution)/shard_map/while/body/eval_jaxpr/tgjd,sgd->gjts/dot_general | solution.py:70
  259.2 5.2 %fusion.81 = f32[8,256]{1,0:T(8,128)S(1)} fusion(f32[1024,256,8]{1,0,2:T(8,128)} %get-tuple-element.380, f32[8,256]{1,0:T(8,128)S(1)} %select_maximum_fusion.2, pred[256,1024]{0,1:T(8,128)(4,1)S(1)} %compare_and_fusion.2), kind=kLoop, calls=%fused_computation.11.clone.1 | loop fusion | flops 8386560 | bytes 8667136 | tf_op jit(solution)/shard_map/while/body/eval_jaxpr/reduce_sum | solution.py:80
  265.2 3.4 fusion.83
  271.1 5.6 %fusion.80 = (f32[8,256]{1,0:T(8,128)S(1)}, f32[1024,256,8]{1,0,2:T(8,128)}) fusion(pred[256,1024]{0,1:T(8,128)(4,1)S(1)} %compare_and_fusion.2, bf16[256,1,8,128]{3,0,2,1:T(8,128)(2,1)S(1)} %get-tuple-element.452, bf16[8,1024,1,128]{3,1,2,0:T(8,128)(2,1)} %get-tuple-element.451, s32[]{:T(128)} %get-tuple-element.430), kind=kOutput, calls=%fused_computation.8.clone.1 | convolution fusion | flops 543160320 | bytes 9445888 | tf_op jit(solution)/shard_map/while/body/eval_jaxpr/tgjd,sgd->gjts/dot_general | solution.py:70
  276.7 5.3 %fusion.81 = f32[8,256]{1,0:T(8,128)S(1)} fusion(f32[1024,256,8]{1,0,2:T(8,128)} %get-tuple-element.380, f32[8,256]{1,0:T(8,128)S(1)} %select_maximum_fusion.2, pred[256,1024]{0,1:T(8,128)(4,1)S(1)} %compare_and_fusion.2), kind=kLoop, calls=%fused_computation.11.clone.1 | loop fusion | flops 8386560 | bytes 8667136 | tf_op jit(solution)/shard_map/while/body/eval_jaxpr/reduce_sum | solution.py:80
  282.6 3.4 fusion.83
  288.5 5.6 %fusion.80 = (f32[8,256]{1,0:T(8,128)S(1)}, f32[1024,256,8]{1,0,2:T(8,128)}) fusion(pred[256,1024]{0,1:T(8,128)(4,1)S(1)} %compare_and_fusion.2, bf16[256,1,8,128]{3,0,2,1:T(8,128)(2,1)S(1)} %get-tuple-element.452, bf16[8,1024,1,128]{3,1,2,0:T(8,128)(2,1)} %get-tuple-element.451, s32[]{:T(128)} %get-tuple-element.430), kind=kOutput, calls=%fused_computation.8.clone.1 | convolution fusion | flops 543160320 | bytes 9445888 | tf_op jit(solution)/shard_map/while/body/eval_jaxpr/tgjd,sgd->gjts/dot_general | solution.py:70
  294.1 5.2 %fusion.81 = f32[8,256]{1,0:T(8,128)S(1)} fusion(f32[1024,256,8]{1,0,2:T(8,128)} %get-tuple-element.380, f32[8,256]{1,0:T(8,128)S(1)} %select_maximum_fusion.2, pred[256,1024]{0,1:T(8,128)(4,1)S(1)} %compare_and_fusion.2), kind=kLoop, calls=%fused_computation.11.clone.1 | loop fusion | flops 8386560 | bytes 8667136 | tf_op jit(solution)/shard_map/while/body/eval_jaxpr/reduce_sum | solution.py:80
  299.9 3.4 fusion.83
  304.6 117.0 %while.10 = (s32[]{:T(128)}, f32[8,128,128]{2,1,0:T(8,128)S(1)}, f32[1]{0:T(128)}, s32[]{:T(128)}, f32[32,1]{0,1:T(1,128)S(1)}, /*index=5*/f32[32,8]{1,0:T(8,128...) while((s32[]{:T(128)}, f32[8,128,128]{2,1,0:T(8,128)S(1)}, ...), condition=%wide.region_1.2_spmd, body=%wide.region_0.1_spmd.sunk | while | flops 262161 | bytes 1573157 | solution.py:22
  321.6 1.2 bitcast_add_fusion.2
  325.4 1.2 bitcast_add_fusion.2
  344.3 1.2 bitcast_add_fusion.2
  348.0 1.2 bitcast_add_fusion.2
  366.9 1.2 bitcast_add_fusion.2
  370.7 1.2 bitcast_add_fusion.2
  393.3 1.2 bitcast_add_fusion.2
  397.1 1.2 bitcast_add_fusion.2
  416.0 1.2 bitcast_add_fusion.2
  419.8 1.2 bitcast_add_fusion.2
  422.3 2.8 fusion.30
  425.2 1.9 multiply_reduce_fusion
  427.4 13.4 %psum.7 = f32[256]{0:T(256)S(1)} all-reduce(f32[256]{0:T(256)S(1)} %get-tuple-element.262), channel_id=1, replica_groups=mesh['seq'=32,'heads'=8] {'heads'}, use_global_device_ids=true, to_apply=%region_3.4 | all-reduce | flops 256 | bytes 2048 | tf_op jit(solution)/shard_map/psum | solution.py:127
  (203 shorter events, 69.3 us)
Async XLA Ops:
  7.2 414.6 %copy-start = (bf16[256,1024]{1,0:T(8,128)(2,1)S(1)}, bf16[256,1024]{1,0:T(8,128)(2,1)}, u32[]{:S(2)}) copy-start(bf16[256,1024]{1,0:T(8,128)(2,1)} %param.13) | copy-start | bytes 1572868
  7.2 126.6 %all-gather.8.cloned.1.call-start = ((), (), s32[]{:S(2)}) async-start(), calls=%async_computation | async-start | bytes 2162688 | tf_op jit(solution)/shard_map/all_gather | solution.py:159
  7.9 155.6 %all-gather.10.cloned.1.call-start = ((), (), s32[]{:S(2)}) async-start(), calls=%async_computation.1 | async-start | bytes 2162688 | tf_op jit(solution)/shard_map/all_gather | solution.py:160
  8.7 295.9 %all-gather.12.cloned.1.call-start = ((), (), s32[]{:S(2)}) async-start(), calls=%async_computation.2 | async-start | bytes 17301504 | tf_op jit(solution)/shard_map/all_gather | solution.py:14
  171.5 5.8 %copy-start.1 = (f32[1024,256,8]{1,0,2:T(8,128)S(1)}, f32[1024,256,8]{1,0,2:T(8,128)}, u32[]{:S(2)}) copy-start(f32[1024,256,8]{1,0,2:T(8,128)} %get-tuple-element.380) | copy-start | bytes 25165828 | tf_op jit(solution)/shard_map/while
  188.8 6.0 %copy-start.1 = (f32[1024,256,8]{1,0,2:T(8,128)S(1)}, f32[1024,256,8]{1,0,2:T(8,128)}, u32[]{:S(2)}) copy-start(f32[1024,256,8]{1,0,2:T(8,128)} %get-tuple-element.380) | copy-start | bytes 25165828 | tf_op jit(solution)/shard_map/while
  206.3 5.8 %copy-start.1 = (f32[1024,256,8]{1,0,2:T(8,128)S(1)}, f32[1024,256,8]{1,0,2:T(8,128)}, u32[]{:S(2)}) copy-start(f32[1024,256,8]{1,0,2:T(8,128)} %get-tuple-element.380) | copy-start | bytes 25165828 | tf_op jit(solution)/shard_map/while
  223.9 5.9 %copy-start.1 = (f32[1024,256,8]{1,0,2:T(8,128)S(1)}, f32[1024,256,8]{1,0,2:T(8,128)}, u32[]{:S(2)}) copy-start(f32[1024,256,8]{1,0,2:T(8,128)} %get-tuple-element.380) | copy-start | bytes 25165828 | tf_op jit(solution)/shard_map/while
  241.4 6.3 %copy-start.1 = (f32[1024,256,8]{1,0,2:T(8,128)S(1)}, f32[1024,256,8]{1,0,2:T(8,128)}, u32[]{:S(2)}) copy-start(f32[1024,256,8]{1,0,2:T(8,128)} %get-tuple-element.380) | copy-start | bytes 25165828 | tf_op jit(solution)/shard_map/while
  259.2 6.0 %copy-start.1 = (f32[1024,256,8]{1,0,2:T(8,128)S(1)}, f32[1024,256,8]{1,0,2:T(8,128)}, u32[]{:S(2)}) copy-start(f32[1024,256,8]{1,0,2:T(8,128)} %get-tuple-element.380) | copy-start | bytes 25165828 | tf_op jit(solution)/shard_map/while
  276.7 5.9 %copy-start.1 = (f32[1024,256,8]{1,0,2:T(8,128)S(1)}, f32[1024,256,8]{1,0,2:T(8,128)}, u32[]{:S(2)}) copy-start(f32[1024,256,8]{1,0,2:T(8,128)} %get-tuple-element.380) | copy-start | bytes 25165828 | tf_op jit(solution)/shard_map/while
  294.1 5.8 %copy-start.1 = (f32[1024,256,8]{1,0,2:T(8,128)S(1)}, f32[1024,256,8]{1,0,2:T(8,128)}, u32[]{:S(2)}) copy-start(f32[1024,256,8]{1,0,2:T(8,128)} %get-tuple-element.380) | copy-start | bytes 25165828 | tf_op jit(solution)/shard_map/while
  303.4 118.3 %copy-start.2 = (s32[256]{0:T(256)S(1)}, s32[256]{0:T(256)}, u32[]{:S(2)}) copy-start(s32[256]{0:T(256)} %get-tuple-element.465) | copy-start | bytes 3076
  304.6 136.3 %copy-start.3 = (f32[1024]{0:T(1024)S(1)}, f32[1024]{0:T(1024)}, u32[]{:S(2)}) copy-start(f32[1024]{0:T(1024)} %param.17) | copy-start | bytes 12292
Sparse Core Ops, SparseCore 0:
  10.6 75.2 all-gather.7
  88.5 74.9 all-gather.9
  166.6 137.0 all-gather.11
where the time goes:
time: 452 us; the launch traced here: 448 us
  blocking collectives  126 us (28%)
  other arithmetic  93.2 us (21%)
  matrix products  80.3 us (18%)
  loops' own time  67.7 us (15%)
  local copies, waits for them, and re-layouts  34.4 us (8%)
  waiting for transfers between devices  31.1 us (7%)
  between operations  15.2 us (3%)
    unnamed x1, blocking collectives  69.7 us
    another operation x1, loops' own time, carried_in(): return lax.fori_loop(0, place, carried_one, state)  61.6 us
    dot_general x8, matrix products, block_update(): jnp.einsum('tgjd,sgd->gjts', queries, k_blk, preferred_element_type=jnp.f...  45.2 us
    all_gather x1, blocking collectives, body(): seg_keys = lax.all_gather(segment_ids, 'seq', axis=0, tiled=True)  43.2 us
    reduce_sum x8, other arithmetic, block_update(): den = den * corr + jnp.sum(p, axis=2)  42.1 us
    add x31, other arithmetic, combine_states(): factor[:, None, None] * state_e + state_l  36.9 us
    all_gather x1, waiting for transfers between devices, body(): values = lax.all_gather(soft_v, 'seq', axis=0, tiled=True)  29.7 us
    dot_general x8, matrix products, block_update(): jnp.einsum('gjts,sgd->gjtd', weights, v_blk, preferred_element_type=jnp.f...  27.6 us
  transfers between devices with their start and end apart: 3, of which 1 were waited for; matrix products, arithmetic and copies ran while one was open for 31% of the time, Pallas kernels for 0%

commit v1 on v0

--- a/solution.py
+++ b/solution.py
@@ -11,15 +11,20 @@
 
 def carried_in(part, axis, combine, identity):
     place = lax.axis_index(axis)
-    gathered = jax.tree.map(lambda a: lax.all_gather(a, axis), part)
-    state = jax.tree.map(lambda a, e: jnp.zeros_like(a) + jnp.asarray(e, a.dtype), part, identity)
-
-    def carried_one(step, state):
-        return combine(
-            state, jax.tree.map(lambda a: lax.dynamic_index_in_dim(a, step, 0, False), gathered)
-        )
-
-    return lax.fori_loop(0, place, carried_one, state)
+    size = lax.axis_size(axis)
+    ident = jax.tree.map(lambda a, e: jnp.zeros_like(a) + jnp.asarray(e, a.dtype), part, identity)
+    shifted = jax.tree.map(
+        lambda a: lax.ppermute(a, axis, [(i, i + 1) for i in range(size - 1)]), part
+    )
+    state = jax.tree.map(lambda s, e: jnp.where(place == 0, e, s), shifted, ident)
+    step = 1
+    while step < size:
+        pairs = [(i, i + step) for i in range(size - step)]
+        earlier = jax.tree.map(lambda a: lax.ppermute(a, axis, pairs), state)
+        merged = combine(earlier, state)
+        state = jax.tree.map(lambda m, s: jnp.where(place >= step, m, s), merged, state)
+        step *= 2
+    return state
 
 
 def light_block(carry, inputs, rates):

time: 452 us -> 401 us (0.89)
  the two profiles are of different devices: /device:TPU:230 before, /device:TPU:166 now
where the time goes in v1:
time: 401 us; the launch traced here: 397 us
  blocking collectives  80.6 us (20%)
  matrix products  80.2 us (20%)
  starting transfers between devices  68.9 us (17%)
  waiting for transfers between devices  67.1 us (17%)
  other arithmetic  53.5 us (13%)
  between operations  21.7 us (5%)
  local copies, waits for them, and re-layouts  19.5 us (5%)
  loops' own time  5.89 us (1%)
    all_gather x1, blocking collectives, body(): seg_keys = lax.all_gather(segment_ids, 'seq', axis=0, tiled=True)  65.4 us
    ppermute x14, starting transfers between devices, carried_in(): earlier = jax.tree.map(lambda a: lax.ppermute(a, axis, pairs), state)  54.6 us
    dot_general x8, matrix products, block_update(): jnp.einsum('tgjd,sgd->gjts', queries, k_blk, preferred_element_type=jnp.f...  45.8 us
    ppermute x14, waiting for transfers between devices, carried_in(): earlier = jax.tree.map(lambda a: lax.ppermute(a, axis, pairs), state)  44.6 us
    reduce_sum x8, other arithmetic, block_update(): den = den * corr + jnp.sum(p, axis=2)  41.9 us
    dot_general x8, matrix products, block_update(): jnp.einsum('gjts,sgd->gjtd', weights, v_blk, preferred_element_type=jnp.f...  27.5 us
    ppermute x3, waiting for transfers between devices, carried_in(): lax.ppermute(a, axis, [(i, i + 1) for i in range(size - 1)])  21.8 us
    psum x1, blocking collectives, body(): total_sq = lax.psum(sums, 'heads')  15.2 us
  transfers between devices with their start and end apart: 19, of which 12 were waited for; matrix products, arithmetic and copies ran while one was open for 4% of the time, Pallas kernels for 0%

profile of v1, /device:TPU:166, one launch (start us, length us, event | category | flops | bytes accessed | tf_op | source)
XLA Modules:
  0.0 397.4 jit_solution(9282533641575457791)
XLA Ops:
  9.3 2.8 collective-permute-start
  15.4 6.2 %collective-permute-start.1 = (f32[1]{0:T(128)}, f32[1]{0:T(128)}, u32[]{:S(2)}, u32[]{:S(2)}) collective-permute-start(f32[1]{0:T(128)} %select_n.151), channel_id=1, source_target_pairs={{0,8},{8,16},{16,24},{24,32},{32,40},{40,48},{48,56},{56,64},{64,7... | collective-permute-start | bytes 20 | tf_op jit(solution)/shard_map/ppermute | solution.py:23
  22.2 5.0 %collective-permute-start.2 = (f32[1]{0:T(128)}, f32[1]{0:T(128)}, u32[]{:S(2)}, u32[]{:S(2)}) collective-permute-start(f32[1]{0:T(128)} %select_n.152), channel_id=1, source_target_pairs={{0,16},{8,24},{16,32},{24,40},{32,48},{40,56},{48,64},{56,72},{64,... | collective-permute-start | bytes 20 | tf_op jit(solution)/shard_map/ppermute | solution.py:23
  29.7 4.2 %collective-permute-start.3 = (f32[1]{0:T(128)}, f32[1]{0:T(128)}, u32[]{:S(2)}, u32[]{:S(2)}) collective-permute-start(f32[1]{0:T(128)} %select_n.153), channel_id=1, source_target_pairs={{0,32},{8,40},{16,48},{24,56},{32,64},{40,72},{48,80},{56,88},{64,... | collective-permute-start | bytes 20 | tf_op jit(solution)/shard_map/ppermute | solution.py:23
  35.9 4.0 collective-permute-start.4
  39.8 3.5 collective-permute-done.4
  45.3 8.1 %collective-permute-done.5 = f32[1]{0:T(128)} collective-permute-done((f32[1]{0:T(128)}, f32[1]{0:T(128)}, u32[]{:S(2)}, u32[]{:S(2)}) %collective-permute-start.5) | collective-permute-done | bytes 36 | tf_op jit(solution)/shard_map/ppermute | solution.py:23
  56.8 9.4 %collective-permute-start.11 = (f32[8,128,128]{2,1,0:T(8,128)S(1)}, f32[8,128,128]{2,1,0:T(8,128)S(1)}, u32[]{:S(2)}, u32[]{:S(2)}) collective-permute-start(f32[8,128,128]{2,1,0:T(8,128)S(1)} %convolution_add_fusion), channel_id=1, source_target_pairs={{0,8},{8,16},{16,24},{24,32},{32,40},{40,48},{48,56},{56,64},{64,7... | collective-permute-start | bytes 1572872 | tf_op jit(solution)/shard_map/ppermute | solution.py:17
  66.2 13.9 %collective-permute-done.11 = f32[8,128,128]{2,1,0:T(8,128)S(1)} collective-permute-done((f32[8,128,128]{2,1,0:T(8,128)S(1)}, f32[8,128,128]{2,1,0:T(8,128)S(1)}, u32[]{:S(2)}, u32[]{:S(2)}) %collective-permute-start.11) | collective-permute-done | bytes 524320 | tf_op jit(solution)/shard_map/ppermute | solution.py:17
  80.1 6.5 %collective-permute-start.12 = (f32[8,128,128]{2,1,0:T(8,128)S(1)}, f32[8,128,128]{2,1,0:T(8,128)S(1)}, u32[]{:S(2)}, u32[]{:S(2)}) collective-permute-start(f32[8,128,128]{2,1,0:T(8,128)S(1)} %broadcast_select_fusion), channel_id=1, source_target_pairs={{0,8},{8,16},{16,24},{24,32},{32,40},{40,48},{48,56},{56,64},{64,7... | collective-permute-start | bytes 1572872 | tf_op jit(solution)/shard_map/ppermute | solution.py:23
  89.1 7.9 %collective-permute-done.6 = f32[8]{0:T(128)S(1)} collective-permute-done((f32[8]{0:T(128)S(1)}, f32[8]{0:T(128)S(1)}, u32[]{:S(2)}, u32[]{:S(2)}) %collective-permute-start.6) | collective-permute-done | bytes 64 | tf_op jit(solution)/shard_map/ppermute | solution.py:17
  99.8 7.6 %collective-permute-start.7 = (f32[8]{0:T(128)S(1)}, f32[8]{0:T(128)S(1)}, u32[]{:S(2)}, u32[]{:S(2)}) collective-permute-start(f32[8]{0:T(128)S(1)} %get-tuple-element.181), channel_id=1, source_target_pairs={{0,8},{8,16},{16,24},{24,32},{32,40},{40,48},{48,56},{56,64},{64,7... | collective-permute-start | bytes 104 | tf_op jit(solution)/shard_map/ppermute | solution.py:23
  107.4 3.3 collective-permute-done.7
  113.5 6.8 %collective-permute-start.8 = (f32[8]{0:T(128)S(1)}, f32[8]{0:T(128)S(1)}, u32[]{:S(2)}, u32[]{:S(2)}) collective-permute-start(f32[8]{0:T(128)S(1)} %get-tuple-element.179), channel_id=1, source_target_pairs={{0,16},{8,24},{16,32},{24,40},{32,48},{40,56},{48,64},{56,72},{64,... | collective-permute-start | bytes 104 | tf_op jit(solution)/shard_map/ppermute | solution.py:23
  120.3 4.9 %collective-permute-done.8 = f32[8]{0:T(128)S(1)} collective-permute-done((f32[8]{0:T(128)S(1)}, f32[8]{0:T(128)S(1)}, u32[]{:S(2)}, u32[]{:S(2)}) %collective-permute-start.8) | collective-permute-done | bytes 64 | tf_op jit(solution)/shard_map/ppermute | solution.py:23
  125.2 5.8 %collective-permute-done.14 = f32[8,128,128]{2,1,0:T(8,128)S(1)} collective-permute-done((f32[8,128,128]{2,1,0:T(8,128)S(1)}, f32[8,128,128]{2,1,0:T(8,128)S(1)}, u32[]{:S(2)}, u32[]{:S(2)}) %collective-permute-start.14) | collective-permute-done | bytes 524320 | tf_op jit(solution)/shard_map/ppermute | solution.py:23
  133.7 65.4 %all-gather = s32[32,1,256]{2,1,0:T(1,128)S(1)} all-gather(s32[1,1,256]{2,1,0:T(1,128)S(1)} %bitcast.148), channel_id=1, replica_groups=mesh['seq'=32,'heads'=8] {'seq'}, dimensions={0}, use_global_device_ids=true | all-gather | bytes 33792 | tf_op jit(solution)/shard_map/all_gather | solution.py:166
  203.0 3.5 collective-permute-done.9
  209.6 3.0 fusion.29
  212.7 4.0 %collective-permute-start.10 = (f32[8]{0:T(128)S(1)}, f32[8]{0:T(128)S(1)}, u32[]{:S(2)}, u32[]{:S(2)}) collective-permute-start(f32[8]{0:T(128)S(1)} %get-tuple-element.175), channel_id=1, source_target_pairs={{0,64},{8,72},{16,80},{24,88},{32,96},{40,104},{48,112},{56,120},{... | collective-permute-start | bytes 104 | tf_op jit(solution)/shard_map/ppermute | solution.py:23
  216.7 5.8 %collective-permute-done.10 = f32[8]{0:T(128)S(1)} collective-permute-done((f32[8]{0:T(128)S(1)}, f32[8]{0:T(128)S(1)}, u32[]{:S(2)}, u32[]{:S(2)}) %collective-permute-start.10) | collective-permute-done | bytes 64 | tf_op jit(solution)/shard_map/ppermute | solution.py:23
  222.5 6.5 %collective-permute-done.16 = f32[8,128,128]{2,1,0:T(8,128)S(1)} collective-permute-done((f32[8,128,128]{2,1,0:T(8,128)S(1)}, f32[8,128,128]{2,1,0:T(8,128)S(1)}, u32[]{:S(2)}, u32[]{:S(2)}) %collective-permute-start.16) | collective-permute-done | bytes 524320 | tf_op jit(solution)/shard_map/ppermute | solution.py:23
  231.3 15.2 %psum.7 = f32[256]{0:T(256)S(1)} all-reduce(f32[256]{0:T(256)S(1)} %get-tuple-element.193), channel_id=1, replica_groups=mesh['seq'=32,'heads'=8] {'heads'}, use_global_device_ids=true, to_apply=%region_1.2 | all-reduce | flops 256 | bytes 2048 | tf_op jit(solution)/shard_map/psum | solution.py:132
  247.5 140.7 %while.3 = (s32[]{:T(128)}, f32[8,256]{1,0:T(8,128)S(1)}, f32[8,256]{1,0:T(8,128)S(1)}, f32[8,256,128]{2,1,0:T(8,128)}, s32[8]{0:T(128)S(1)}, /*index=5*/s32[8,1...) while((s32[]{:T(128)}, f32[8,256]{1,0:T(8,128)S(1)}, ...), condition=%wide.region_5.6_spmd.clone, body=%wide.region_2.5_spmd.clone.sunk | while | flops 1098394880 | bytes 71459088 | solution.py:196
  249.1 5.7 %fusion.77 = (f32[8,256]{1,0:T(8,128)S(1)}, f32[1024,256,8]{1,0,2:T(8,128)}) fusion(pred[256,1024]{0,1:T(8,128)(4,1)S(1)} %compare_and_fusion.2, bf16[256,1,8,128]{3,0,2,1:T(8,128)(2,1)S(1)} %get-tuple-element.308, bf16[8,1024,1,128]{3,1,2,0:T(8,128)(2,1)} %get-tuple-element.307, s32[]{:T(128)} %get-tuple-element.286), kind=kOutput, calls=%fused_computation.3.clone.1 | convolution fusion | flops 543160320 | bytes 9445888 | tf_op jit(solution)/shard_map/while/body/eval_jaxpr/tgjd,sgd->gjts/dot_general | solution.py:75
  254.9 5.2 %fusion.78 = f32[8,256]{1,0:T(8,128)S(1)} fusion(f32[1024,256,8]{1,0,2:T(8,128)} %get-tuple-element.269, f32[8,256]{1,0:T(8,128)S(1)} %select_maximum_fusion.2, pred[256,1024]{0,1:T(8,128)(4,1)S(1)} %compare_and_fusion.2), kind=kLoop, calls=%fused_computation.6.clone.1 | loop fusion | flops 8386560 | bytes 8667136 | tf_op jit(solution)/shard_map/while/body/eval_jaxpr/reduce_sum | solution.py:85
  260.6 3.4 fusion.80
  266.7 5.7 %fusion.77 = (f32[8,256]{1,0:T(8,128)S(1)}, f32[1024,256,8]{1,0,2:T(8,128)}) fusion(pred[256,1024]{0,1:T(8,128)(4,1)S(1)} %compare_and_fusion.2, bf16[256,1,8,128]{3,0,2,1:T(8,128)(2,1)S(1)} %get-tuple-element.308, bf16[8,1024,1,128]{3,1,2,0:T(8,128)(2,1)} %get-tuple-element.307, s32[]{:T(128)} %get-tuple-element.286), kind=kOutput, calls=%fused_computation.3.clone.1 | convolution fusion | flops 543160320 | bytes 9445888 | tf_op jit(solution)/shard_map/while/body/eval_jaxpr/tgjd,sgd->gjts/dot_general | solution.py:75
  272.4 5.2 %fusion.78 = f32[8,256]{1,0:T(8,128)S(1)} fusion(f32[1024,256,8]{1,0,2:T(8,128)} %get-tuple-element.269, f32[8,256]{1,0:T(8,128)S(1)} %select_maximum_fusion.2, pred[256,1024]{0,1:T(8,128)(4,1)S(1)} %compare_and_fusion.2), kind=kLoop, calls=%fused_computation.6.clone.1 | loop fusion | flops 8386560 | bytes 8667136 | tf_op jit(solution)/shard_map/while/body/eval_jaxpr/reduce_sum | solution.py:85
  278.2 3.4 fusion.80
  284.3 5.7 %fusion.77 = (f32[8,256]{1,0:T(8,128)S(1)}, f32[1024,256,8]{1,0,2:T(8,128)}) fusion(pred[256,1024]{0,1:T(8,128)(4,1)S(1)} %compare_and_fusion.2, bf16[256,1,8,128]{3,0,2,1:T(8,128)(2,1)S(1)} %get-tuple-element.308, bf16[8,1024,1,128]{3,1,2,0:T(8,128)(2,1)} %get-tuple-element.307, s32[]{:T(128)} %get-tuple-element.286), kind=kOutput, calls=%fused_computation.3.clone.1 | convolution fusion | flops 543160320 | bytes 9445888 | tf_op jit(solution)/shard_map/while/body/eval_jaxpr/tgjd,sgd->gjts/dot_general | solution.py:75
  290.0 5.2 %fusion.78 = f32[8,256]{1,0:T(8,128)S(1)} fusion(f32[1024,256,8]{1,0,2:T(8,128)} %get-tuple-element.269, f32[8,256]{1,0:T(8,128)S(1)} %select_maximum_fusion.2, pred[256,1024]{0,1:T(8,128)(4,1)S(1)} %compare_and_fusion.2), kind=kLoop, calls=%fused_computation.6.clone.1 | loop fusion | flops 8386560 | bytes 8667136 | tf_op jit(solution)/shard_map/while/body/eval_jaxpr/reduce_sum | solution.py:85
  295.8 3.4 fusion.80
  301.9 5.7 %fusion.77 = (f32[8,256]{1,0:T(8,128)S(1)}, f32[1024,256,8]{1,0,2:T(8,128)}) fusion(pred[256,1024]{0,1:T(8,128)(4,1)S(1)} %compare_and_fusion.2, bf16[256,1,8,128]{3,0,2,1:T(8,128)(2,1)S(1)} %get-tuple-element.308, bf16[8,1024,1,128]{3,1,2,0:T(8,128)(2,1)} %get-tuple-element.307, s32[]{:T(128)} %get-tuple-element.286), kind=kOutput, calls=%fused_computation.3.clone.1 | convolution fusion | flops 543160320 | bytes 9445888 | tf_op jit(solution)/shard_map/while/body/eval_jaxpr/tgjd,sgd->gjts/dot_general | solution.py:75
  307.6 5.2 %fusion.78 = f32[8,256]{1,0:T(8,128)S(1)} fusion(f32[1024,256,8]{1,0,2:T(8,128)} %get-tuple-element.269, f32[8,256]{1,0:T(8,128)S(1)} %select_maximum_fusion.2, pred[256,1024]{0,1:T(8,128)(4,1)S(1)} %compare_and_fusion.2), kind=kLoop, calls=%fused_computation.6.clone.1 | loop fusion | flops 8386560 | bytes 8667136 | tf_op jit(solution)/shard_map/while/body/eval_jaxpr/reduce_sum | solution.py:85
  313.4 3.4 fusion.80
  319.5 5.7 %fusion.77 = (f32[8,256]{1,0:T(8,128)S(1)}, f32[1024,256,8]{1,0,2:T(8,128)}) fusion(pred[256,1024]{0,1:T(8,128)(4,1)S(1)} %compare_and_fusion.2, bf16[256,1,8,128]{3,0,2,1:T(8,128)(2,1)S(1)} %get-tuple-element.308, bf16[8,1024,1,128]{3,1,2,0:T(8,128)(2,1)} %get-tuple-element.307, s32[]{:T(128)} %get-tuple-element.286), kind=kOutput, calls=%fused_computation.3.clone.1 | convolution fusion | flops 543160320 | bytes 9445888 | tf_op jit(solution)/shard_map/while/body/eval_jaxpr/tgjd,sgd->gjts/dot_general | solution.py:75
  325.2 5.2 %fusion.78 = f32[8,256]{1,0:T(8,128)S(1)} fusion(f32[1024,256,8]{1,0,2:T(8,128)} %get-tuple-element.269, f32[8,256]{1,0:T(8,128)S(1)} %select_maximum_fusion.2, pred[256,1024]{0,1:T(8,128)(4,1)S(1)} %compare_and_fusion.2), kind=kLoop, calls=%fused_computation.6.clone.1 | loop fusion | flops 8386560 | bytes 8667136 | tf_op jit(solution)/shard_map/while/body/eval_jaxpr/reduce_sum | solution.py:85
  331.0 3.4 fusion.80
  337.0 5.7 %fusion.77 = (f32[8,256]{1,0:T(8,128)S(1)}, f32[1024,256,8]{1,0,2:T(8,128)}) fusion(pred[256,1024]{0,1:T(8,128)(4,1)S(1)} %compare_and_fusion.2, bf16[256,1,8,128]{3,0,2,1:T(8,128)(2,1)S(1)} %get-tuple-element.308, bf16[8,1024,1,128]{3,1,2,0:T(8,128)(2,1)} %get-tuple-element.307, s32[]{:T(128)} %get-tuple-element.286), kind=kOutput, calls=%fused_computation.3.clone.1 | convolution fusion | flops 543160320 | bytes 9445888 | tf_op jit(solution)/shard_map/while/body/eval_jaxpr/tgjd,sgd->gjts/dot_general | solution.py:75
  342.8 5.2 %fusion.78 = f32[8,256]{1,0:T(8,128)S(1)} fusion(f32[1024,256,8]{1,0,2:T(8,128)} %get-tuple-element.269, f32[8,256]{1,0:T(8,128)S(1)} %select_maximum_fusion.2, pred[256,1024]{0,1:T(8,128)(4,1)S(1)} %compare_and_fusion.2), kind=kLoop, calls=%fused_computation.6.clone.1 | loop fusion | flops 8386560 | bytes 8667136 | tf_op jit(solution)/shard_map/while/body/eval_jaxpr/reduce_sum | solution.py:85
  348.5 3.4 fusion.80
  354.6 5.7 %fusion.77 = (f32[8,256]{1,0:T(8,128)S(1)}, f32[1024,256,8]{1,0,2:T(8,128)}) fusion(pred[256,1024]{0,1:T(8,128)(4,1)S(1)} %compare_and_fusion.2, bf16[256,1,8,128]{3,0,2,1:T(8,128)(2,1)S(1)} %get-tuple-element.308, bf16[8,1024,1,128]{3,1,2,0:T(8,128)(2,1)} %get-tuple-element.307, s32[]{:T(128)} %get-tuple-element.286), kind=kOutput, calls=%fused_computation.3.clone.1 | convolution fusion | flops 543160320 | bytes 9445888 | tf_op jit(solution)/shard_map/while/body/eval_jaxpr/tgjd,sgd->gjts/dot_general | solution.py:75
  360.4 5.2 %fusion.78 = f32[8,256]{1,0:T(8,128)S(1)} fusion(f32[1024,256,8]{1,0,2:T(8,128)} %get-tuple-element.269, f32[8,256]{1,0:T(8,128)S(1)} %select_maximum_fusion.2, pred[256,1024]{0,1:T(8,128)(4,1)S(1)} %compare_and_fusion.2), kind=kLoop, calls=%fused_computation.6.clone.1 | loop fusion | flops 8386560 | bytes 8667136 | tf_op jit(solution)/shard_map/while/body/eval_jaxpr/reduce_sum | solution.py:85
  366.1 3.4 fusion.80
  372.2 5.7 %fusion.77 = (f32[8,256]{1,0:T(8,128)S(1)}, f32[1024,256,8]{1,0,2:T(8,128)}) fusion(pred[256,1024]{0,1:T(8,128)(4,1)S(1)} %compare_and_fusion.2, bf16[256,1,8,128]{3,0,2,1:T(8,128)(2,1)S(1)} %get-tuple-element.308, bf16[8,1024,1,128]{3,1,2,0:T(8,128)(2,1)} %get-tuple-element.307, s32[]{:T(128)} %get-tuple-element.286), kind=kOutput, calls=%fused_computation.3.clone.1 | convolution fusion | flops 543160320 | bytes 9445888 | tf_op jit(solution)/shard_map/while/body/eval_jaxpr/tgjd,sgd->gjts/dot_general | solution.py:75
  377.9 5.2 %fusion.78 = f32[8,256]{1,0:T(8,128)S(1)} fusion(f32[1024,256,8]{1,0,2:T(8,128)} %get-tuple-element.269, f32[8,256]{1,0:T(8,128)S(1)} %select_maximum_fusion.2, pred[256,1024]{0,1:T(8,128)(4,1)S(1)} %compare_and_fusion.2), kind=kLoop, calls=%fused_computation.6.clone.1 | loop fusion | flops 8386560 | bytes 8667136 | tf_op jit(solution)/shard_map/while/body/eval_jaxpr/reduce_sum | solution.py:85
  383.7 3.4 fusion.80
  (179 shorter events, 51.2 us)
Async XLA Ops:
  7.2 193.3 %copy-start = (bf16[256,1024]{1,0:T(8,128)(2,1)S(1)}, bf16[256,1024]{1,0:T(8,128)(2,1)}, u32[]{:S(2)}) copy-start(bf16[256,1024]{1,0:T(8,128)(2,1)} %param.11) | copy-start | bytes 1572868
  7.2 126.5 %copy-start.6 = (s32[256]{0:T(256)S(1)}, s32[256]{0:T(256)}, u32[]{:S(2)}) copy-start(s32[256]{0:T(256)} %param.19) | copy-start | bytes 3076
  7.2 126.0 %copy-start.4 = (bf16[256,1024]{1,0:T(8,128)(2,1)S(1)}, bf16[256,1024]{1,0:T(8,128)(2,1)}, u32[]{:S(2)}) copy-start(bf16[256,1024]{1,0:T(8,128)(2,1)} %param.16) | copy-start | bytes 1572868
  7.2 240.3 %all-gather.4.cloned.1.call-start = ((), (), s32[]{:S(2)}) async-start(), calls=%async_computation | async-start | bytes 2162688 | tf_op jit(solution)/shard_map/all_gather | solution.py:164
  7.9 239.6 %all-gather.6.cloned.1.call-start = ((), (), s32[]{:S(2)}) async-start(), calls=%async_computation.1 | async-start | bytes 2162688 | tf_op jit(solution)/shard_map/all_gather | solution.py:165
  9.3 5.4 %collective-permute-start = (f32[1]{0:T(128)}, f32[1]{0:T(128)}, u32[]{:S(2)}, u32[]{:S(2)}) collective-permute-start(f32[1]{0:T(128)} %slice.4), channel_id=1, source_target_pairs={{0,8},{8,16},{16,24},{24,32},{32,40},{40,48},{48,56},{56,64},{64,7... | collective-permute-start | bytes 20 | tf_op jit(solution)/shard_map/ppermute | solution.py:17
  13.4 42.0 %copy-start.5 = (bf16[256,1024]{0,1:T(8,128)(2,1)}, bf16[256,1024]{0,1:T(8,128)(2,1)S(1)}, u32[]{:S(2)}) copy-start(bf16[256,1024]{0,1:T(8,128)(2,1)S(1)} %copy.50) | copy-start | bytes 1572868
  15.4 6.2 %collective-permute-start.1 = (f32[1]{0:T(128)}, f32[1]{0:T(128)}, u32[]{:S(2)}, u32[]{:S(2)}) collective-permute-start(f32[1]{0:T(128)} %select_n.151), channel_id=1, source_target_pairs={{0,8},{8,16},{16,24},{24,32},{32,40},{40,48},{48,56},{56,64},{64,7... | collective-permute-start | bytes 20 | tf_op jit(solution)/shard_map/ppermute | solution.py:23
  22.2 6.9 %collective-permute-start.2 = (f32[1]{0:T(128)}, f32[1]{0:T(128)}, u32[]{:S(2)}, u32[]{:S(2)}) collective-permute-start(f32[1]{0:T(128)} %select_n.152), channel_id=1, source_target_pairs={{0,16},{8,24},{16,32},{24,40},{32,48},{40,56},{48,64},{56,72},{64,... | collective-permute-start | bytes 20 | tf_op jit(solution)/shard_map/ppermute | solution.py:23
  29.7 5.5 %collective-permute-start.3 = (f32[1]{0:T(128)}, f32[1]{0:T(128)}, u32[]{:S(2)}, u32[]{:S(2)}) collective-permute-start(f32[1]{0:T(128)} %select_n.153), channel_id=1, source_target_pairs={{0,32},{8,40},{16,48},{24,56},{32,64},{40,72},{48,80},{56,88},{64,... | collective-permute-start | bytes 20 | tf_op jit(solution)/shard_map/ppermute | solution.py:23
  35.9 7.5 %collective-permute-start.4 = (f32[1]{0:T(128)}, f32[1]{0:T(128)}, u32[]{:S(2)}, u32[]{:S(2)}) collective-permute-start(f32[1]{0:T(128)} %select_n.154), channel_id=1, source_target_pairs={{0,64},{8,72},{16,80},{24,88},{32,96},{40,104},{48,112},{56,120},{... | collective-permute-start | bytes 20 | tf_op jit(solution)/shard_map/ppermute | solution.py:23
  44.0 9.4 %collective-permute-start.5 = (f32[1]{0:T(128)}, f32[1]{0:T(128)}, u32[]{:S(2)}, u32[]{:S(2)}) collective-permute-start(f32[1]{0:T(128)} %select_n.155), channel_id=1, source_target_pairs={{0,128},{8,136},{16,144},{24,152},{32,160},{40,168},{48,176},{56,1... | collective-permute-start | bytes 20 | tf_op jit(solution)/shard_map/ppermute | solution.py:23
  56.8 23.3 %collective-permute-start.11 = (f32[8,128,128]{2,1,0:T(8,128)S(1)}, f32[8,128,128]{2,1,0:T(8,128)S(1)}, u32[]{:S(2)}, u32[]{:S(2)}) collective-permute-start(f32[8,128,128]{2,1,0:T(8,128)S(1)} %convolution_add_fusion), channel_id=1, source_target_pairs={{0,8},{8,16},{16,24},{24,32},{32,40},{40,48},{48,56},{56,64},{64,7... | collective-permute-start | bytes 1572872 | tf_op jit(solution)/shard_map/ppermute | solution.py:17
  80.1 17.0 %collective-permute-start.12 = (f32[8,128,128]{2,1,0:T(8,128)S(1)}, f32[8,128,128]{2,1,0:T(8,128)S(1)}, u32[]{:S(2)}, u32[]{:S(2)}) collective-permute-start(f32[8,128,128]{2,1,0:T(8,128)S(1)} %broadcast_select_fusion), channel_id=1, source_target_pairs={{0,8},{8,16},{16,24},{24,32},{32,40},{40,48},{48,56},{56,64},{64,7... | collective-permute-start | bytes 1572872 | tf_op jit(solution)/shard_map/ppermute | solution.py:23
  86.6 10.5 %collective-permute-start.6 = (f32[8]{0:T(128)S(1)}, f32[8]{0:T(128)S(1)}, u32[]{:S(2)}, u32[]{:S(2)}) collective-permute-start(f32[8]{0:T(128)S(1)} %get-tuple-element.190), channel_id=1, source_target_pairs={{0,8},{8,16},{16,24},{24,32},{32,40},{40,48},{48,56},{56,64},{64,7... | collective-permute-start | bytes 104 | tf_op jit(solution)/shard_map/ppermute | solution.py:17
  97.2 13.5 %collective-permute-start.13 = (f32[8,128,128]{2,1,0:T(8,128)S(1)}, f32[8,128,128]{2,1,0:T(8,128)S(1)}, u32[]{:S(2)}, u32[]{:S(2)}) collective-permute-start(f32[8,128,128]{2,1,0:T(8,128)S(1)} %add_select_fusion.4), channel_id=1, source_target_pairs={{0,16},{8,24},{16,32},{24,40},{32,48},{40,56},{48,64},{56,72},{64,... | collective-permute-start | bytes 1572872 | tf_op jit(solution)/shard_map/ppermute | solution.py:23
  99.8 10.9 %collective-permute-start.7 = (f32[8]{0:T(128)S(1)}, f32[8]{0:T(128)S(1)}, u32[]{:S(2)}, u32[]{:S(2)}) collective-permute-start(f32[8]{0:T(128)S(1)} %get-tuple-element.181), channel_id=1, source_target_pairs={{0,8},{8,16},{16,24},{24,32},{32,40},{40,48},{48,56},{56,64},{64,7... | collective-permute-start | bytes 104 | tf_op jit(solution)/shard_map/ppermute | solution.py:23
  110.8 20.2 %collective-permute-start.14 = (f32[8,128,128]{2,1,0:T(8,128)S(1)}, f32[8,128,128]{2,1,0:T(8,128)S(1)}, u32[]{:S(2)}, u32[]{:S(2)}) collective-permute-start(f32[8,128,128]{2,1,0:T(8,128)S(1)} %add_select_fusion.3), channel_id=1, source_target_pairs={{0,32},{8,40},{16,48},{24,56},{32,64},{40,72},{48,80},{56,88},{64,... | collective-permute-start | bytes 1572872 | tf_op jit(solution)/shard_map/ppermute | solution.py:23
  113.5 11.7 %collective-permute-start.8 = (f32[8]{0:T(128)S(1)}, f32[8]{0:T(128)S(1)}, u32[]{:S(2)}, u32[]{:S(2)}) collective-permute-start(f32[8]{0:T(128)S(1)} %get-tuple-element.179), channel_id=1, source_target_pairs={{0,16},{8,24},{16,32},{24,40},{32,48},{40,56},{48,64},{56,72},{64,... | collective-permute-start | bytes 104 | tf_op jit(solution)/shard_map/ppermute | solution.py:23
  125.2 81.3 %copy-start.8 = (f32[8]{0:T(128)}, f32[8]{0:T(128)S(1)}, u32[]{:S(2)}) copy-start(f32[8]{0:T(128)S(1)} %get-tuple-element.177) | copy-start | bytes 100
  131.1 115.4 %copy-start.7 = (f32[1024]{0:T(1024)S(1)}, f32[1024]{0:T(1024)}, u32[]{:S(2)}) copy-start(f32[1024]{0:T(1024)} %param.15) | copy-start | bytes 12292
  131.1 76.1 %collective-permute-start.15 = (f32[8,128,128]{2,1,0:T(8,128)S(1)}, f32[8,128,128]{2,1,0:T(8,128)}, u32[]{:S(2)}, u32[]{:S(2)}) collective-permute-start(f32[8,128,128]{2,1,0:T(8,128)S(1)} %add_select_fusion.2), channel_id=1, source_target_pairs={{0,64},{8,72},{16,80},{24,88},{32,96},{40,104},{48,112},{56,120},{... | collective-permute-start | bytes 1572872 | tf_op jit(solution)/shard_map/ppermute | solution.py:23
  201.1 5.4 %collective-permute-start.9 = (f32[8]{0:T(128)S(1)}, f32[8]{0:T(128)S(1)}, u32[]{:S(2)}, u32[]{:S(2)}) collective-permute-start(f32[8]{0:T(128)S(1)} %get-tuple-element.177), channel_id=1, source_target_pairs={{0,32},{8,40},{16,48},{24,56},{32,64},{40,72},{48,80},{56,88},{64,... | collective-permute-start | bytes 104 | tf_op jit(solution)/shard_map/ppermute | solution.py:23
  208.3 20.6 %collective-permute-start.16 = (f32[8,128,128]{2,1,0:T(8,128)S(1)}, f32[8,128,128]{2,1,0:T(8,128)S(1)}, u32[]{:S(2)}, u32[]{:S(2)}) collective-permute-start(f32[8,128,128]{2,1,0:T(8,128)S(1)} %add_select_fusion.1), channel_id=1, source_target_pairs={{0,128},{8,136},{16,144},{24,152},{32,160},{40,168},{48,176},{56,1... | collective-permute-start | bytes 1572872 | tf_op jit(solution)/shard_map/ppermute | solution.py:23
  212.7 9.8 %collective-permute-start.10 = (f32[8]{0:T(128)S(1)}, f32[8]{0:T(128)S(1)}, u32[]{:S(2)}, u32[]{:S(2)}) collective-permute-start(f32[8]{0:T(128)S(1)} %get-tuple-element.175), channel_id=1, source_target_pairs={{0,64},{8,72},{16,80},{24,88},{32,96},{40,104},{48,112},{56,120},{... | collective-permute-start | bytes 104 | tf_op jit(solution)/shard_map/ppermute | solution.py:23
  249.1 11.0 %copy-start.2 = (f32[8,256,128]{2,1,0:T(8,128)S(1)}, f32[8,256,128]{2,1,0:T(8,128)}, u32[]{:S(2)}) copy-start(f32[8,256,128]{2,1,0:T(8,128)} %get-tuple-element.289) | copy-start | bytes 3145732 | tf_op jit(solution)/shard_map/while
  254.8 5.8 %copy-start.1 = (f32[1024,256,8]{1,0,2:T(8,128)S(1)}, f32[1024,256,8]{1,0,2:T(8,128)}, u32[]{:S(2)}) copy-start(f32[1024,256,8]{1,0,2:T(8,128)} %get-tuple-element.269) | copy-start | bytes 25165828 | tf_op jit(solution)/shard_map/while
  264.1 1.0 copy-start.3
  266.7 11.0 %copy-start.2 = (f32[8,256,128]{2,1,0:T(8,128)S(1)}, f32[8,256,128]{2,1,0:T(8,128)}, u32[]{:S(2)}) copy-start(f32[8,256,128]{2,1,0:T(8,128)} %get-tuple-element.289) | copy-start | bytes 3145732 | tf_op jit(solution)/shard_map/while
  272.4 5.8 %copy-start.1 = (f32[1024,256,8]{1,0,2:T(8,128)S(1)}, f32[1024,256,8]{1,0,2:T(8,128)}, u32[]{:S(2)}) copy-start(f32[1024,256,8]{1,0,2:T(8,128)} %get-tuple-element.269) | copy-start | bytes 25165828 | tf_op jit(solution)/shard_map/while
  281.6 1.0 copy-start.3
  284.3 11.0 %copy-start.2 = (f32[8,256,128]{2,1,0:T(8,128)S(1)}, f32[8,256,128]{2,1,0:T(8,128)}, u32[]{:S(2)}) copy-start(f32[8,256,128]{2,1,0:T(8,128)} %get-tuple-element.289) | copy-start | bytes 3145732 | tf_op jit(solution)/shard_map/while
  290.0 5.8 %copy-start.1 = (f32[1024,256,8]{1,0,2:T(8,128)S(1)}, f32[1024,256,8]{1,0,2:T(8,128)}, u32[]{:S(2)}) copy-start(f32[1024,256,8]{1,0,2:T(8,128)} %get-tuple-element.269) | copy-start | bytes 25165828 | tf_op jit(solution)/shard_map/while
  299.2 1.0 copy-start.3
  301.9 11.0 %copy-start.2 = (f32[8,256,128]{2,1,0:T(8,128)S(1)}, f32[8,256,128]{2,1,0:T(8,128)}, u32[]{:S(2)}) copy-start(f32[8,256,128]{2,1,0:T(8,128)} %get-tuple-element.289) | copy-start | bytes 3145732 | tf_op jit(solution)/shard_map/while
  307.6 5.8 %copy-start.1 = (f32[1024,256,8]{1,0,2:T(8,128)S(1)}, f32[1024,256,8]{1,0,2:T(8,128)}, u32[]{:S(2)}) copy-start(f32[1024,256,8]{1,0,2:T(8,128)} %get-tuple-element.269) | copy-start | bytes 25165828 | tf_op jit(solution)/shard_map/while
  316.8 1.0 copy-start.3
  319.5 11.0 %copy-start.2 = (f32[8,256,128]{2,1,0:T(8,128)S(1)}, f32[8,256,128]{2,1,0:T(8,128)}, u32[]{:S(2)}) copy-start(f32[8,256,128]{2,1,0:T(8,128)} %get-tuple-element.289) | copy-start | bytes 3145732 | tf_op jit(solution)/shard_map/while
  325.2 5.8 %copy-start.1 = (f32[1024,256,8]{1,0,2:T(8,128)S(1)}, f32[1024,256,8]{1,0,2:T(8,128)}, u32[]{:S(2)}) copy-start(f32[1024,256,8]{1,0,2:T(8,128)} %get-tuple-element.269) | copy-start | bytes 25165828 | tf_op jit(solution)/shard_map/while
  334.4 1.0 copy-start.3
  337.0 11.0 %copy-start.2 = (f32[8,256,128]{2,1,0:T(8,128)S(1)}, f32[8,256,128]{2,1,0:T(8,128)}, u32[]{:S(2)}) copy-start(f32[8,256,128]{2,1,0:T(8,128)} %get-tuple-element.289) | copy-start | bytes 3145732 | tf_op jit(solution)/shard_map/while
  342.8 5.8 %copy-start.1 = (f32[1024,256,8]{1,0,2:T(8,128)S(1)}, f32[1024,256,8]{1,0,2:T(8,128)}, u32[]{:S(2)}) copy-start(f32[1024,256,8]{1,0,2:T(8,128)} %get-tuple-element.269) | copy-start | bytes 25165828 | tf_op jit(solution)/shard_map/while
  352.0 1.0 copy-start.3
  354.6 11.0 %copy-start.2 = (f32[8,256,128]{2,1,0:T(8,128)S(1)}, f32[8,256,128]{2,1,0:T(8,128)}, u32[]{:S(2)}) copy-start(f32[8,256,128]{2,1,0:T(8,128)} %get-tuple-element.289) | copy-start | bytes 3145732 | tf_op jit(solution)/shard_map/while
  360.4 5.8 %copy-start.1 = (f32[1024,256,8]{1,0,2:T(8,128)S(1)}, f32[1024,256,8]{1,0,2:T(8,128)}, u32[]{:S(2)}) copy-start(f32[1024,256,8]{1,0,2:T(8,128)} %get-tuple-element.269) | copy-start | bytes 25165828 | tf_op jit(solution)/shard_map/while
  369.6 1.0 copy-start.3
  372.2 11.0 %copy-start.2 = (f32[8,256,128]{2,1,0:T(8,128)S(1)}, f32[8,256,128]{2,1,0:T(8,128)}, u32[]{:S(2)}) copy-start(f32[8,256,128]{2,1,0:T(8,128)} %get-tuple-element.289) | copy-start | bytes 3145732 | tf_op jit(solution)/shard_map/while
  377.9 5.8 %copy-start.1 = (f32[1024,256,8]{1,0,2:T(8,128)S(1)}, f32[1024,256,8]{1,0,2:T(8,128)}, u32[]{:S(2)}) copy-start(f32[1024,256,8]{1,0,2:T(8,128)} %get-tuple-element.269) | copy-start | bytes 25165828 | tf_op jit(solution)/shard_map/while
  (1 other events, 1.0 us)
Sparse Core Ops, SparseCore 0:
  10.6 76.8 all-gather.3
  90.1 84.0 all-gather.5

commit v2 on v1

--- a/solution.py
+++ b/solution.py
@@ -1,12 +1,114 @@
-from functools import partial
 import math
 
 import jax
 import jax.numpy as jnp
 from jax import lax
+from jax.experimental import pallas as pl
+from jax.experimental.pallas import tpu as pltpu
 from jax.sharding import PartitionSpec as P
 
 BLOCK = 256
+KEY_BLOCK = 512
+
+
+def flash_body(sref, q_ref, k_ref, v_ref, st_ref, o_ref, m_ref, l_ref, acc_ref, *, heads, width, scale):
+    j = pl.program_id(0)
+    lo, hi, flo, fhi, q0 = sref[0], sref[1], sref[2], sref[3], sref[4]
+    rows = q_ref.shape[0]
+    kb = k_ref.shape[0]
+
+    @pl.when(j == 0)
+    def _():
+        m_ref[...] = jnp.full(m_ref.shape, -1e30, jnp.float32)
+        l_ref[...] = jnp.zeros(l_ref.shape, jnp.float32)
+        acc_ref[...] = jnp.zeros(acc_ref.shape, jnp.float32)
+
+    def step(masked):
+        k = k_ref[...]
+        v = v_ref[...]
+        if masked:
+            kpos = j * kb + lax.broadcasted_iota(jnp.int32, (rows, kb), 1)
+            qpos = q0 + lax.broadcasted_iota(jnp.int32, (rows, kb), 0)
+            valid = (kpos <= qpos) & (kpos >= st_ref[...])
+        for h in range(heads):
+            q = q_ref[:, h * width:(h + 1) * width]
+            s = lax.dot_general(q, k, (((1,), (1,)), ((), ())), preferred_element_type=jnp.float32) * scale
+            m_prev = m_ref[h]
+            if masked:
+                top = jnp.max(jnp.where(valid, s, -1e30), axis=1, keepdims=True)
+            else:
+                top = jnp.max(s, axis=1, keepdims=True)
+            m_new = jnp.maximum(m_prev, top)
+            corr = jnp.exp(m_prev - m_new)
+            e = jnp.exp(s - m_new)
+            p = jnp.where(valid, e, 0.0) if masked else e
+            l_ref[h] = l_ref[h] * corr + jnp.sum(p, axis=1, keepdims=True)
+            pv = jnp.dot(p.astype(jnp.bfloat16), v, preferred_element_type=jnp.float32)
+            acc_ref[h] = acc_ref[h] * corr + pv
+            m_ref[h] = m_new
+
+    inside = (j >= lo) & (j <= hi)
+    full = (j >= flo) & (j <= fhi)
+
+    @pl.when(inside & full)
+    def _():
+        step(False)
+
+    @pl.when(inside & jnp.logical_not(full))
+    def _():
+        step(True)
+
+    @pl.when(j == pl.num_programs(0) - 1)
+    def _():
+        for h in range(heads):
+            o_ref[:, h * width:(h + 1) * width] = (acc_ref[h] / l_ref[h]).astype(o_ref.dtype)
+
+
+def flash_attention(q, keys, values, starts, q0):
+    rows, total = q.shape
+    length, width = keys.shape
+    heads = total // width
+    kb = min(KEY_BLOCK, length)
+    nk = length // kb
+    scale = 1.0 / math.sqrt(width)
+    first = starts[0]
+    last_start = starts[rows - 1]
+    lo = first // kb
+    hi = (q0 + rows - 1) // kb
+    flo = (last_start + kb - 1) // kb
+    fhi = (q0 + 1) // kb - 1
+    sref = jnp.stack([lo, hi, flo, fhi, q0]).astype(jnp.int32)
+
+    def kv_map(j, s):
+        return (jnp.minimum(jnp.maximum(j, s[0]), s[1]), 0)
+
+    kernel = lambda *refs: flash_body(*refs, heads=heads, width=width, scale=scale)
+    return pl.pallas_call(
+        kernel,
+        out_shape=jax.ShapeDtypeStruct((rows, total), jnp.bfloat16),
+        grid_spec=pltpu.PrefetchScalarGridSpec(
+            num_scalar_prefetch=1,
+            grid=(nk,),
+            in_specs=[
+                pl.BlockSpec((rows, total), lambda j, s: (0, 0)),
+                pl.BlockSpec((kb, width), kv_map),
+                pl.BlockSpec((kb, width), kv_map),
+                pl.BlockSpec((rows, 1), lambda j, s: (0, 0)),
+            ],
+            out_specs=pl.BlockSpec((rows, total), lambda j, s: (0, 0)),
+            scratch_shapes=[
+                pltpu.VMEM((heads, rows, 1), jnp.float32),
+                pltpu.VMEM((heads, rows, 1), jnp.float32),
+                pltpu.VMEM((heads, rows, width), jnp.float32),
+            ],
+        ),
+        compiler_params=pltpu.CompilerParams(dimension_semantics=("arbitrary",)),
+        cost_estimate=pl.CostEstimate(
+            flops=4 * rows * heads * length * width // 2,
+            transcendentals=rows * heads * length // 2,
+            bytes_accessed=2 * length * width * 2 + 2 * rows * total * 2,
+        ),
+    )(sref, q, keys, values, starts.reshape(rows, 1))
 
 
 def carried_in(part, axis, combine, identity):
@@ -62,33 +164,6 @@
     match = (last_e == last_l) | (last_l < 0.0)
     factor = jnp.where(match, dec_l, 0.0)
     return (factor[:, None, None] * state_e + state_l, dec_e * dec_l, jnp.maximum(last_e, last_l))
-
-
-def block_update(inner, queries, qpos, seg_rows, k_blk, v_blk, s_blk, kpos, scale):
-    mx, den, acc = inner
-    shared_heads = k_blk.shape[1]
-    group = queries.shape[2]
-    query_count = queries.shape[0]
-    key_count = k_blk.shape[0]
-    heads = shared_heads * group
-    s = (
-        jnp.einsum("tgjd,sgd->gjts", queries, k_blk, preferred_element_type=jnp.float32).reshape(
-            heads, query_count, key_count
-        )
-        * scale
-    )
-    mask = (kpos[None, :] <= qpos[:, None]) & (s_blk[None, :] == seg_rows[:, None])
-    top = jnp.max(jnp.where(mask[None], s, -1e30), axis=2)
-    new_mx = jnp.maximum(mx, top)
-    corr = jnp.exp(mx - new_mx)
-    p = jnp.where(mask[None], jnp.exp(s - new_mx[:, :, None]), 0.0)
-    den = den * corr + jnp.sum(p, axis=2)
-    weights = p.astype(jnp.bfloat16).reshape(shared_heads, group, query_count, key_count)
-    mixed = jnp.einsum(
-        "gjts,sgd->gjtd", weights, v_blk, preferred_element_type=jnp.float32
-    ).reshape(heads, query_count, -1)
-    acc = acc * corr[:, :, None] + mixed
-    return (new_mx, den, acc)
 
 
 def body(lin_q, lin_k, lin_v, decay_rates, norm_gain, soft_q, soft_k, soft_v, segment_ids):
@@ -134,75 +209,29 @@
     lin_out = (raw * lax.rsqrt(total_sq / count + 1e-06)[:, None] * norm_gain[None, :]).astype(
         jnp.bfloat16
     )
-    scale = 1.0 / math.sqrt(width)
     shared_heads = soft_k.shape[1] // width
     group = heads // shared_heads
     mine = lax.axis_index("seq")
-    plans = (soft_q, segment_ids, mine * tok)
-    query_sets = []
-    query_rows, seg_rows, first = plans
-    count_rows = query_rows.shape[0]
-    query_sets.append(
-        (
-            query_rows.reshape(count_rows, shared_heads, group, width),
-            first + jnp.arange(count_rows),
-            seg_rows,
-            first + count_rows - 1,
-        )
-    )
-    start_carry = tuple(
-        (
-            (
-                jnp.full((heads, qs[0].shape[0]), -1e30, jnp.float32),
-                jnp.zeros((heads, qs[0].shape[0]), jnp.float32),
-                jnp.zeros((heads, qs[0].shape[0], width), jnp.float32),
-            )
-            for qs in query_sets
-        )
-    )
-    carry = start_carry
     keys = lax.all_gather(soft_k, "seq", axis=0, tiled=True)
     values = lax.all_gather(soft_v, "seq", axis=0, tiled=True)
-    seg_keys = lax.all_gather(segment_ids, "seq", axis=0, tiled=True)
-    length = keys.shape[0]
-    rows = math.gcd(length, 1024)
-    count_blk = length // rows
-    k_blocks = keys.reshape(count_blk, rows, shared_heads, width)
-    v_blocks = values.reshape(count_blk, rows, shared_heads, width)
-    s_blocks = seg_keys.reshape(count_blk, rows)
-
-    def attend_one(state, item):
-        k_blk, v_blk, s_blk, index = item
-        blk_start = index * rows
-        kpos = blk_start + jnp.arange(rows)
-        fresh = []
-        for query_set, inner in zip(query_sets, state):
-            queries, qpos, seg_rows, last_pos = query_set
-            update = partial(
-                block_update,
-                queries=queries,
-                qpos=qpos,
-                seg_rows=seg_rows,
-                k_blk=k_blk,
-                v_blk=v_blk,
-                s_blk=s_blk,
-                kpos=kpos,
-                scale=scale,
+    seg_keys = lax.all_gather(segment_ids.astype(jnp.float32), "seq", axis=0, tiled=True)
+    starts = jnp.sum(
+        (seg_keys[None, :] < segment_ids.astype(jnp.float32)[:, None]).astype(jnp.int32), axis=1
+    )
+    q0 = (mine * tok).astype(jnp.int32)
+    pieces = []
+    for g in range(shared_heads):
+        cols = slice(g * group * width, (g + 1) * group * width)
+        pieces.append(
+            flash_attention(
+                soft_q[:, cols],
+                keys[:, g * width:(g + 1) * width],
+                values[:, g * width:(g + 1) * width],
+                starts,
+                q0,
             )
-            inner = update(inner)
-            fresh.append(inner)
-        return (tuple(fresh), None)
-
-    carry, _ = lax.scan(attend_one, carry, (k_blocks, v_blocks, s_blocks, jnp.arange(count_blk)))
-    outputs = []
-    for mx, den, acc in carry:
-        outputs.append(
-            (acc / den[:, :, None])
-            .transpose(1, 0, 2)
-            .reshape(acc.shape[1], heads * width)
-            .astype(jnp.bfloat16)
         )
-    soft_out = outputs[0]
+    soft_out = pieces[0] if shared_heads == 1 else jnp.concatenate(pieces, axis=1)
     return (lin_out, soft_out)
 
 

time: 401 us -> 297 us (0.74)
  the two profiles are of different devices: /device:TPU:166 before, /device:TPU:193 now
where the time goes in v2:
time: 297 us; the launch traced here: 296 us
  blocking collectives  89.4 us (30%)
  waiting for transfers between devices  80.6 us (27%)
  Pallas kernels  47.7 us (16%)
  starting transfers between devices  36.3 us (12%)
  between operations  24.9 us (8%)
  matrix products  6.99 us (2%)
  other arithmetic  5.55 us (2%)
  local copies, waits for them, and re-layouts  4.22 us (1%)
    ppermute x14, waiting for transfers between devices, carried_in(): earlier = jax.tree.map(lambda a: lax.ppermute(a, axis, pairs), state)  64.4 us
    psum x1, blocking collectives, body(): total_sq = lax.psum(sums, 'heads')  51 us
    pallas_call x1, Pallas kernels, flash_attention(): pl.pallas_call(kernel, out_shape=jax.ShapeDtypeStruct((rows, total), jnp....  47.7 us
    all_gather x1, blocking collectives, body(): lax.all_gather(segment_ids.astype(jnp.float32), 'seq', axis=0, tiled=True)  38.4 us
    ppermute x14, starting transfers between devices, carried_in(): earlier = jax.tree.map(lambda a: lax.ppermute(a, axis, pairs), state)  29.3 us
    ppermute x3, waiting for transfers between devices, carried_in(): lax.ppermute(a, axis, [(i, i + 1) for i in range(size - 1)])  15.5 us
    ppermute x3, starting transfers between devices, carried_in(): lax.ppermute(a, axis, [(i, i + 1) for i in range(size - 1)])  6.95 us
  transfers between devices with their start and end apart: 19, of which 13 were waited for; matrix products, arithmetic and copies ran while one was open for 6% of the time, Pallas kernels for 0%

profile of v2, /device:TPU:193, one launch (start us, length us, event | category | flops | bytes accessed | tf_op | source)
XLA Modules:
  0.0 295.7 jit_solution(676448539581319536)
XLA Ops:
  7.2 0.7 all-gather.4.cloned.1.call-update
  8.0 0.7 convert_element_type.75
  8.6 0.6 slice.10
  9.2 3.1 %collective-permute-start = (f32[1]{0:T(128)}, f32[1]{0:T(128)}, u32[]{:S(2)}, u32[]{:S(2)}) collective-permute-start(f32[1]{0:T(128)} %slice.10), channel_id=1, source_target_pairs={{0,8},{8,16},{16,24},{24,32},{32,40},{40,48},{48,56},{56,64},{64,7... | collective-permute-start | bytes 20 | tf_op jit(solution)/shard_map/ppermute | solution.py:119
  12.4 1.2 copy.52
  14.2 0.7 multiply_exponential_fusion.1
  14.9 0.7 collective-permute-done
  16.3 3.1 %collective-permute-start.1 = (f32[1]{0:T(128)}, f32[1]{0:T(128)}, u32[]{:S(2)}, u32[]{:S(2)}) collective-permute-start(f32[1]{0:T(128)} %select_n.155), channel_id=1, source_target_pairs={{0,8},{8,16},{16,24},{24,32},{32,40},{40,48},{48,56},{56,64},{64,7... | collective-permute-start | bytes 20 | tf_op jit(solution)/shard_map/ppermute | solution.py:125
  19.3 3.3 %collective-permute-done.1 = f32[1]{0:T(128)} collective-permute-done((f32[1]{0:T(128)}, f32[1]{0:T(128)}, u32[]{:S(2)}, u32[]{:S(2)}) %collective-permute-start.1) | collective-permute-done | bytes 36 | tf_op jit(solution)/shard_map/ppermute | solution.py:125
  23.2 2.6 collective-permute-start.2
  25.9 4.0 %collective-permute-done.2 = f32[1]{0:T(128)} collective-permute-done((f32[1]{0:T(128)}, f32[1]{0:T(128)}, u32[]{:S(2)}, u32[]{:S(2)}) %collective-permute-start.2) | collective-permute-done | bytes 36 | tf_op jit(solution)/shard_map/ppermute | solution.py:125
  30.5 3.4 %collective-permute-start.3 = (f32[1]{0:T(128)}, f32[1]{0:T(128)}, u32[]{:S(2)}, u32[]{:S(2)}) collective-permute-start(f32[1]{0:T(128)} %select_n.157), channel_id=1, source_target_pairs={{0,32},{8,40},{16,48},{24,56},{32,64},{40,72},{48,80},{56,88},{64,... | collective-permute-start | bytes 20 | tf_op jit(solution)/shard_map/ppermute | solution.py:125
  33.8 1.3 collective-permute-done.3
  35.9 1.3 collective-permute-start.4
  37.2 7.2 %collective-permute-done.4 = f32[1]{0:T(128)} collective-permute-done((f32[1]{0:T(128)}, f32[1]{0:T(128)}, u32[]{:S(2)}, u32[]{:S(2)}) %collective-permute-start.4) | collective-permute-done | bytes 36 | tf_op jit(solution)/shard_map/ppermute | solution.py:125
  44.9 1.3 collective-permute-start.5
  46.2 7.0 %collective-permute-done.5 = f32[1]{0:T(128)} collective-permute-done((f32[1]{0:T(128)}, f32[1]{0:T(128)}, u32[]{:S(2)}, u32[]{:S(2)}) %collective-permute-start.5) | collective-permute-done | bytes 36 | tf_op jit(solution)/shard_map/ppermute | solution.py:125
  53.8 1.3 compare_convert_fusion.1
  55.2 1.3 convolution_add_fusion
  56.5 1.9 collective-permute-start.11
  58.5 14.8 %collective-permute-done.11 = f32[8,128,128]{2,1,0:T(8,128)S(1)} collective-permute-done((f32[8,128,128]{2,1,0:T(8,128)S(1)}, f32[8,128,128]{2,1,0:T(8,128)S(1)}, u32[]{:S(2)}, u32[]{:S(2)}) %collective-permute-start.11) | collective-permute-done | bytes 524320 | tf_op jit(solution)/shard_map/ppermute | solution.py:119
  73.3 1.9 collective-permute-start.12
  75.2 1.9 collective-permute-start.6
  77.1 38.4 %all-gather = f32[32,1,256]{2,1,0:T(1,128)S(1)} all-gather(f32[1,1,256]{2,1,0:T(1,128)S(1)} %bitcast.77), channel_id=1, replica_groups=mesh['seq'=32,'heads'=8] {'seq'}, dimensions={0}, use_global_device_ids=true | all-gather | bytes 33792 | tf_op jit(solution)/shard_map/all_gather | solution.py:217
  116.3 2.1 collective-permute-start.13
  119.2 3.2 %collective-permute-start.7 = (f32[8]{0:T(128)S(1)}, f32[8]{0:T(128)S(1)}, u32[]{:S(2)}, u32[]{:S(2)}) collective-permute-start(f32[8]{0:T(128)S(1)} %get-tuple-element.36), channel_id=1, source_target_pairs={{0,8},{8,16},{16,24},{24,32},{32,40},{40,48},{48,56},{56,64},{64,7... | collective-permute-start | bytes 104 | tf_op jit(solution)/shard_map/ppermute | solution.py:125
  122.4 6.2 %collective-permute-done.7 = f32[8]{0:T(128)S(1)} collective-permute-done((f32[8]{0:T(128)S(1)}, f32[8]{0:T(128)S(1)}, u32[]{:S(2)}, u32[]{:S(2)}) %collective-permute-start.7) | collective-permute-done | bytes 64 | tf_op jit(solution)/shard_map/ppermute | solution.py:125
  128.6 0.8 collective-permute-done.13
  129.5 2.5 collective-permute-start.14
  132.0 1.1 convert_reduce_fusion
  133.9 1.9 collective-permute-start.8
  135.8 4.8 %collective-permute-done.8 = f32[8]{0:T(128)S(1)} collective-permute-done((f32[8]{0:T(128)S(1)}, f32[8]{0:T(128)S(1)}, u32[]{:S(2)}, u32[]{:S(2)}) %collective-permute-start.8) | collective-permute-done | bytes 64 | tf_op jit(solution)/shard_map/ppermute | solution.py:125
  140.8 1.4 collective-permute-start.15
  142.2 0.6 fusion.34
  145.9 0.8 copy.49.refs_4_
  146.7 0.7 stack.23.refs_0_
  148.6 1.6 fusion.5
  150.2 1.9 collective-permute-start.9
  152.1 9.7 %collective-permute-done.9 = f32[8]{0:T(128)S(1)} collective-permute-done((f32[8]{0:T(128)S(1)}, f32[8]{0:T(128)S(1)}, u32[]{:S(2)}, u32[]{:S(2)}) %collective-permute-start.9) | collective-permute-done | bytes 64 | tf_op jit(solution)/shard_map/ppermute | solution.py:125
  162.0 1.3 collective-permute-start.16
  163.3 2.2 fusion.2
  165.5 1.3 collective-permute-start.10
  166.8 5.4 %collective-permute-done.10 = f32[8]{0:T(128)S(1)} collective-permute-done((f32[8]{0:T(128)S(1)}, f32[8]{0:T(128)S(1)}, u32[]{:S(2)}, u32[]{:S(2)}) %collective-permute-start.10) | collective-permute-done | bytes 64 | tf_op jit(solution)/shard_map/ppermute | solution.py:125
  172.2 14.7 %collective-permute-done.16 = f32[8,128,128]{2,1,0:T(8,128)} collective-permute-done((f32[8,128,128]{2,1,0:T(8,128)S(1)}, f32[8,128,128]{2,1,0:T(8,128)}, u32[]{:S(2)}, u32[]{:S(2)}) %collective-permute-start.16) | collective-permute-done | bytes 524320 | tf_op jit(solution)/shard_map/ppermute | solution.py:125
  187.0 1.8 multiply_reduce_fusion
  189.1 51.0 %psum.7 = f32[256]{0:T(256)S(1)} all-reduce(f32[256]{0:T(256)S(1)} %get-tuple-element.48), channel_id=1, replica_groups=mesh['seq'=32,'heads'=8] {'heads'}, use_global_device_ids=true, to_apply=%region_1.2 | all-reduce | flops 256 | bytes 2048 | tf_op jit(solution)/shard_map/psum | solution.py:207
  240.1 1.0 multiply_convert_fusion
  241.1 47.7 %shard_map.104 = bf16[256,1024]{1,0:T(8,128)(2,1)} custom-call(s32[5]{0:T(128)} %stack.23.refs_0_, bf16[256,1024]{1,0:T(8,128)(2,1)} %refs_1_.1, bf16[8192,128]{1,0:T(8,128)(2,1)} %all-gather.4.cloned.1.call-done.refs_2_, bf16[8192,128]{1,0:T(8,128)(2,1)} %all-gather.6.cloned.1.call-done.refs_3_, s32[256,1]{1,0:T(8,128)} %copy.49.refs_4_), custom_call_target="tpu_custom_call" | custom-call | flops 4294967296 | bytes 5242880 | tf_op jit(solution)/shard_map/pallas_call | solution.py:86
  (34 shorter events, 1.4 us)
Async XLA Ops:
  7.2 141.4 %copy-start = (bf16[256,1024]{1,0:T(8,128)(2,1)S(1)}, bf16[256,1024]{1,0:T(8,128)(2,1)}, u32[]{:S(2)}) copy-start(bf16[256,1024]{1,0:T(8,128)(2,1)} %param.9) | copy-start | bytes 1572868
  7.2 233.9 %all-gather.4.cloned.1.call-start = ((), (), s32[]{:S(2)}) async-start(), calls=%async_computation | async-start | bytes 2162688 | tf_op jit(solution)/shard_map/all_gather | solution.py:215
  7.9 233.2 %all-gather.6.cloned.1.call-start = ((), (), s32[]{:S(2)}) async-start(), calls=%async_computation.1 | async-start | bytes 2162688 | tf_op jit(solution)/shard_map/all_gather | solution.py:216
  9.2 6.4 %collective-permute-start = (f32[1]{0:T(128)}, f32[1]{0:T(128)}, u32[]{:S(2)}, u32[]{:S(2)}) collective-permute-start(f32[1]{0:T(128)} %slice.10), channel_id=1, source_target_pairs={{0,8},{8,16},{16,24},{24,32},{32,40},{40,48},{48,56},{56,64},{64,7... | collective-permute-start | bytes 20 | tf_op jit(solution)/shard_map/ppermute | solution.py:119
  13.6 41.6 %copy-start.1 = (bf16[256,1024]{0,1:T(8,128)(2,1)}, bf16[256,1024]{0,1:T(8,128)(2,1)S(1)}, u32[]{:S(2)}) copy-start(bf16[256,1024]{0,1:T(8,128)(2,1)S(1)} %copy.52) | copy-start | bytes 1572868
  16.3 6.3 %collective-permute-start.1 = (f32[1]{0:T(128)}, f32[1]{0:T(128)}, u32[]{:S(2)}, u32[]{:S(2)}) collective-permute-start(f32[1]{0:T(128)} %select_n.155), channel_id=1, source_target_pairs={{0,8},{8,16},{16,24},{24,32},{32,40},{40,48},{48,56},{56,64},{64,7... | collective-permute-start | bytes 20 | tf_op jit(solution)/shard_map/ppermute | solution.py:125
  23.2 6.6 %collective-permute-start.2 = (f32[1]{0:T(128)}, f32[1]{0:T(128)}, u32[]{:S(2)}, u32[]{:S(2)}) collective-permute-start(f32[1]{0:T(128)} %select_n.156), channel_id=1, source_target_pairs={{0,16},{8,24},{16,32},{24,40},{32,48},{40,56},{48,64},{56,72},{64,... | collective-permute-start | bytes 20 | tf_op jit(solution)/shard_map/ppermute | solution.py:125
  30.5 4.7 %collective-permute-start.3 = (f32[1]{0:T(128)}, f32[1]{0:T(128)}, u32[]{:S(2)}, u32[]{:S(2)}) collective-permute-start(f32[1]{0:T(128)} %select_n.157), channel_id=1, source_target_pairs={{0,32},{8,40},{16,48},{24,56},{32,64},{40,72},{48,80},{56,88},{64,... | collective-permute-start | bytes 20 | tf_op jit(solution)/shard_map/ppermute | solution.py:125
  35.9 8.5 %collective-permute-start.4 = (f32[1]{0:T(128)}, f32[1]{0:T(128)}, u32[]{:S(2)}, u32[]{:S(2)}) collective-permute-start(f32[1]{0:T(128)} %select_n.158), channel_id=1, source_target_pairs={{0,64},{8,72},{16,80},{24,88},{32,96},{40,104},{48,112},{56,120},{... | collective-permute-start | bytes 20 | tf_op jit(solution)/shard_map/ppermute | solution.py:125
  44.9 8.3 %collective-permute-start.5 = (f32[1]{0:T(128)}, f32[1]{0:T(128)}, u32[]{:S(2)}, u32[]{:S(2)}) collective-permute-start(f32[1]{0:T(128)} %select_n.159), channel_id=1, source_target_pairs={{0,128},{8,136},{16,144},{24,152},{32,160},{40,168},{48,176},{56,1... | collective-permute-start | bytes 20 | tf_op jit(solution)/shard_map/ppermute | solution.py:125
  56.5 16.7 %collective-permute-start.11 = (f32[8,128,128]{2,1,0:T(8,128)S(1)}, f32[8,128,128]{2,1,0:T(8,128)S(1)}, u32[]{:S(2)}, u32[]{:S(2)}) collective-permute-start(f32[8,128,128]{2,1,0:T(8,128)S(1)} %convolution_add_fusion), channel_id=1, source_target_pairs={{0,8},{8,16},{16,24},{24,32},{32,40},{40,48},{48,56},{56,64},{64,7... | collective-permute-start | bytes 1572872 | tf_op jit(solution)/shard_map/ppermute | solution.py:119
  73.3 42.9 %collective-permute-start.12 = (f32[8,128,128]{2,1,0:T(8,128)S(1)}, f32[8,128,128]{2,1,0:T(8,128)S(1)}, u32[]{:S(2)}, u32[]{:S(2)}) collective-permute-start(f32[8,128,128]{2,1,0:T(8,128)S(1)} %broadcast_select_fusion), channel_id=1, source_target_pairs={{0,8},{8,16},{16,24},{24,32},{32,40},{40,48},{48,56},{56,64},{64,7... | collective-permute-start | bytes 1572872 | tf_op jit(solution)/shard_map/ppermute | solution.py:125
  75.2 41.0 %collective-permute-start.6 = (f32[8]{0:T(128)S(1)}, f32[8]{0:T(128)S(1)}, u32[]{:S(2)}, u32[]{:S(2)}) collective-permute-start(f32[8]{0:T(128)S(1)} %get-tuple-element.45), channel_id=1, source_target_pairs={{0,8},{8,16},{16,24},{24,32},{32,40},{40,48},{48,56},{56,64},{64,7... | collective-permute-start | bytes 104 | tf_op jit(solution)/shard_map/ppermute | solution.py:119
  116.3 13.0 %collective-permute-start.13 = (f32[8,128,128]{2,1,0:T(8,128)S(1)}, f32[8,128,128]{2,1,0:T(8,128)S(1)}, u32[]{:S(2)}, u32[]{:S(2)}) collective-permute-start(f32[8,128,128]{2,1,0:T(8,128)S(1)} %add_select_fusion.4), channel_id=1, source_target_pairs={{0,16},{8,24},{16,32},{24,40},{32,48},{40,56},{48,64},{56,72},{64,... | collective-permute-start | bytes 1572872 | tf_op jit(solution)/shard_map/ppermute | solution.py:125
  119.2 9.4 %collective-permute-start.7 = (f32[8]{0:T(128)S(1)}, f32[8]{0:T(128)S(1)}, u32[]{:S(2)}, u32[]{:S(2)}) collective-permute-start(f32[8]{0:T(128)S(1)} %get-tuple-element.36), channel_id=1, source_target_pairs={{0,8},{8,16},{16,24},{24,32},{32,40},{40,48},{48,56},{56,64},{64,7... | collective-permute-start | bytes 104 | tf_op jit(solution)/shard_map/ppermute | solution.py:125
  129.5 11.1 %collective-permute-start.14 = (f32[8,128,128]{2,1,0:T(8,128)S(1)}, f32[8,128,128]{2,1,0:T(8,128)S(1)}, u32[]{:S(2)}, u32[]{:S(2)}) collective-permute-start(f32[8,128,128]{2,1,0:T(8,128)S(1)} %add_select_fusion.3), channel_id=1, source_target_pairs={{0,32},{8,40},{16,48},{24,56},{32,64},{40,72},{48,80},{56,88},{64,... | collective-permute-start | bytes 1572872 | tf_op jit(solution)/shard_map/ppermute | solution.py:125
  133.9 6.7 %collective-permute-start.8 = (f32[8]{0:T(128)S(1)}, f32[8]{0:T(128)S(1)}, u32[]{:S(2)}, u32[]{:S(2)}) collective-permute-start(f32[8]{0:T(128)S(1)} %get-tuple-element.25), channel_id=1, source_target_pairs={{0,16},{8,24},{16,32},{24,40},{32,48},{40,56},{48,64},{56,72},{64,... | collective-permute-start | bytes 104 | tf_op jit(solution)/shard_map/ppermute | solution.py:125
  140.7 22.5 %copy-start.2 = (bf16[256,1024]{0,1:T(8,128)(2,1)S(1)}, bf16[256,1024]{0,1:T(8,128)(2,1)}, u32[]{:S(2)}) copy-start(bf16[256,1024]{0,1:T(8,128)(2,1)} %copy-done.1) | copy-start | bytes 1572868
  140.8 21.1 %collective-permute-start.15 = (f32[8,128,128]{2,1,0:T(8,128)S(1)}, f32[8,128,128]{2,1,0:T(8,128)S(1)}, u32[]{:S(2)}, u32[]{:S(2)}) collective-permute-start(f32[8,128,128]{2,1,0:T(8,128)S(1)} %add_select_fusion.2), channel_id=1, source_target_pairs={{0,64},{8,72},{16,80},{24,88},{32,96},{40,104},{48,112},{56,120},{... | collective-permute-start | bytes 1572872 | tf_op jit(solution)/shard_map/ppermute | solution.py:125
  150.2 11.7 %collective-permute-start.9 = (f32[8]{0:T(128)S(1)}, f32[8]{0:T(128)S(1)}, u32[]{:S(2)}, u32[]{:S(2)}) collective-permute-start(f32[8]{0:T(128)S(1)} %get-tuple-element.23), channel_id=1, source_target_pairs={{0,32},{8,40},{16,48},{24,56},{32,64},{40,72},{48,80},{56,88},{64,... | collective-permute-start | bytes 104 | tf_op jit(solution)/shard_map/ppermute | solution.py:125
  162.0 25.0 %collective-permute-start.16 = (f32[8,128,128]{2,1,0:T(8,128)S(1)}, f32[8,128,128]{2,1,0:T(8,128)}, u32[]{:S(2)}, u32[]{:S(2)}) collective-permute-start(f32[8,128,128]{2,1,0:T(8,128)S(1)} %add_select_fusion.1), channel_id=1, source_target_pairs={{0,128},{8,136},{16,144},{24,152},{32,160},{40,168},{48,176},{56,1... | collective-permute-start | bytes 1572872 | tf_op jit(solution)/shard_map/ppermute | solution.py:125
  165.5 6.7 %collective-permute-start.10 = (f32[8]{0:T(128)S(1)}, f32[8]{0:T(128)S(1)}, u32[]{:S(2)}, u32[]{:S(2)}) collective-permute-start(f32[8]{0:T(128)S(1)} %get-tuple-element.21), channel_id=1, source_target_pairs={{0,64},{8,72},{16,80},{24,88},{32,96},{40,104},{48,112},{56,120},{... | collective-permute-start | bytes 104 | tf_op jit(solution)/shard_map/ppermute | solution.py:125
  187.0 53.2 %copy-start.3 = (f32[1024]{0:T(1024)S(1)}, f32[1024]{0:T(1024)}, u32[]{:S(2)}) copy-start(f32[1024]{0:T(1024)} %param.13) | copy-start | bytes 12292
Sparse Core Ops, SparseCore 0:
  10.6 77.9 all-gather.3
  91.2 79.2 all-gather.5

commit v3 on v2

--- a/solution.py
+++ b/solution.py
@@ -158,6 +158,13 @@
     return ((keep[:, None, None] * state + local, last), out)
 
 
+def combine_bounds(earlier, later):
+    last_e, first_e = earlier
+    last_l, first_l = later
+    keep = (last_e == last_l) | (last_l < 0.0)
+    return (jnp.maximum(last_e, last_l), jnp.where(keep, first_e, first_l))
+
+
 def combine_states(earlier, later):
     state_e, dec_e, last_e = earlier
     state_l, dec_l, last_l = later
@@ -214,11 +221,20 @@
     mine = lax.axis_index("seq")
     keys = lax.all_gather(soft_k, "seq", axis=0, tiled=True)
     values = lax.all_gather(soft_v, "seq", axis=0, tiled=True)
-    seg_keys = lax.all_gather(segment_ids.astype(jnp.float32), "seq", axis=0, tiled=True)
-    starts = jnp.sum(
-        (seg_keys[None, :] < segment_ids.astype(jnp.float32)[:, None]).astype(jnp.int32), axis=1
-    )
     q0 = (mine * tok).astype(jnp.int32)
+    seg_i = segment_ids.astype(jnp.float32)
+    below = jnp.sum((seg_i[None, :] < seg_i[:, None]).astype(jnp.int32), axis=1)
+    last_here = seg_i[tok - 1]
+    first_here = (q0 + jnp.sum((seg_i < last_here).astype(jnp.int32))).astype(jnp.float32)
+    last_before, first_before = carried_in(
+        (last_here.reshape(1), first_here.reshape(1)),
+        "seq",
+        combine_bounds,
+        (jnp.full((1,), -1.0, jnp.float32), jnp.zeros((1,), jnp.float32)),
+    )
+    starts = jnp.where(
+        seg_i == last_before[0], first_before[0].astype(jnp.int32), q0 + below
+    )
     pieces = []
     for g in range(shared_heads):
         cols = slice(g * group * width, (g + 1) * group * width)

time: 297 us -> 294 us (0.990)
  the two profiles are of different devices: /device:TPU:193 before, /device:TPU:229 now
where the time goes in v3:
time: 294 us; the launch traced here: 292 us
  waiting for transfers between devices  104 us (35%)
  Pallas kernels  52.6 us (18%)
  starting transfers between devices  50.6 us (17%)
  blocking collectives  39 us (13%)
  between operations  29.4 us (10%)
  matrix products  7 us (2%)
  other arithmetic  5.97 us (2%)
  local copies, waits for them, and re-layouts  4.33 us (1%)
    ppermute x19, waiting for transfers between devices, carried_in(): earlier = jax.tree.map(lambda a: lax.ppermute(a, axis, pairs), state)  92.8 us
    pallas_call x1, Pallas kernels, flash_attention(): pl.pallas_call(kernel, out_shape=jax.ShapeDtypeStruct((rows, total), jnp....  52.6 us
    psum x1, blocking collectives, body(): total_sq = lax.psum(sums, 'heads')  39 us
    ppermute x19, starting transfers between devices, carried_in(): earlier = jax.tree.map(lambda a: lax.ppermute(a, axis, pairs), state)  28.6 us
    ppermute x4, starting transfers between devices, carried_in(): lax.ppermute(a, axis, [(i, i + 1) for i in range(size - 1)])  21.9 us
    ppermute x4, waiting for transfers between devices, carried_in(): lax.ppermute(a, axis, [(i, i + 1) for i in range(size - 1)])  10.1 us
  transfers between devices with their start and end apart: 25, of which 19 were waited for; matrix products, arithmetic and copies ran while one was open for 6% of the time, Pallas kernels for 0%

profile of v3, /device:TPU:229, one launch (start us, length us, event | category | flops | bytes accessed | tf_op | source)
XLA Modules:
  0.0 292.5 jit_solution(9350529577654767182)
XLA Ops:
  9.3 2.8 collective-permute-start
  15.3 2.6 collective-permute-start.1
  17.9 1.6 collective-permute-done.1
  20.2 1.3 collective-permute-start.2
  21.5 4.9 %collective-permute-done.2 = f32[1]{0:T(128)} collective-permute-done((f32[1]{0:T(128)}, f32[1]{0:T(128)}, u32[]{:S(2)}, u32[]{:S(2)}) %collective-permute-start.2) | collective-permute-done | bytes 36 | tf_op jit(solution)/shard_map/ppermute | solution.py:125
  27.1 1.3 collective-permute-start.3
  28.4 2.9 %collective-permute-done.3 = f32[1]{0:T(128)} collective-permute-done((f32[1]{0:T(128)}, f32[1]{0:T(128)}, u32[]{:S(2)}, u32[]{:S(2)}) %collective-permute-start.3) | collective-permute-done | bytes 36 | tf_op jit(solution)/shard_map/ppermute | solution.py:125
  31.9 1.3 collective-permute-start.4
  33.2 4.9 %collective-permute-done.4 = f32[1]{0:T(128)} collective-permute-done((f32[1]{0:T(128)}, f32[1]{0:T(128)}, u32[]{:S(2)}, u32[]{:S(2)}) %collective-permute-start.4) | collective-permute-done | bytes 36 | tf_op jit(solution)/shard_map/ppermute | solution.py:125
  38.6 1.3 collective-permute-start.5
  39.9 7.0 %collective-permute-done.5 = f32[1]{0:T(128)} collective-permute-done((f32[1]{0:T(128)}, f32[1]{0:T(128)}, u32[]{:S(2)}, u32[]{:S(2)}) %collective-permute-start.5) | collective-permute-done | bytes 36 | tf_op jit(solution)/shard_map/ppermute | solution.py:125
  47.6 1.3 fusion.35
  49.0 1.3 convolution_add_fusion
  50.4 1.9 collective-permute-start.11
  52.3 8.0 %collective-permute-done.11 = f32[8,128,128]{2,1,0:T(8,128)S(1)} collective-permute-done((f32[8,128,128]{2,1,0:T(8,128)S(1)}, f32[8,128,128]{2,1,0:T(8,128)S(1)}, u32[]{:S(2)}, u32[]{:S(2)}) %collective-permute-start.11) | collective-permute-done | bytes 524320 | tf_op jit(solution)/shard_map/ppermute | solution.py:119
  60.3 1.9 collective-permute-start.12
  64.1 15.3 %collective-permute-start.17 = (f32[1]{0:T(128)}, f32[1]{0:T(128)}, u32[]{:S(2)}, u32[]{:S(2)}) collective-permute-start(f32[1]{0:T(128)} %bitcast.18), channel_id=1, source_target_pairs={{0,8},{8,16},{16,24},{24,32},{32,40},{40,48},{48,56},{56,64},{64,7... | collective-permute-start | bytes 20 | tf_op jit(solution)/shard_map/ppermute | solution.py:119
  79.4 1.9 collective-permute-start.6
  82.0 2.1 collective-permute-done.6
  84.2 1.3 collective-permute-start.13
  86.4 1.9 collective-permute-start.7
  88.3 4.1 %collective-permute-done.7 = f32[8]{0:T(128)S(1)} collective-permute-done((f32[8]{0:T(128)S(1)}, f32[8]{0:T(128)S(1)}, u32[]{:S(2)}, u32[]{:S(2)}) %collective-permute-start.7) | collective-permute-done | bytes 64 | tf_op jit(solution)/shard_map/ppermute | solution.py:125
  92.5 7.5 %collective-permute-done.13 = f32[8,128,128]{2,1,0:T(8,128)S(1)} collective-permute-done((f32[8,128,128]{2,1,0:T(8,128)S(1)}, f32[8,128,128]{2,1,0:T(8,128)S(1)}, u32[]{:S(2)}, u32[]{:S(2)}) %collective-permute-start.13) | collective-permute-done | bytes 524320 | tf_op jit(solution)/shard_map/ppermute | solution.py:125
  100.1 1.3 collective-permute-start.14
  102.1 2.6 collective-permute-start.18
  104.8 2.0 collective-permute-done.18
  107.3 1.3 collective-permute-start.19
  108.7 8.8 %collective-permute-done.19 = f32[1]{0:T(128)} collective-permute-done((f32[1]{0:T(128)}, f32[1]{0:T(128)}, u32[]{:S(2)}, u32[]{:S(2)}) %collective-permute-start.19) | collective-permute-done | bytes 36 | tf_op jit(solution)/shard_map/ppermute | solution.py:125
  118.1 1.3 collective-permute-start.20
  120.0 5.4 %collective-permute-done.20 = f32[1]{0:T(128)} collective-permute-done((f32[1]{0:T(128)}, f32[1]{0:T(128)}, u32[]{:S(2)}, u32[]{:S(2)}) %collective-permute-start.20) | collective-permute-done | bytes 36 | tf_op jit(solution)/shard_map/ppermute | solution.py:125
  126.0 1.3 collective-permute-start.21
  127.9 8.1 %collective-permute-done.21 = f32[1]{0:T(128)} collective-permute-done((f32[1]{0:T(128)}, f32[1]{0:T(128)}, u32[]{:S(2)}, u32[]{:S(2)}) %collective-permute-start.21) | collective-permute-done | bytes 36 | tf_op jit(solution)/shard_map/ppermute | solution.py:125
  136.7 1.3 collective-permute-start.22
  138.7 6.2 %collective-permute-done.22 = f32[1]{0:T(128)} collective-permute-done((f32[1]{0:T(128)}, f32[1]{0:T(128)}, u32[]{:S(2)}, u32[]{:S(2)}) %collective-permute-start.22) | collective-permute-done | bytes 36 | tf_op jit(solution)/shard_map/ppermute | solution.py:125
  145.5 1.3 collective-permute-start.8
  146.8 6.4 %collective-permute-done.8 = f32[8]{0:T(128)S(1)} collective-permute-done((f32[8]{0:T(128)S(1)}, f32[8]{0:T(128)S(1)}, u32[]{:S(2)}, u32[]{:S(2)}) %collective-permute-start.8) | collective-permute-done | bytes 64 | tf_op jit(solution)/shard_map/ppermute | solution.py:125
  153.3 1.4 collective-permute-start.15
  160.0 1.6 fusion.5
  162.9 4.5 %collective-permute-done.9 = f32[8]{0:T(128)S(1)} collective-permute-done((f32[8]{0:T(128)S(1)}, f32[8]{0:T(128)S(1)}, u32[]{:S(2)}, u32[]{:S(2)}) %collective-permute-start.9) | collective-permute-done | bytes 64 | tf_op jit(solution)/shard_map/ppermute | solution.py:125
  167.5 9.3 %collective-permute-done.15 = f32[8,128,128]{2,1,0:T(8,128)S(1)} collective-permute-done((f32[8,128,128]{2,1,0:T(8,128)S(1)}, f32[8,128,128]{2,1,0:T(8,128)S(1)}, u32[]{:S(2)}, u32[]{:S(2)}) %collective-permute-start.15) | collective-permute-done | bytes 524320 | tf_op jit(solution)/shard_map/ppermute | solution.py:125
  176.9 1.3 collective-permute-start.16
  178.2 2.2 fusion.2
  180.4 1.3 collective-permute-start.10
  181.7 4.2 %collective-permute-done.10 = f32[8]{0:T(128)S(1)} collective-permute-done((f32[8]{0:T(128)S(1)}, f32[8]{0:T(128)S(1)}, u32[]{:S(2)}, u32[]{:S(2)}) %collective-permute-start.10) | collective-permute-done | bytes 64 | tf_op jit(solution)/shard_map/ppermute | solution.py:125
  185.9 5.0 %collective-permute-done.16 = f32[8,128,128]{2,1,0:T(8,128)} collective-permute-done((f32[8,128,128]{2,1,0:T(8,128)S(1)}, f32[8,128,128]{2,1,0:T(8,128)}, u32[]{:S(2)}, u32[]{:S(2)}) %collective-permute-start.16) | collective-permute-done | bytes 524320 | tf_op jit(solution)/shard_map/ppermute | solution.py:125
  190.9 1.8 multiply_reduce_fusion
  193.1 39.0 %psum.7 = f32[256]{0:T(256)S(1)} all-reduce(f32[256]{0:T(256)S(1)} %get-tuple-element.48), channel_id=1, replica_groups=mesh['seq'=32,'heads'=8] {'heads'}, use_global_device_ids=true, to_apply=%region_1.2 | all-reduce | flops 256 | bytes 2048 | tf_op jit(solution)/shard_map/psum | solution.py:214
  233.0 52.6 %shard_map.104 = bf16[256,1024]{1,0:T(8,128)(2,1)} custom-call(s32[5]{0:T(128)} %stack.23.refs_0_, bf16[256,1024]{1,0:T(8,128)(2,1)} %refs_1_.1, bf16[8192,128]{1,0:T(8,128)(2,1)} %all-gather.3.cloned.1.call-done.refs_2_, bf16[8192,128]{1,0:T(8,128)(2,1)} %all-gather.5.cloned.1.call-done.refs_3_, s32[256,1]{1,0:T(8,128)} %copy.27.refs_4_), custom_call_target="tpu_custom_call" | custom-call | flops 4294967296 | bytes 5242880 | tf_op jit(solution)/shard_map/pallas_call | solution.py:86
  (49 shorter events, 11.1 us)
Async XLA Ops:
  7.2 152.9 %copy-start = (bf16[256,1024]{1,0:T(8,128)(2,1)S(1)}, bf16[256,1024]{1,0:T(8,128)(2,1)}, u32[]{:S(2)}) copy-start(bf16[256,1024]{1,0:T(8,128)(2,1)} %param.9) | copy-start | bytes 1572868
  7.2 55.1 %copy-start.3 = (s32[256]{0:T(256)S(1)}, s32[256]{0:T(256)}, u32[]{:S(2)}) copy-start(s32[256]{0:T(256)} %param.17) | copy-start | bytes 3076
  7.2 225.8 %all-gather.3.cloned.1.call-start = ((), (), s32[]{:S(2)}) async-start(), calls=%async_computation | async-start | bytes 2162688 | tf_op jit(solution)/shard_map/all_gather | solution.py:222
  7.9 225.1 %all-gather.5.cloned.1.call-start = ((), (), s32[]{:S(2)}) async-start(), calls=%async_computation.1 | async-start | bytes 2162688 | tf_op jit(solution)/shard_map/all_gather | solution.py:223
  9.3 5.4 %collective-permute-start = (f32[1]{0:T(128)}, f32[1]{0:T(128)}, u32[]{:S(2)}, u32[]{:S(2)}) collective-permute-start(f32[1]{0:T(128)} %slice.11), channel_id=1, source_target_pairs={{0,8},{8,16},{16,24},{24,32},{32,40},{40,48},{48,56},{56,64},{64,7... | collective-permute-start | bytes 20 | tf_op jit(solution)/shard_map/ppermute | solution.py:119
  13.4 35.6 %copy-start.1 = (bf16[256,1024]{0,1:T(8,128)(2,1)}, bf16[256,1024]{0,1:T(8,128)(2,1)S(1)}, u32[]{:S(2)}) copy-start(bf16[256,1024]{0,1:T(8,128)(2,1)S(1)} %copy.30) | copy-start | bytes 1572868
  15.3 4.2 %collective-permute-start.1 = (f32[1]{0:T(128)}, f32[1]{0:T(128)}, u32[]{:S(2)}, u32[]{:S(2)}) collective-permute-start(f32[1]{0:T(128)} %select_n.211), channel_id=1, source_target_pairs={{0,8},{8,16},{16,24},{24,32},{32,40},{40,48},{48,56},{56,64},{64,7... | collective-permute-start | bytes 20 | tf_op jit(solution)/shard_map/ppermute | solution.py:125
  20.2 6.2 %collective-permute-start.2 = (f32[1]{0:T(128)}, f32[1]{0:T(128)}, u32[]{:S(2)}, u32[]{:S(2)}) collective-permute-start(f32[1]{0:T(128)} %select_n.212), channel_id=1, source_target_pairs={{0,16},{8,24},{16,32},{24,40},{32,48},{40,56},{48,64},{56,72},{64,... | collective-permute-start | bytes 20 | tf_op jit(solution)/shard_map/ppermute | solution.py:125
  27.1 4.2 %collective-permute-start.3 = (f32[1]{0:T(128)}, f32[1]{0:T(128)}, u32[]{:S(2)}, u32[]{:S(2)}) collective-permute-start(f32[1]{0:T(128)} %select_n.213), channel_id=1, source_target_pairs={{0,32},{8,40},{16,48},{24,56},{32,64},{40,72},{48,80},{56,88},{64,... | collective-permute-start | bytes 20 | tf_op jit(solution)/shard_map/ppermute | solution.py:125
  31.9 6.2 %collective-permute-start.4 = (f32[1]{0:T(128)}, f32[1]{0:T(128)}, u32[]{:S(2)}, u32[]{:S(2)}) collective-permute-start(f32[1]{0:T(128)} %select_n.214), channel_id=1, source_target_pairs={{0,64},{8,72},{16,80},{24,88},{32,96},{40,104},{48,112},{56,120},{... | collective-permute-start | bytes 20 | tf_op jit(solution)/shard_map/ppermute | solution.py:125
  38.6 8.3 %collective-permute-start.5 = (f32[1]{0:T(128)}, f32[1]{0:T(128)}, u32[]{:S(2)}, u32[]{:S(2)}) collective-permute-start(f32[1]{0:T(128)} %select_n.215), channel_id=1, source_target_pairs={{0,128},{8,136},{16,144},{24,152},{32,160},{40,168},{48,176},{56,1... | collective-permute-start | bytes 20 | tf_op jit(solution)/shard_map/ppermute | solution.py:125
  50.4 9.9 %collective-permute-start.11 = (f32[8,128,128]{2,1,0:T(8,128)S(1)}, f32[8,128,128]{2,1,0:T(8,128)S(1)}, u32[]{:S(2)}, u32[]{:S(2)}) collective-permute-start(f32[8,128,128]{2,1,0:T(8,128)S(1)} %convolution_add_fusion), channel_id=1, source_target_pairs={{0,8},{8,16},{16,24},{24,32},{32,40},{40,48},{48,56},{56,64},{64,7... | collective-permute-start | bytes 1572872 | tf_op jit(solution)/shard_map/ppermute | solution.py:119
  60.3 23.7 %collective-permute-start.12 = (f32[8,128,128]{2,1,0:T(8,128)S(1)}, f32[8,128,128]{2,1,0:T(8,128)S(1)}, u32[]{:S(2)}, u32[]{:S(2)}) collective-permute-start(f32[8,128,128]{2,1,0:T(8,128)S(1)} %broadcast_select_fusion), channel_id=1, source_target_pairs={{0,8},{8,16},{16,24},{24,32},{32,40},{40,48},{48,56},{56,64},{64,7... | collective-permute-start | bytes 1572872 | tf_op jit(solution)/shard_map/ppermute | solution.py:125
  64.1 37.4 %collective-permute-start.17 = (f32[1]{0:T(128)}, f32[1]{0:T(128)}, u32[]{:S(2)}, u32[]{:S(2)}) collective-permute-start(f32[1]{0:T(128)} %bitcast.18), channel_id=1, source_target_pairs={{0,8},{8,16},{16,24},{24,32},{32,40},{40,48},{48,56},{56,64},{64,7... | collective-permute-start | bytes 20 | tf_op jit(solution)/shard_map/ppermute | solution.py:119
  79.4 4.7 %collective-permute-start.6 = (f32[8]{0:T(128)S(1)}, f32[8]{0:T(128)S(1)}, u32[]{:S(2)}, u32[]{:S(2)}) collective-permute-start(f32[8]{0:T(128)S(1)} %get-tuple-element.45), channel_id=1, source_target_pairs={{0,8},{8,16},{16,24},{24,32},{32,40},{40,48},{48,56},{56,64},{64,7... | collective-permute-start | bytes 104 | tf_op jit(solution)/shard_map/ppermute | solution.py:119
  84.2 15.7 %collective-permute-start.13 = (f32[8,128,128]{2,1,0:T(8,128)S(1)}, f32[8,128,128]{2,1,0:T(8,128)S(1)}, u32[]{:S(2)}, u32[]{:S(2)}) collective-permute-start(f32[8,128,128]{2,1,0:T(8,128)S(1)} %add_select_fusion.4), channel_id=1, source_target_pairs={{0,16},{8,24},{16,32},{24,40},{32,48},{40,56},{48,64},{56,72},{64,... | collective-permute-start | bytes 1572872 | tf_op jit(solution)/shard_map/ppermute | solution.py:125
  86.4 6.1 %collective-permute-start.7 = (f32[8]{0:T(128)S(1)}, f32[8]{0:T(128)S(1)}, u32[]{:S(2)}, u32[]{:S(2)}) collective-permute-start(f32[8]{0:T(128)S(1)} %get-tuple-element.36), channel_id=1, source_target_pairs={{0,8},{8,16},{16,24},{24,32},{32,40},{40,48},{48,56},{56,64},{64,7... | collective-permute-start | bytes 104 | tf_op jit(solution)/shard_map/ppermute | solution.py:125
  100.1 53.1 %collective-permute-start.14 = (f32[8,128,128]{2,1,0:T(8,128)S(1)}, f32[8,128,128]{2,1,0:T(8,128)S(1)}, u32[]{:S(2)}, u32[]{:S(2)}) collective-permute-start(f32[8,128,128]{2,1,0:T(8,128)S(1)} %add_select_fusion.3), channel_id=1, source_target_pairs={{0,32},{8,40},{16,48},{24,56},{32,64},{40,72},{48,80},{56,88},{64,... | collective-permute-start | bytes 1572872 | tf_op jit(solution)/shard_map/ppermute | solution.py:125
  102.1 4.6 %collective-permute-start.18 = (f32[1]{0:T(128)}, f32[1]{0:T(128)}, u32[]{:S(2)}, u32[]{:S(2)}) collective-permute-start(f32[1]{0:T(128)} %select_n.245), channel_id=1, source_target_pairs={{0,8},{8,16},{16,24},{24,32},{32,40},{40,48},{48,56},{56,64},{64,7... | collective-permute-start | bytes 20 | tf_op jit(solution)/shard_map/ppermute | solution.py:125
  107.3 10.2 %collective-permute-start.19 = (f32[1]{0:T(128)}, f32[1]{0:T(128)}, u32[]{:S(2)}, u32[]{:S(2)}) collective-permute-start(f32[1]{0:T(128)} %select_n.247), channel_id=1, source_target_pairs={{0,16},{8,24},{16,32},{24,40},{32,48},{40,56},{48,64},{56,72},{64,... | collective-permute-start | bytes 20 | tf_op jit(solution)/shard_map/ppermute | solution.py:125
  118.1 7.2 %collective-permute-start.20 = (f32[1]{0:T(128)}, f32[1]{0:T(128)}, u32[]{:S(2)}, u32[]{:S(2)}) collective-permute-start(f32[1]{0:T(128)} %select_n.249), channel_id=1, source_target_pairs={{0,32},{8,40},{16,48},{24,56},{32,64},{40,72},{48,80},{56,88},{64,... | collective-permute-start | bytes 20 | tf_op jit(solution)/shard_map/ppermute | solution.py:125
  126.0 10.0 %collective-permute-start.21 = (f32[1]{0:T(128)}, f32[1]{0:T(128)}, u32[]{:S(2)}, u32[]{:S(2)}) collective-permute-start(f32[1]{0:T(128)} %select_n.251), channel_id=1, source_target_pairs={{0,64},{8,72},{16,80},{24,88},{32,96},{40,104},{48,112},{56,120},{... | collective-permute-start | bytes 20 | tf_op jit(solution)/shard_map/ppermute | solution.py:125
  136.7 8.1 %collective-permute-start.22 = (f32[1]{0:T(128)}, f32[1]{0:T(128)}, u32[]{:S(2)}, u32[]{:S(2)}) collective-permute-start(f32[1]{0:T(128)} %select_n.253), channel_id=1, source_target_pairs={{0,128},{8,136},{16,144},{24,152},{32,160},{40,168},{48,176},{56,1... | collective-permute-start | bytes 20 | tf_op jit(solution)/shard_map/ppermute | solution.py:125
  145.5 7.7 %collective-permute-start.8 = (f32[8]{0:T(128)S(1)}, f32[8]{0:T(128)S(1)}, u32[]{:S(2)}, u32[]{:S(2)}) collective-permute-start(f32[8]{0:T(128)S(1)} %get-tuple-element.25), channel_id=1, source_target_pairs={{0,16},{8,24},{16,32},{24,40},{32,48},{40,56},{48,64},{56,72},{64,... | collective-permute-start | bytes 104 | tf_op jit(solution)/shard_map/ppermute | solution.py:125
  153.3 24.8 %copy-start.2 = (bf16[256,1024]{0,1:T(8,128)(2,1)S(1)}, bf16[256,1024]{0,1:T(8,128)(2,1)}, u32[]{:S(2)}) copy-start(bf16[256,1024]{0,1:T(8,128)(2,1)} %copy-done.1) | copy-start | bytes 1572868
  153.3 23.4 %collective-permute-start.15 = (f32[8,128,128]{2,1,0:T(8,128)S(1)}, f32[8,128,128]{2,1,0:T(8,128)S(1)}, u32[]{:S(2)}, u32[]{:S(2)}) collective-permute-start(f32[8,128,128]{2,1,0:T(8,128)S(1)} %add_select_fusion.2), channel_id=1, source_target_pairs={{0,64},{8,72},{16,80},{24,88},{32,96},{40,104},{48,112},{56,120},{... | collective-permute-start | bytes 1572872 | tf_op jit(solution)/shard_map/ppermute | solution.py:125
  161.6 5.8 %collective-permute-start.9 = (f32[8]{0:T(128)S(1)}, f32[8]{0:T(128)S(1)}, u32[]{:S(2)}, u32[]{:S(2)}) collective-permute-start(f32[8]{0:T(128)S(1)} %get-tuple-element.23), channel_id=1, source_target_pairs={{0,32},{8,40},{16,48},{24,56},{32,64},{40,72},{48,80},{56,88},{64,... | collective-permute-start | bytes 104 | tf_op jit(solution)/shard_map/ppermute | solution.py:125
  176.9 14.0 %collective-permute-start.16 = (f32[8,128,128]{2,1,0:T(8,128)S(1)}, f32[8,128,128]{2,1,0:T(8,128)}, u32[]{:S(2)}, u32[]{:S(2)}) collective-permute-start(f32[8,128,128]{2,1,0:T(8,128)S(1)} %add_select_fusion.1), channel_id=1, source_target_pairs={{0,128},{8,136},{16,144},{24,152},{32,160},{40,168},{48,176},{56,1... | collective-permute-start | bytes 1572872 | tf_op jit(solution)/shard_map/ppermute | solution.py:125
  180.4 5.5 %collective-permute-start.10 = (f32[8]{0:T(128)S(1)}, f32[8]{0:T(128)S(1)}, u32[]{:S(2)}, u32[]{:S(2)}) collective-permute-start(f32[8]{0:T(128)S(1)} %get-tuple-element.21), channel_id=1, source_target_pairs={{0,64},{8,72},{16,80},{24,88},{32,96},{40,104},{48,112},{56,120},{... | collective-permute-start | bytes 104 | tf_op jit(solution)/shard_map/ppermute | solution.py:125
  190.9 41.2 %copy-start.4 = (f32[1024]{0:T(1024)S(1)}, f32[1024]{0:T(1024)}, u32[]{:S(2)}) copy-start(f32[1024]{0:T(1024)} %param.13) | copy-start | bytes 12292
Sparse Core Ops, SparseCore 0:
  10.6 72.0 all-gather.2
  85.3 86.7 all-gather.4

commit v4 on v2

--- a/solution.py
+++ b/solution.py
@@ -111,24 +111,6 @@
     )(sref, q, keys, values, starts.reshape(rows, 1))
 
 
-def carried_in(part, axis, combine, identity):
-    place = lax.axis_index(axis)
-    size = lax.axis_size(axis)
-    ident = jax.tree.map(lambda a, e: jnp.zeros_like(a) + jnp.asarray(e, a.dtype), part, identity)
-    shifted = jax.tree.map(
-        lambda a: lax.ppermute(a, axis, [(i, i + 1) for i in range(size - 1)]), part
-    )
-    state = jax.tree.map(lambda s, e: jnp.where(place == 0, e, s), shifted, ident)
-    step = 1
-    while step < size:
-        pairs = [(i, i + step) for i in range(size - step)]
-        earlier = jax.tree.map(lambda a: lax.ppermute(a, axis, pairs), state)
-        merged = combine(earlier, state)
-        state = jax.tree.map(lambda m, s: jnp.where(place >= step, m, s), merged, state)
-        step *= 2
-    return state
-
-
 def light_block(carry, inputs, rates):
     state, last_prev = carry
     q_blk, k_blk, v_blk, seg_blk = inputs
@@ -156,14 +138,6 @@
     local = jnp.einsum("shd,she->hde", k_dec, v_blk, preferred_element_type=jnp.float32)
     keep = jnp.where(last == last_prev, 1.0, 0.0) * jnp.exp(-rates * size)
     return ((keep[:, None, None] * state + local, last), out)
-
-
-def combine_states(earlier, later):
-    state_e, dec_e, last_e = earlier
-    state_l, dec_l, last_l = later
-    match = (last_e == last_l) | (last_l < 0.0)
-    factor = jnp.where(match, dec_l, 0.0)
-    return (factor[:, None, None] * state_e + state_l, dec_e * dec_l, jnp.maximum(last_e, last_l))
 
 
 def body(lin_q, lin_k, lin_v, decay_rates, norm_gain, soft_q, soft_k, soft_v, segment_ids):
@@ -185,13 +159,34 @@
         ),
     )
     local_out = outs.reshape(tok, heads, width)
-    summary = (state_loc, jnp.exp(-decay_rates * tok), last_loc.reshape(1))
-    identity = (
-        jnp.zeros((heads, width, width), jnp.float32),
-        jnp.ones((heads,), jnp.float32),
-        jnp.full((1,), -1.0, jnp.float32),
-    )
-    state_in, dec_in, last_in = carried_in(summary, "seq", combine_states, identity)
+    mine = lax.axis_index("seq")
+    parts = lax.axis_size("seq")
+    q0 = (mine * tok).astype(jnp.int32)
+    seg_i = segment_ids.astype(jnp.float32)
+    last_here = seg_i[tok - 1]
+    first_here = (q0 + jnp.sum((seg_i < last_here).astype(jnp.int32))).astype(jnp.float32)
+    rows_per = heads * width // parts
+    chunks = state_loc.reshape(parts, rows_per, width)
+    lane = jnp.arange(width)
+    info = jnp.where(lane == 0, last_here, jnp.where(lane == 1, first_here, 0.0))
+    info = jnp.broadcast_to(info[None, None, :], (parts, 8, width))
+    sent = lax.all_to_all(jnp.concatenate([chunks, info], axis=1), "seq", 0, 0)
+    lasts = sent[:, rows_per, 0]
+    firsts = sent[:, rows_per, 1]
+    idx = jnp.arange(parts)
+    last_prev = jnp.where(idx >= 1, jnp.roll(lasts, 1), -1.0)
+    rate = decay_rates[(mine * rows_per) // width]
+    gap = jnp.maximum(idx[:, None] - 1 - idx[None, :], 0).astype(jnp.float32)
+    linked = (idx[None, :] < idx[:, None]) & (lasts[None, :] == last_prev[:, None])
+    weight = jnp.where(linked, jnp.exp(-rate * tok * gap), 0.0)
+    mixed = jnp.einsum(
+        "pj,jrc->prc", weight, sent[:, :rows_per, :], precision=lax.Precision.HIGHEST
+    )
+    state_in = lax.all_to_all(mixed, "seq", 0, 0).reshape(heads, width, width)
+    last_before = last_prev[mine]
+    same_doc = (idx < mine) & (lasts == last_before)
+    first_before = jnp.min(jnp.where(same_doc, firsts, jnp.float32(tok * parts)))
+    last_in = last_before.reshape(1)
     seg_f = segment_ids.astype(jnp.float32)
     pos = jnp.arange(tok).astype(jnp.float32)
     coef = (
@@ -211,14 +206,12 @@
     )
     shared_heads = soft_k.shape[1] // width
     group = heads // shared_heads
-    mine = lax.axis_index("seq")
     keys = lax.all_gather(soft_k, "seq", axis=0, tiled=True)
     values = lax.all_gather(soft_v, "seq", axis=0, tiled=True)
-    seg_keys = lax.all_gather(segment_ids.astype(jnp.float32), "seq", axis=0, tiled=True)
-    starts = jnp.sum(
-        (seg_keys[None, :] < segment_ids.astype(jnp.float32)[:, None]).astype(jnp.int32), axis=1
-    )
-    q0 = (mine * tok).astype(jnp.int32)
+    below = jnp.sum((seg_i[None, :] < seg_i[:, None]).astype(jnp.int32), axis=1)
+    starts = jnp.where(
+        seg_i == last_before, first_before.astype(jnp.int32), q0 + below
+    )
     pieces = []
     for g in range(shared_heads):
         cols = slice(g * group * width, (g + 1) * group * width)

time: 297 us -> 230 us (0.77)
  the two profiles are of different devices: /device:TPU:193 before, /device:TPU:224 now
where the time goes in v4:
time: 230 us; the launch traced here: 229 us
  waiting for transfers between devices  102 us (44%)
  Pallas kernels  51.3 us (22%)
  between operations  20 us (9%)
  starting transfers between devices  16.8 us (7%)
  blocking collectives  13.4 us (6%)
  other arithmetic  10.9 us (5%)
  local copies, waits for them, and re-layouts  7.9 us (3%)
  matrix products  6.62 us (3%)
    all_gather x1, waiting for transfers between devices, body(): values = lax.all_gather(soft_v, 'seq', axis=0, tiled=True)  71.1 us
    pallas_call x1, Pallas kernels, flash_attention(): pl.pallas_call(kernel, out_shape=jax.ShapeDtypeStruct((rows, total), jnp....  51.3 us
    all_to_all x1, waiting for transfers between devices, body(): sent = lax.all_to_all(jnp.concatenate([chunks, info], axis=1), 'seq', 0, 0)  16.2 us
    all_to_all x1, waiting for transfers between devices, body(): state_in = lax.all_to_all(mixed, 'seq', 0, 0).reshape(heads, width, width)  13.7 us
    psum x1, blocking collectives, body(): total_sq = lax.psum(sums, 'heads')  13.4 us
    all_to_all x1, starting transfers between devices, body(): sent = lax.all_to_all(jnp.concatenate([chunks, info], axis=1), 'seq', 0, 0)  8.53 us
    all_to_all x1, starting transfers between devices, body(): state_in = lax.all_to_all(mixed, 'seq', 0, 0).reshape(heads, width, width)  8.17 us
  transfers between devices with their start and end apart: 4, of which 3 were waited for; matrix products, arithmetic and copies ran while one was open for 11% of the time, Pallas kernels for 0%

profile of v4, /device:TPU:224, one launch (start us, length us, event | category | flops | bytes accessed | tf_op | source)
XLA Modules:
  0.0 229.3 jit_solution(4890218543926153867)
XLA Ops:
  7.2 0.0 copy-start
  7.2 0.0 all-gather.3.cloned.1.call-start
  7.2 0.7 all-gather.3.cloned.1.call-update
  7.9 0.7 convert_element_type.86
  8.6 0.6 slice.36
  9.2 2.0 fusion.46
  11.8 1.2 copy.42
  13.7 0.6 compare_select_fusion.1
  14.4 0.7 multiply_multiply_fusion
  15.0 1.3 compare_convert_fusion.1
  16.4 0.1 exponential_multiply_fusion
  16.4 1.4 convolution_add_fusion
  17.8 0.9 pad_maximum_fusion
  18.7 8.5 %all-to-all-start = ((f32[32,40,128]{2,1,0:T(8,128)}), f32[32,40,128]{2,1,0:T(8,128)S(1)}, u32[]{:S(2)}, u32[]{:S(2)}) async-start(f32[32,40,128]{2,1,0:T(8,128)} %pad_maximum_fusion), calls=%async_computation | async-start | bytes 1310720 | tf_op jit(solution)/shard_map/all_to_all | solution.py:173
  27.3 0.0 all-gather.5.cloned.1.call-start
  27.3 0.7 all-gather.5.cloned.1.call-update
  28.0 0.0 copy-done.3
  28.0 0.6 dynamic_slice.17
  29.3 0.2 convert_reduce_fusion
  29.5 0.1 fusion.26
  29.7 0.1 subtract_maximum_fusion
  29.8 16.2 %all-to-all-done = f32[32,40,128]{2,1,0:T(8,128)S(1)} async-done(((f32[32,40,128]{2,1,0:T(8,128)}), f32[32,40,128]{2,1,0:T(8,128)S(1)}, u32[]{:S(2)}, u32[]{:S(2)}) %all-to-all-start) | async-done | bytes 655392 | tf_op jit(solution)/shard_map/all_to_all | solution.py:173
  45.9 0.5 slice.46
  46.5 0.3 slice_reduce_fusion.2
  46.8 0.7 compare_select_fusion.2
  47.5 0.6 dynamic_slice.16
  48.1 0.6 slice_reduce_fusion
  48.7 1.2 fusion.49
  50.5 0.6 add_select_fusion
  51.2 0.6 fusion.55
  54.8 0.1 slice.49
  54.9 0.9 fusion.16
  55.8 0.0 copy-start.4
  55.8 1.1 copy.35
  56.9 8.2 %all-to-all-start.1 = ((f32[32,32,128]{2,1,0:T(8,128)}), f32[32,32,128]{2,1,0:T(8,128)S(1)}, u32[]{:S(2)}, u32[]{:S(2)}) async-start(f32[32,32,128]{2,1,0:T(8,128)} %copy.35), calls=%async_computation.1 | async-start | bytes 1048576 | tf_op jit(solution)/shard_map/all_to_all | solution.py:185
  65.1 0.8 copy.39.refs_4_
  65.9 0.6 stack.23.refs_0_
  66.5 0.6 fusion.54
  67.1 0.1 fusion.43
  67.2 0.6 fusion.5
  67.8 1.8 fusion.2
  69.7 13.7 %all-to-all-done.1 = f32[32,32,128]{2,1,0:T(8,128)S(1)} async-done(((f32[32,32,128]{2,1,0:T(8,128)}), f32[32,32,128]{2,1,0:T(8,128)S(1)}, u32[]{:S(2)}, u32[]{:S(2)}) %all-to-all-start.1) | async-done | bytes 524320 | tf_op jit(solution)/shard_map/all_to_all | solution.py:185
  83.3 2.0 multiply_reduce_fusion
  85.3 0.3 copy.38
  85.6 13.4 %psum.7 = f32[256]{0:T(256)S(1)} all-reduce(f32[256]{0:T(256)S(1)} %get-tuple-element.39), channel_id=1, replica_groups=mesh['seq'=32,'heads'=8] {'heads'}, use_global_device_ids=true, to_apply=%region_2.3 | all-reduce | flops 256 | bytes 2048 | tf_op jit(solution)/shard_map/psum | solution.py:202
  99.0 1.0 multiply_convert_fusion
  99.9 71.1 %all-gather.5.cloned.1.call-done.refs_3_ = bf16[8192,128]{1,0:T(8,128)(2,1)} async-done(((bf16[256,128]{1,0:T(8,128)(2,1)}), bf16[8192,128]{1,0:T(8,128)(2,1)}) %all-gather.5.cloned.1.call-update) | async-done | bytes 2097168 | tf_op jit(solution)/shard_map/all_gather | solution.py:210
  171.1 51.3 %shard_map.104 = bf16[256,1024]{1,0:T(8,128)(2,1)} custom-call(s32[5]{0:T(128)} %stack.23.refs_0_, bf16[256,1024]{1,0:T(8,128)(2,1)} %refs_1_.1, bf16[8192,128]{1,0:T(8,128)(2,1)} %all-gather.3.cloned.1.call-done.refs_2_, bf16[8192,128]{1,0:T(8,128)(2,1)} %all-gather.5.cloned.1.call-done.refs_3_, s32[256,1]{1,0:T(8,128)} %copy.39.refs_4_), custom_call_target="tpu_custom_call" | custom-call | flops 4294967296 | bytes 5242880 | tf_op jit(solution)/shard_map/pallas_call | solution.py:86
  (14 shorter events, 0.1 us)
Async XLA Ops:
  7.2 60.1 %copy-start = (bf16[256,1024]{1,0:T(8,128)(2,1)S(1)}, bf16[256,1024]{1,0:T(8,128)(2,1)}, u32[]{:S(2)}) copy-start(bf16[256,1024]{1,0:T(8,128)(2,1)} %param.9) | copy-start | bytes 1572868
  7.2 92.8 %all-gather.3.cloned.1.call-start = ((), (), s32[]{:S(2)}) async-start(), calls=%async_computation.2 | async-start | bytes 2162688 | tf_op jit(solution)/shard_map/all_gather | solution.py:209
  16.4 11.6 %copy-start.3 = (f32[8]{0:T(128)S(1)}, f32[8]{0:T(128)}, u32[]{:S(2)}) copy-start(f32[8]{0:T(128)} %param.12) | copy-start | bytes 100
  16.4 34.1 %copy-start.1 = (s32[256]{0:T(256)S(1)}, s32[256]{0:T(256)}, u32[]{:S(2)}) copy-start(s32[256]{0:T(256)} %param.17) | copy-start | bytes 3076
  18.7 27.2 %all-to-all-start = ((f32[32,40,128]{2,1,0:T(8,128)}), f32[32,40,128]{2,1,0:T(8,128)S(1)}, u32[]{:S(2)}, u32[]{:S(2)}) async-start(f32[32,40,128]{2,1,0:T(8,128)} %pad_maximum_fusion), calls=%async_computation | async-start | bytes 1310720 | tf_op jit(solution)/shard_map/all_to_all | solution.py:173
  27.3 143.8 %all-gather.5.cloned.1.call-start = ((), (), s32[]{:S(2)}) async-start(), calls=%async_computation.3 | async-start | bytes 2162688 | tf_op jit(solution)/shard_map/all_gather | solution.py:210
  55.8 12.0 %copy-start.4 = (bf16[256,1024]{1,0:T(8,128)(2,1)S(1)}, bf16[256,1024]{1,0:T(8,128)(2,1)}, u32[]{:S(2)}) copy-start(bf16[256,1024]{1,0:T(8,128)(2,1)} %param.11) | copy-start | bytes 1572868
  56.9 26.4 %all-to-all-start.1 = ((f32[32,32,128]{2,1,0:T(8,128)}), f32[32,32,128]{2,1,0:T(8,128)S(1)}, u32[]{:S(2)}, u32[]{:S(2)}) async-start(f32[32,32,128]{2,1,0:T(8,128)} %copy.35), calls=%async_computation.1 | async-start | bytes 1048576 | tf_op jit(solution)/shard_map/all_to_all | solution.py:185
  83.3 15.7 %copy-start.2 = (f32[1024]{0:T(1024)S(1)}, f32[1024]{0:T(1024)}, u32[]{:S(2)}) copy-start(f32[1024]{0:T(1024)} %param.13) | copy-start | bytes 12292
Sparse Core Ops, SparseCore 0:
  10.6 81.9 all-gather.2
  95.2 75.8 all-gather.4

commit v5 on v4

--- a/solution.py
+++ b/solution.py
@@ -8,7 +8,7 @@
 from jax.sharding import PartitionSpec as P
 
 BLOCK = 256
-KEY_BLOCK = 512
+KEY_BLOCK = 256
 
 
 def flash_body(sref, q_ref, k_ref, v_ref, st_ref, o_ref, m_ref, l_ref, acc_ref, *, heads, width, scale):
@@ -111,6 +111,75 @@
     )(sref, q, keys, values, starts.reshape(rows, 1))
 
 
+def gather_body(k_ref, v_ref, ko_ref, vo_ref, send_sem, recv_sem, own_sem, *, parts, rows):
+    me = lax.axis_index("seq")
+    col = lax.axis_index("heads")
+    mine = pl.ds(pl.multiple_of(me * rows, rows), rows)
+    own = [
+        pltpu.make_async_copy(k_ref, ko_ref.at[mine], own_sem.at[0]),
+        pltpu.make_async_copy(v_ref, vo_ref.at[mine], own_sem.at[1]),
+    ]
+    for c in own:
+        c.start()
+
+    def remote(step, src, dst, which):
+        return pltpu.make_async_remote_copy(
+            src_ref=src,
+            dst_ref=dst.at[mine],
+            send_sem=send_sem.at[step, which],
+            recv_sem=recv_sem.at[me, which],
+            device_id=(me + step, col),
+            device_id_type=pl.DeviceIdType.MESH,
+        )
+
+    for step in range(1, parts):
+        @pl.when(me + step < parts)
+        def _():
+            remote(step, k_ref, ko_ref, 0).start()
+            remote(step, v_ref, vo_ref, 1).start()
+
+    for src_slot in range(parts - 1):
+        @pl.when(src_slot < me)
+        def _():
+            slot = pl.ds(src_slot * rows, rows)
+            for which, (src, dst) in enumerate(((k_ref, ko_ref), (v_ref, vo_ref))):
+                pltpu.make_async_remote_copy(
+                    src_ref=src,
+                    dst_ref=dst.at[slot],
+                    send_sem=send_sem.at[0, which],
+                    recv_sem=recv_sem.at[src_slot, which],
+                    device_id=(me, col),
+                    device_id_type=pl.DeviceIdType.MESH,
+                ).wait_recv()
+
+    for step in range(1, parts):
+        @pl.when(me + step < parts)
+        def _():
+            remote(step, k_ref, ko_ref, 0).wait_send()
+            remote(step, v_ref, vo_ref, 1).wait_send()
+
+    for c in own:
+        c.wait()
+
+
+def gather_earlier(keys, values, parts):
+    rows, width = keys.shape
+    body = lambda *refs: gather_body(*refs, parts=parts, rows=rows)
+    full = jax.ShapeDtypeStruct((parts * rows, width), keys.dtype)
+    return pl.pallas_call(
+        body,
+        out_shape=(full, full),
+        in_specs=[pl.BlockSpec(memory_space=pl.ANY)] * 2,
+        out_specs=(pl.BlockSpec(memory_space=pl.ANY), pl.BlockSpec(memory_space=pl.ANY)),
+        scratch_shapes=[
+            pltpu.SemaphoreType.DMA((parts, 2)),
+            pltpu.SemaphoreType.DMA((parts, 2)),
+            pltpu.SemaphoreType.DMA((2,)),
+        ],
+        compiler_params=pltpu.CompilerParams(has_side_effects=True),
+    )(keys, values)
+
+
 def light_block(carry, inputs, rates):
     state, last_prev = carry
     q_blk, k_blk, v_blk, seg_blk = inputs
@@ -206,8 +275,7 @@
     )
     shared_heads = soft_k.shape[1] // width
     group = heads // shared_heads
-    keys = lax.all_gather(soft_k, "seq", axis=0, tiled=True)
-    values = lax.all_gather(soft_v, "seq", axis=0, tiled=True)
+    keys, values = gather_earlier(soft_k, soft_v, parts)
     below = jnp.sum((seg_i[None, :] < seg_i[:, None]).astype(jnp.int32), axis=1)
     starts = jnp.where(
         seg_i == last_before, first_before.astype(jnp.int32), q0 + below

time: 230 us -> 262 us (1.14)
  the two profiles are of different devices: /device:TPU:224 before, /device:TPU:230 now
where the time goes in v5:
time: 262 us; the launch traced here: 261 us
  Pallas kernels  200 us (76%)
  starting transfers between devices  15.9 us (6%)
  blocking collectives  13.9 us (5%)
  other arithmetic  11 us (4%)
  local copies, waits for them, and re-layouts  7.95 us (3%)
  between operations  6.55 us (2%)
  matrix products  5.57 us (2%)
    pallas_call x1, Pallas kernels, gather_earlier(): pl.pallas_call(body, out_shape=(full, full), in_specs=[pl.BlockSpec(memor...  113 us
    pallas_call x1, Pallas kernels, flash_attention(): pl.pallas_call(kernel, out_shape=jax.ShapeDtypeStruct((rows, total), jnp....  87.7 us
    psum x1, blocking collectives, body(): total_sq = lax.psum(sums, 'heads')  13.9 us
    all_to_all x1, starting transfers between devices, body(): sent = lax.all_to_all(jnp.concatenate([chunks, info], axis=1), 'seq', 0, 0)  8.46 us
    all_to_all x1, starting transfers between devices, body(): state_in = lax.all_to_all(mixed, 'seq', 0, 0).reshape(heads, width, width)  7.46 us
  transfers between devices with their start and end apart: 2, of which 0 were waited for; matrix products, arithmetic and copies ran while one was open for 2% of the time, Pallas kernels for 77%

profile of v5, /device:TPU:230, one launch (start us, length us, event | category | flops | bytes accessed | tf_op | source)
XLA Modules:
  0.0 261.4 jit_solution(1672135203343458992)
XLA Ops:
  0.6 0.0 copy-start
  0.6 0.7 convert_element_type.86
  1.4 0.6 slice.36
  2.0 2.0 fusion.46
  3.9 1.3 compare_convert_fusion.1
  6.6 0.6 compare_select_fusion.1
  7.2 1.2 copy.42
  8.5 0.0 copy-start.1
  8.5 0.7 multiply_multiply_fusion
  9.2 0.1 exponential_multiply_fusion
  9.3 1.4 convolution_add_fusion
  10.7 0.9 pad_maximum_fusion
  11.6 0.0 copy-done.1
  11.6 8.5 %all-to-all-start = ((f32[32,40,128]{2,1,0:T(8,128)}), f32[32,40,128]{2,1,0:T(8,128)S(1)}, u32[]{:S(2)}, u32[]{:S(2)}) async-start(f32[32,40,128]{2,1,0:T(8,128)} %pad_maximum_fusion), calls=%async_computation | async-start | bytes 1310720 | tf_op jit(solution)/shard_map/all_to_all | solution.py:242
  20.1 0.0 copy-done.4
  20.1 0.6 dynamic_slice.17
  21.3 112.7 %shard_map.104 = (bf16[8192,128]{1,0:T(8,128)(2,1)}, bf16[8192,128]{1,0:T(8,128)(2,1)}) custom-call(bf16[256,128]{1,0:T(8,128)(2,1)} %refs_0_.1, bf16[256,128]{1,0:T(8,128)(2,1)} %refs_1_.2), custom_call_target="tpu_custom_call" | custom-call | tf_op jit(solution)/shard_map/pallas_call | solution.py:169
  134.1 0.2 convert_reduce_fusion
  134.3 0.1 fusion.26
  134.4 0.1 subtract_maximum_fusion
  134.5 0.0 all-to-all-done
  134.5 0.5 slice.46
  135.1 0.3 slice_reduce_fusion.2
  135.4 0.7 compare_select_fusion.2
  136.1 0.6 dynamic_slice.16
  136.7 0.0 copy-done.2
  136.7 0.6 fusion.54
  137.3 0.6 slice_reduce_fusion
  137.9 1.2 fusion.49
  139.8 0.1 slice.49
  139.8 0.9 fusion.16
  140.7 1.1 copy.35
  141.8 7.5 %all-to-all-start.1 = ((f32[32,32,128]{2,1,0:T(8,128)}), f32[32,32,128]{2,1,0:T(8,128)S(1)}, u32[]{:S(2)}, u32[]{:S(2)}) async-start(f32[32,32,128]{2,1,0:T(8,128)} %copy.35), calls=%async_computation.1 | async-start | bytes 1048576 | tf_op jit(solution)/shard_map/all_to_all | solution.py:254
  149.3 0.6 add_select_fusion
  149.9 0.1 fusion.43
  150.0 0.6 fusion.55
  153.7 0.8 copy.39.refs_4_
  154.4 0.6 stack.23.refs_0_
  155.1 0.0 copy-done
  155.1 0.6 fusion.5
  155.7 2.0 fusion.2
  157.7 87.7 %shard_map.105 = bf16[256,1024]{1,0:T(8,128)(2,1)} custom-call(s32[5]{0:T(128)} %stack.23.refs_0_, bf16[256,1024]{1,0:T(8,128)(2,1)} %refs_1_.3, bf16[8192,128]{1,0:T(8,128)(2,1)} %get-tuple-element.22.refs_2_, bf16[8192,128]{1,0:T(8,128)(2,1)} %get-tuple-element.23.refs_3_, s32[256,1]{1,0:T(8,128)} %copy.39.refs_4_), custom_call_target="tpu_custom_call" | custom-call | flops 4294967296 | bytes 5242880 | tf_op jit(solution)/shard_map/pallas_call | solution.py:86
  245.4 0.0 all-to-all-done.1
  245.4 0.7 multiply_reduce_fusion
  246.2 13.9 %psum.7 = f32[256]{0:T(256)S(1)} all-reduce(f32[256]{0:T(256)S(1)} %get-tuple-element.43), channel_id=1, replica_groups=mesh['seq'=32,'heads'=8] {'heads'}, use_global_device_ids=true, to_apply=%region_2.3 | all-reduce | flops 256 | bytes 2048 | tf_op jit(solution)/shard_map/psum | solution.py:271
  260.1 0.3 copy.38
  260.4 0.0 copy-done.3
  260.4 0.9 multiply_convert_fusion
  (9 shorter events, 0.0 us)
Async XLA Ops:
  0.6 154.4 %copy-start = (bf16[256,1024]{1,0:T(8,128)(2,1)S(1)}, bf16[256,1024]{1,0:T(8,128)(2,1)}, u32[]{:S(2)}) copy-start(bf16[256,1024]{1,0:T(8,128)(2,1)} %param.9) | copy-start | bytes 1572868
  8.5 3.1 %copy-start.1 = (bf16[256,1024]{0,1:T(8,128)(2,1)}, bf16[256,1024]{0,1:T(8,128)(2,1)S(1)}, u32[]{:S(2)}) copy-start(bf16[256,1024]{0,1:T(8,128)(2,1)S(1)} %copy.42) | copy-start | bytes 1572868
  9.3 10.8 %copy-start.4 = (f32[8]{0:T(128)S(1)}, f32[8]{0:T(128)}, u32[]{:S(2)}) copy-start(f32[8]{0:T(128)} %param.12) | copy-start | bytes 100
  9.3 127.4 %copy-start.2 = (s32[256]{0:T(256)S(1)}, s32[256]{0:T(256)}, u32[]{:S(2)}) copy-start(s32[256]{0:T(256)} %param.17) | copy-start | bytes 3076
  11.6 122.9 %all-to-all-start = ((f32[32,40,128]{2,1,0:T(8,128)}), f32[32,40,128]{2,1,0:T(8,128)S(1)}, u32[]{:S(2)}, u32[]{:S(2)}) async-start(f32[32,40,128]{2,1,0:T(8,128)} %pad_maximum_fusion), calls=%async_computation | async-start | bytes 1310720 | tf_op jit(solution)/shard_map/all_to_all | solution.py:242
  141.8 103.6 %all-to-all-start.1 = ((f32[32,32,128]{2,1,0:T(8,128)}), f32[32,32,128]{2,1,0:T(8,128)S(1)}, u32[]{:S(2)}, u32[]{:S(2)}) async-start(f32[32,32,128]{2,1,0:T(8,128)} %copy.35), calls=%async_computation.1 | async-start | bytes 1048576 | tf_op jit(solution)/shard_map/all_to_all | solution.py:254
  245.4 15.0 %copy-start.3 = (f32[1024]{0:T(1024)S(1)}, f32[1024]{0:T(1024)}, u32[]{:S(2)}) copy-start(f32[1024]{0:T(1024)} %param.13) | copy-start | bytes 12292

commit v6 on v4

--- a/solution.py
+++ b/solution.py
@@ -206,8 +206,17 @@
     )
     shared_heads = soft_k.shape[1] // width
     group = heads // shared_heads
-    keys = lax.all_gather(soft_k, "seq", axis=0, tiled=True)
-    values = lax.all_gather(soft_v, "seq", axis=0, tiled=True)
+    window = jnp.concatenate([soft_k, soft_v], axis=1)
+    reach = 1
+    while reach < parts:
+        pairs = [(i, i + reach) for i in range(parts - reach)]
+        window = jnp.concatenate([lax.ppermute(window, "seq", pairs), window], axis=0)
+        reach *= 2
+    padded = jnp.concatenate([window, jnp.zeros_like(window[: (parts - 1) * tok])], axis=0)
+    ordered = lax.dynamic_slice_in_dim(padded, (parts - 1 - mine) * tok, parts * tok, axis=0)
+    kv_cols = soft_k.shape[1]
+    keys = ordered[:, :kv_cols]
+    values = ordered[:, kv_cols:]
     below = jnp.sum((seg_i[None, :] < seg_i[:, None]).astype(jnp.int32), axis=1)
     starts = jnp.where(
         seg_i == last_before, first_before.astype(jnp.int32), q0 + below

time: 230 us -> 343 us (1.49)
  the two profiles are of different devices: /device:TPU:224 before, /device:TPU:166 now
where the time goes in v6:
time: 343 us; the launch traced here: 339 us
  waiting for transfers between devices  125 us (36%)
  starting transfers between devices  102 us (30%)
  Pallas kernels  47.7 us (14%)
  local copies, waits for them, and re-layouts  20.6 us (6%)
  blocking collectives  13.5 us (4%)
  other arithmetic  13 us (4%)
  matrix products  9.99 us (3%)
  between operations  7.07 us (2%)
    ppermute x5, waiting for transfers between devices, body(): lax.ppermute(window, 'seq', pairs)  85.3 us
    all_to_all x1, starting transfers between devices, body(): state_in = lax.all_to_all(mixed, 'seq', 0, 0).reshape(heads, width, width)  79 us
    pallas_call x1, Pallas kernels, flash_attention(): pl.pallas_call(kernel, out_shape=jax.ShapeDtypeStruct((rows, total), jnp....  47.7 us
    all_to_all x1, waiting for transfers between devices, body(): state_in = lax.all_to_all(mixed, 'seq', 0, 0).reshape(heads, width, width)  39.9 us
    psum x1, blocking collectives, body(): total_sq = lax.psum(sums, 'heads')  13.5 us
    ppermute x5, starting transfers between devices, body(): lax.ppermute(window, 'seq', pairs)  13.5 us
    all_to_all x1, starting transfers between devices, body(): sent = lax.all_to_all(jnp.concatenate([chunks, info], axis=1), 'seq', 0, 0)  9.19 us
    unnamed x33, local copies, waits for them, and re-layouts  7.44 us
  transfers between devices with their start and end apart: 7, of which 3 were waited for; matrix products, arithmetic and copies ran while one was open for 9% of the time, Pallas kernels for 0%

profile of v6, /device:TPU:166, one launch (start us, length us, event | category | flops | bytes accessed | tf_op | source)
XLA Modules:
  0.0 338.9 jit_solution(9083544712307068475)
XLA Ops:
  0.7 0.9 constant_dynamic-update-slice_fusion.1
  1.6 0.9 constant_dynamic-update-slice_fusion
  2.4 2.8 collective-permute-start
  5.3 0.7 convert_element_type.86
  6.6 1.2 copy.42
  7.8 1.4 compare_convert_fusion.1
  9.8 0.7 multiply_multiply_fusion
  10.6 1.3 convolution_add_fusion
  12.0 4.3 %collective-permute-start.1 = (bf16[512,256]{1,0:T(8,128)(2,1)S(1)}, bf16[512,256]{1,0:T(8,128)(2,1)S(1)}, u32[]{:S(2)}, u32[]{:S(2)}) collective-permute-start(bf16[512,256]{1,0:T(8,128)(2,1)S(1)} %pad_maximum_fusion.3), channel_id=1, source_target_pairs={{0,16},{8,24},{16,32},{24,40},{32,48},{40,56},{48,64},{56,72},{64,... | collective-permute-start | bytes 786440 | tf_op jit(solution)/shard_map/ppermute | solution.py:213
  16.3 1.3 fusion.46
  18.3 0.7 compare_select_fusion.1
  19.0 0.9 pad_maximum_fusion.1
  19.9 9.2 %all-to-all-start = ((f32[32,40,128]{2,1,0:T(8,128)}), f32[32,40,128]{2,1,0:T(8,128)S(1)}, u32[]{:S(2)}, u32[]{:S(2)}) async-start(f32[32,40,128]{2,1,0:T(8,128)} %pad_maximum_fusion.1), calls=%async_computation | async-start | bytes 1310720 | tf_op jit(solution)/shard_map/all_to_all | solution.py:173
  29.2 2.5 collective-permute-start.2
  31.7 0.8 fusion.26
  32.5 23.0 %collective-permute-done.2 = bf16[1024,256]{1,0:T(8,128)(2,1)S(1)} collective-permute-done((bf16[1024,256]{1,0:T(8,128)(2,1)S(1)}, bf16[1024,256]{1,0:T(8,128)(2,1)S(1)}, u32[]{:S(2)}, u32[]{:S(2)}) %collective-permute-start.2) | collective-permute-done | bytes 524320 | tf_op jit(solution)/shard_map/ppermute | solution.py:213
  55.5 1.0 pad_maximum_fusion
  56.5 2.5 collective-permute-start.3
  60.5 0.8 subtract_maximum_fusion
  62.2 0.7 compare_select_fusion.2
  62.9 0.7 dynamic_slice.19
  64.1 1.3 fusion.49
  66.0 0.7 add_select_fusion
  66.7 62.3 %collective-permute-done.3 = bf16[2048,256]{1,0:T(8,128)(2,1)S(1)} collective-permute-done((bf16[2048,256]{1,0:T(8,128)(2,1)}, bf16[2048,256]{1,0:T(8,128)(2,1)S(1)}, u32[]{:S(2)}, u32[]{:S(2)}) %collective-permute-start.3) | collective-permute-done | bytes 1048608 | tf_op jit(solution)/shard_map/ppermute | solution.py:213
  129.0 1.1 constant_dynamic-update-slice_fusion.6
  130.1 0.8 constant_dynamic-update-slice_fusion.5
  130.9 0.7 constant_dynamic-update-slice_fusion.4
  131.7 0.7 constant_dynamic-update-slice_fusion.3
  132.3 0.6 constant_dynamic-update-slice_fusion.2
  133.0 0.6 constant_dynamic-update-slice_fusion.13
  133.6 1.3 collective-permute-start.4
  139.0 0.9 fusion.16
  139.9 1.1 copy.35
  141.0 79.0 %all-to-all-start.1 = ((f32[32,32,128]{2,1,0:T(8,128)}), f32[32,32,128]{2,1,0:T(8,128)S(1)}, u32[]{:S(2)}, u32[]{:S(2)}) async-start(f32[32,32,128]{2,1,0:T(8,128)} %copy.35), calls=%async_computation.1 | async-start | bytes 1048576 | tf_op jit(solution)/shard_map/all_to_all | solution.py:185
  220.1 0.8 copy.39.refs_4_
  220.9 0.6 stack.23.refs_0_
  221.5 0.7 fusion.54
  222.3 1.6 fusion.5
  223.8 3.3 fusion.2
  227.1 39.9 %all-to-all-done.1 = f32[32,32,128]{2,1,0:T(8,128)S(1)} async-done(((f32[32,32,128]{2,1,0:T(8,128)}), f32[32,32,128]{2,1,0:T(8,128)S(1)}, u32[]{:S(2)}, u32[]{:S(2)}) %all-to-all-start.1) | async-done | bytes 524320 | tf_op jit(solution)/shard_map/all_to_all | solution.py:185
  267.0 2.9 multiply_reduce_fusion
  269.9 1.6 copy.38
  271.5 13.5 %psum.7 = f32[256]{0:T(256)S(1)} all-reduce(f32[256]{0:T(256)S(1)} %get-tuple-element.41), channel_id=1, replica_groups=mesh['seq'=32,'heads'=8] {'heads'}, use_global_device_ids=true, to_apply=%region_2.3 | all-reduce | flops 256 | bytes 2048 | tf_op jit(solution)/shard_map/psum | solution.py:202
  285.0 1.0 multiply_convert_fusion
  286.0 1.7 constant_dynamic-update-slice_fusion.12
  287.9 0.7 copy-done.2
  288.9 2.2 fusion.55
  291.1 47.7 %shard_map.104 = bf16[256,1024]{1,0:T(8,128)(2,1)} custom-call(s32[5]{0:T(128)} %stack.23.refs_0_, bf16[256,1024]{1,0:T(8,128)(2,1)} %refs_1_.1, bf16[8192,128]{1,0:T(8,128)(2,1)} %get-tuple-element.23.refs_2_, bf16[8192,128]{1,0:T(8,128)(2,1)} %get-tuple-element.22.refs_3_, s32[256,1]{1,0:T(8,128)} %copy.39.refs_4_), custom_call_target="tpu_custom_call" | custom-call | flops 4294967296 | bytes 5242880 | tf_op jit(solution)/shard_map/pallas_call | solution.py:86
  (48 shorter events, 4.1 us)
Async XLA Ops:
  0.6 221.6 %copy-start = (bf16[256,1024]{1,0:T(8,128)(2,1)S(1)}, bf16[256,1024]{1,0:T(8,128)(2,1)}, u32[]{:S(2)}) copy-start(bf16[256,1024]{1,0:T(8,128)(2,1)} %param.9) | copy-start | bytes 1572868
  0.6 15.7 %copy-start.7 = (s32[256]{0:T(256)S(1)}, s32[256]{0:T(256)}, u32[]{:S(2)}) copy-start(s32[256]{0:T(256)} %param.17) | copy-start | bytes 3076
  2.4 9.5 %collective-permute-start = (bf16[256,256]{1,0:T(8,128)(2,1)S(1)}, bf16[256,256]{1,0:T(8,128)(2,1)S(1)}, u32[]{:S(2)}, u32[]{:S(2)}) collective-permute-start(bf16[256,256]{1,0:T(8,128)(2,1)S(1)} %constant_dynamic-update-slice_fusion), channel_id=1, source_target_pairs={{0,8},{8,16},{16,24},{24,32},{32,40},{40,48},{48,56},{56,64},{64,7... | collective-permute-start | bytes 393224 | tf_op jit(solution)/shard_map/ppermute | solution.py:213
  7.8 4.1 %copy-start.5 = (bf16[256,1024]{0,1:T(8,128)(2,1)}, bf16[256,1024]{0,1:T(8,128)(2,1)S(1)}, u32[]{:S(2)}) copy-start(bf16[256,1024]{0,1:T(8,128)(2,1)S(1)} %copy.42) | copy-start | bytes 1572868
  12.0 17.1 %collective-permute-start.1 = (bf16[512,256]{1,0:T(8,128)(2,1)S(1)}, bf16[512,256]{1,0:T(8,128)(2,1)S(1)}, u32[]{:S(2)}, u32[]{:S(2)}) collective-permute-start(bf16[512,256]{1,0:T(8,128)(2,1)S(1)} %pad_maximum_fusion.3), channel_id=1, source_target_pairs={{0,16},{8,24},{16,32},{24,40},{32,48},{40,56},{48,64},{56,72},{64,... | collective-permute-start | bytes 786440 | tf_op jit(solution)/shard_map/ppermute | solution.py:213
  19.9 39.2 %copy-start.9 = (f32[8]{0:T(128)S(1)}, f32[8]{0:T(128)}, u32[]{:S(2)}) copy-start(f32[8]{0:T(128)} %param.12) | copy-start | bytes 100
  19.9 41.4 %all-to-all-start = ((f32[32,40,128]{2,1,0:T(8,128)}), f32[32,40,128]{2,1,0:T(8,128)S(1)}, u32[]{:S(2)}, u32[]{:S(2)}) async-start(f32[32,40,128]{2,1,0:T(8,128)} %pad_maximum_fusion.1), calls=%async_computation | async-start | bytes 1310720 | tf_op jit(solution)/shard_map/all_to_all | solution.py:173
  29.2 26.3 %collective-permute-start.2 = (bf16[1024,256]{1,0:T(8,128)(2,1)S(1)}, bf16[1024,256]{1,0:T(8,128)(2,1)S(1)}, u32[]{:S(2)}, u32[]{:S(2)}) collective-permute-start(bf16[1024,256]{1,0:T(8,128)(2,1)S(1)} %pad_maximum_fusion.2), channel_id=1, source_target_pairs={{0,32},{8,40},{16,48},{24,56},{32,64},{40,72},{48,80},{56,88},{64,... | collective-permute-start | bytes 1572872 | tf_op jit(solution)/shard_map/ppermute | solution.py:213
  56.5 72.5 %collective-permute-start.3 = (bf16[2048,256]{1,0:T(8,128)(2,1)}, bf16[2048,256]{1,0:T(8,128)(2,1)S(1)}, u32[]{:S(2)}, u32[]{:S(2)}) collective-permute-start(bf16[2048,256]{1,0:T(8,128)(2,1)} %pad_maximum_fusion), channel_id=1, source_target_pairs={{0,64},{8,72},{16,80},{24,88},{32,96},{40,104},{48,112},{56,120},{... | collective-permute-start | bytes 3145736 | tf_op jit(solution)/shard_map/ppermute | solution.py:213
  60.5 71.8 %copy-start.1 = (bf16[256,128]{1,0:T(8,128)(2,1)S(1)}, bf16[256,128]{1,0:T(8,128)(2,1)}, u32[]{:S(2)}) copy-start(bf16[256,128]{1,0:T(8,128)(2,1)} %param.15) | copy-start | bytes 196612
  61.3 71.6 %copy-start.3 = (bf16[256,128]{1,0:T(8,128)(2,1)S(1)}, bf16[256,128]{1,0:T(8,128)(2,1)}, u32[]{:S(2)}) copy-start(bf16[256,128]{1,0:T(8,128)(2,1)} %param.16) | copy-start | bytes 196612
  133.6 152.4 %collective-permute-start.4 = (bf16[4096,256]{1,0:T(8,128)(2,1)}, bf16[4096,256]{1,0:T(8,128)(2,1)}, u32[]{:S(2)}, u32[]{:S(2)}) collective-permute-start(bf16[4096,256]{1,0:T(8,128)(2,1)} %constant_dynamic-update-slice_fusion.13), channel_id=1, source_target_pairs={{0,128},{8,136},{16,144},{24,152},{32,160},{40,168},{48,176},{56,1... | collective-permute-start | bytes 6291464 | tf_op jit(solution)/shard_map/ppermute | solution.py:213
  139.9 84.0 %copy-start.6 = (bf16[256,1024]{0,1:T(8,128)(2,1)S(1)}, bf16[256,1024]{0,1:T(8,128)(2,1)}, u32[]{:S(2)}) copy-start(bf16[256,1024]{0,1:T(8,128)(2,1)} %copy-done.5) | copy-start | bytes 1572868
  141.0 126.1 %all-to-all-start.1 = ((f32[32,32,128]{2,1,0:T(8,128)}), f32[32,32,128]{2,1,0:T(8,128)S(1)}, u32[]{:S(2)}, u32[]{:S(2)}) async-start(f32[32,32,128]{2,1,0:T(8,128)} %copy.35), calls=%async_computation.1 | async-start | bytes 1048576 | tf_op jit(solution)/shard_map/all_to_all | solution.py:185
  267.0 18.0 %copy-start.8 = (f32[1024]{0:T(1024)S(1)}, f32[1024]{0:T(1024)}, u32[]{:S(2)}) copy-start(f32[1024]{0:T(1024)} %param.13) | copy-start | bytes 12292
  287.7 0.8 copy-start.2
  287.7 0.9 copy-start.4

commit v7 on v4

--- a/solution.py
+++ b/solution.py
@@ -206,8 +206,10 @@
     )
     shared_heads = soft_k.shape[1] // width
     group = heads // shared_heads
-    keys = lax.all_gather(soft_k, "seq", axis=0, tiled=True)
-    values = lax.all_gather(soft_v, "seq", axis=0, tiled=True)
+    both = lax.all_gather(jnp.concatenate([soft_k, soft_v], axis=1), "seq", axis=0, tiled=True)
+    kv_cols = soft_k.shape[1]
+    keys = both[:, :kv_cols]
+    values = both[:, kv_cols:]
     below = jnp.sum((seg_i[None, :] < seg_i[:, None]).astype(jnp.int32), axis=1)
     starts = jnp.where(
         seg_i == last_before, first_before.astype(jnp.int32), q0 + below

time: 230 us -> 164 us (0.71)
  the two profiles are of different devices: /device:TPU:224 before, /device:TPU:166 now
where the time goes in v7:
time: 164 us; the launch traced here: 163 us
  Pallas kernels  47.6 us (29%)
  waiting for transfers between devices  31.3 us (19%)
  between operations  20.2 us (12%)
  starting transfers between devices  19.1 us (12%)
  blocking collectives  13.6 us (8%)
  other arithmetic  12.5 us (8%)
  local copies, waits for them, and re-layouts  12.4 us (8%)
  matrix products  6.62 us (4%)
    pallas_call x1, Pallas kernels, flash_attention(): pl.pallas_call(kernel, out_shape=jax.ShapeDtypeStruct((rows, total), jnp....  47.6 us
    all_to_all x1, waiting for transfers between devices, body(): sent = lax.all_to_all(jnp.concatenate([chunks, info], axis=1), 'seq', 0, 0)  17.2 us
    all_to_all x1, waiting for transfers between devices, body(): state_in = lax.all_to_all(mixed, 'seq', 0, 0).reshape(heads, width, width)  14.1 us
    psum x1, blocking collectives, body(): total_sq = lax.psum(sums, 'heads')  13.6 us
    all_to_all x1, starting transfers between devices, body(): state_in = lax.all_to_all(mixed, 'seq', 0, 0).reshape(heads, width, width)  9.72 us
    all_to_all x1, starting transfers between devices, body(): sent = lax.all_to_all(jnp.concatenate([chunks, info], axis=1), 'seq', 0, 0)  9.32 us
    slice x1, local copies, waits for them, and re-layouts, body(): values = both[:, kv_cols:]  4.46 us
  transfers between devices with their start and end apart: 3, of which 2 were waited for; matrix products, arithmetic and copies ran while one was open for 16% of the time, Pallas kernels for 0%

profile of v7, /device:TPU:166, one launch (start us, length us, event | category | flops | bytes accessed | tf_op | source)
XLA Modules:
  0.0 163.3 jit_solution(13824924874869394242)
XLA Ops:
  7.2 0.0 copy-start
  7.2 0.0 all-gather.2.cloned.1.call-start
  7.2 1.6 pad_maximum_fusion.1
  8.8 0.0 all-gather.2.cloned.1.call-update
  8.8 0.7 convert_element_type.86
  9.5 0.6 slice.42
  10.1 2.0 %fusion.46 = s32[]{:T(128)} fusion(f32[]{:T(128)} %bitcast.2, s32[256]{0:T(256)} %param.17), kind=kLoop, calls=%fused_computation.68 | loop fusion | flops 1023 | bytes 1032 | tf_op jit(solution)/shard_map/reduce_sum | solution.py:167
  13.3 1.2 copy.42
  14.6 0.7 compare_select_fusion.1
  15.3 0.7 multiply_multiply_fusion
  15.9 1.3 compare_convert_fusion.1
  17.3 0.1 exponential_multiply_fusion
  17.3 1.4 convolution_add_fusion
  18.7 0.9 pad_maximum_fusion
  19.6 9.3 %all-to-all-start = ((f32[32,40,128]{2,1,0:T(8,128)}), f32[32,40,128]{2,1,0:T(8,128)S(1)}, u32[]{:S(2)}, u32[]{:S(2)}) async-start(f32[32,40,128]{2,1,0:T(8,128)} %pad_maximum_fusion), calls=%async_computation | async-start | bytes 1310720 | tf_op jit(solution)/shard_map/all_to_all | solution.py:173
  29.0 0.0 copy-done.3
  29.0 0.6 dynamic_slice.17
  30.3 0.2 convert_reduce_fusion
  30.4 0.1 fusion.26
  30.6 0.1 subtract_maximum_fusion
  30.7 17.2 %all-to-all-done = f32[32,40,128]{2,1,0:T(8,128)S(1)} async-done(((f32[32,40,128]{2,1,0:T(8,128)}), f32[32,40,128]{2,1,0:T(8,128)S(1)}, u32[]{:S(2)}, u32[]{:S(2)}) %all-to-all-start) | async-done | bytes 655392 | tf_op jit(solution)/shard_map/all_to_all | solution.py:173
  47.9 0.5 slice.54
  48.5 0.3 slice_reduce_fusion.2
  48.8 0.7 compare_select_fusion.2
  49.5 0.6 dynamic_slice.16
  50.1 0.6 slice_reduce_fusion
  50.7 1.2 fusion.49
  52.5 0.6 add_select_fusion
  53.2 0.6 fusion.56
  57.1 0.1 slice.57
  57.2 0.9 fusion.16
  58.1 0.0 copy-start.4
  58.1 1.1 copy.35
  59.2 9.7 %all-to-all-start.1 = ((f32[32,32,128]{2,1,0:T(8,128)}), f32[32,32,128]{2,1,0:T(8,128)S(1)}, u32[]{:S(2)}, u32[]{:S(2)}) async-start(f32[32,32,128]{2,1,0:T(8,128)} %copy.35), calls=%async_computation.1 | async-start | bytes 1048576 | tf_op jit(solution)/shard_map/all_to_all | solution.py:185
  68.9 0.8 copy.39.refs_4_
  69.7 0.7 stack.23.refs_0_
  70.4 0.6 fusion.54
  71.0 0.1 fusion.43
  71.1 0.0 copy-done
  71.1 0.6 fusion.5
  71.7 1.8 %fusion.2 = f32[256,8,128]{0,2,1:T(8,128)} fusion(f32[256,8,128]{0,2,1:T(8,128)S(1)} %fusion.5, bf16[256,8,128]{0,2,1:T(8,128)(2,1)S(1)} %bitcast.71, f32[256,256]{1,0:T(8,128)S(1)} %subtract_maximum_fusion, f32[8]{0:T(128)S(1)} %get-tuple-element.40, pred[256,256]{1,0:T(8,128)(4,1)S(1)} %fusion.26, bf16[256,1024]{1,0:T(8,128)(2,1)S(1)} %copy-done.4, ...), kind=kOutput, calls=%fused_computation.3 | convolution fusion | flops 270794752 | bytes 3997728 | tf_op jit(solution)/shard_map/while/body/eval_jaxpr/hts,shd->thd/dot_general | solution.py:125
  73.5 14.1 %all-to-all-done.1 = f32[32,32,128]{2,1,0:T(8,128)S(1)} async-done(((f32[32,32,128]{2,1,0:T(8,128)}), f32[32,32,128]{2,1,0:T(8,128)S(1)}, u32[]{:S(2)}, u32[]{:S(2)}) %all-to-all-start.1) | async-done | bytes 524320 | tf_op jit(solution)/shard_map/all_to_all | solution.py:185
  87.5 2.0 %multiply_reduce_fusion = (f32[256]{0:T(256)S(1)}, f32[256,8,128]{0,2,1:T(8,128)S(1)}) fusion(f32[256,8,128]{0,2,1:T(8,128)} %fusion.2, f32[8,128,128]{2,1,0:T(8,128)S(1)} %bitcast.69, f32[256,8]{0,1:T(8,128)S(1)} %get-tuple-element.24, bf16[256,1024]{1,0:T(8,128)(2,1)S(1)} %copy-done), kind=kOutput, calls=%fused_computation.11 | convolution fusion | flops 403701504 | bytes 3154944 | tf_op jit(solution)/shard_map/thd,hde->the/dot_general | solution.py:197
  89.5 0.3 copy.38
  89.9 13.6 %psum.7 = f32[256]{0:T(256)S(1)} all-reduce(f32[256]{0:T(256)S(1)} %get-tuple-element.41), channel_id=1, replica_groups=mesh['seq'=32,'heads'=8] {'heads'}, use_global_device_ids=true, to_apply=%region_2.3 | all-reduce | flops 256 | bytes 2048 | tf_op jit(solution)/shard_map/psum | solution.py:202
  103.4 1.0 multiply_convert_fusion
  104.4 4.5 %fusion.55 = (bf16[8192,128]{1,0:T(8,128)(2,1)}, bf16[8192,128]{1,0:T(8,128)(2,1)}) fusion(bf16[8192,256]{1,0:T(8,128)(2,1)} %all-gather.2.cloned.1.call-done), kind=kLoop, calls=%fused_computation.83 | loop fusion | bytes 8388608 | tf_op jit(solution)/shard_map/slice | solution.py:212
  108.9 47.6 %shard_map.104 = bf16[256,1024]{1,0:T(8,128)(2,1)} custom-call(s32[5]{0:T(128)} %stack.23.refs_0_, bf16[256,1024]{1,0:T(8,128)(2,1)} %refs_1_.1, bf16[8192,128]{1,0:T(8,128)(2,1)} %get-tuple-element.23.refs_2_, bf16[8192,128]{1,0:T(8,128)(2,1)} %get-tuple-element.22.refs_3_, s32[256,1]{1,0:T(8,128)} %copy.39.refs_4_), custom_call_target="tpu_custom_call" | custom-call | flops 4294967296 | bytes 5242880 | tf_op jit(solution)/shard_map/pallas_call | solution.py:86
  (13 shorter events, 0.0 us)
Async XLA Ops:
  7.2 63.9 %copy-start = (bf16[256,1024]{1,0:T(8,128)(2,1)S(1)}, bf16[256,1024]{1,0:T(8,128)(2,1)}, u32[]{:S(2)}) copy-start(bf16[256,1024]{1,0:T(8,128)(2,1)} %param.9) | copy-start | bytes 1572868
  7.2 97.2 %all-gather.2.cloned.1.call-start = ((), (), s32[]{:S(2)}) async-start(), calls=%async_computation.2 | async-start | bytes 4325376 | tf_op jit(solution)/shard_map/all_gather | solution.py:209
  17.3 11.6 %copy-start.3 = (f32[8]{0:T(128)S(1)}, f32[8]{0:T(128)}, u32[]{:S(2)}) copy-start(f32[8]{0:T(128)} %param.12) | copy-start | bytes 100
  17.3 35.2 %copy-start.1 = (s32[256]{0:T(256)S(1)}, s32[256]{0:T(256)}, u32[]{:S(2)}) copy-start(s32[256]{0:T(256)} %param.17) | copy-start | bytes 3076
  19.6 28.3 %all-to-all-start = ((f32[32,40,128]{2,1,0:T(8,128)}), f32[32,40,128]{2,1,0:T(8,128)S(1)}, u32[]{:S(2)}, u32[]{:S(2)}) async-start(f32[32,40,128]{2,1,0:T(8,128)} %pad_maximum_fusion), calls=%async_computation | async-start | bytes 1310720 | tf_op jit(solution)/shard_map/all_to_all | solution.py:173
  58.1 13.6 %copy-start.4 = (bf16[256,1024]{1,0:T(8,128)(2,1)S(1)}, bf16[256,1024]{1,0:T(8,128)(2,1)}, u32[]{:S(2)}) copy-start(bf16[256,1024]{1,0:T(8,128)(2,1)} %param.11) | copy-start | bytes 1572868
  59.2 28.4 %all-to-all-start.1 = ((f32[32,32,128]{2,1,0:T(8,128)}), f32[32,32,128]{2,1,0:T(8,128)S(1)}, u32[]{:S(2)}, u32[]{:S(2)}) async-start(f32[32,32,128]{2,1,0:T(8,128)} %copy.35), calls=%async_computation.1 | async-start | bytes 1048576 | tf_op jit(solution)/shard_map/all_to_all | solution.py:185
  87.5 15.9 %copy-start.2 = (f32[1024]{0:T(1024)S(1)}, f32[1024]{0:T(1024)}, u32[]{:S(2)}) copy-start(f32[1024]{0:T(1024)} %param.13) | copy-start | bytes 12292
Sparse Core Ops, SparseCore 0:
  10.6 90.0 all-gather.1

commit v8 on v7

--- a/solution.py
+++ b/solution.py
@@ -187,23 +187,6 @@
     same_doc = (idx < mine) & (lasts == last_before)
     first_before = jnp.min(jnp.where(same_doc, firsts, jnp.float32(tok * parts)))
     last_in = last_before.reshape(1)
-    seg_f = segment_ids.astype(jnp.float32)
-    pos = jnp.arange(tok).astype(jnp.float32)
-    coef = (
-        jnp.exp(-decay_rates[None, :] * (pos[:, None] + 1.0))
-        * (seg_f == last_in[0]).astype(jnp.float32)[:, None]
-    )
-    q_three = lin_q.reshape(tok, heads, width)
-    q_state = jnp.einsum(
-        "thd,hde->the", q_three.astype(jnp.float32), state_in, precision=lax.Precision.HIGHEST
-    )
-    raw = (local_out + coef[:, :, None] * q_state).reshape(tok, heads * width)
-    sums = jnp.sum(raw * raw, axis=1)
-    total_sq = lax.psum(sums, "heads")
-    count = lax.axis_size("heads") * heads * width
-    lin_out = (raw * lax.rsqrt(total_sq / count + 1e-06)[:, None] * norm_gain[None, :]).astype(
-        jnp.bfloat16
-    )
     shared_heads = soft_k.shape[1] // width
     group = heads // shared_heads
     both = lax.all_gather(jnp.concatenate([soft_k, soft_v], axis=1), "seq", axis=0, tiled=True)
@@ -227,6 +210,24 @@
             )
         )
     soft_out = pieces[0] if shared_heads == 1 else jnp.concatenate(pieces, axis=1)
+    soft_out, state_in = lax.optimization_barrier((soft_out, state_in))
+    seg_f = segment_ids.astype(jnp.float32)
+    pos = jnp.arange(tok).astype(jnp.float32)
+    coef = (
+        jnp.exp(-decay_rates[None, :] * (pos[:, None] + 1.0))
+        * (seg_f == last_in[0]).astype(jnp.float32)[:, None]
+    )
+    q_three = lin_q.reshape(tok, heads, width)
+    q_state = jnp.einsum(
+        "thd,hde->the", q_three.astype(jnp.float32), state_in, precision=lax.Precision.HIGHEST
+    )
+    raw = (local_out + coef[:, :, None] * q_state).reshape(tok, heads * width)
+    sums = jnp.sum(raw * raw, axis=1)
+    total_sq = lax.psum(sums, "heads")
+    count = lax.axis_size("heads") * heads * width
+    lin_out = (raw * lax.rsqrt(total_sq / count + 1e-06)[:, None] * norm_gain[None, :]).astype(
+        jnp.bfloat16
+    )
     return (lin_out, soft_out)
 
 

time: 164 us -> 175 us (1.067)
  the two profiles are of different devices: /device:TPU:166 before, /device:TPU:229 now
where the time goes in v8:
time: 175 us
  Pallas kernels  47.6 us (27%)
  waiting for transfers between devices  43.2 us (25%)
  between operations  20 us (11%)
  starting transfers between devices  18.5 us (11%)
  blocking collectives  14.9 us (9%)
  other arithmetic  12.6 us (7%)
  local copies, waits for them, and re-layouts  12.4 us (7%)
  matrix products  5.58 us (3%)
    pallas_call x1, Pallas kernels, flash_attention(): pl.pallas_call(kernel, out_shape=jax.ShapeDtypeStruct((rows, total), jnp....  47.6 us
    all_gather x1, waiting for transfers between devices, body(): lax.all_gather(jnp.concatenate([soft_k, soft_v], axis=1), 'seq', axis=0,...  27.4 us
    all_to_all x1, waiting for transfers between devices, body(): sent = lax.all_to_all(jnp.concatenate([chunks, info], axis=1), 'seq', 0, 0)  15.8 us
    psum x1, blocking collectives, body(): total_sq = lax.psum(sums, 'heads')  14.9 us
    all_to_all x1, starting transfers between devices, body(): state_in = lax.all_to_all(mixed, 'seq', 0, 0).reshape(heads, width, width)  10.5 us
    all_to_all x1, starting transfers between devices, body(): sent = lax.all_to_all(jnp.concatenate([chunks, info], axis=1), 'seq', 0, 0)  7.94 us
    slice x1, local copies, waits for them, and re-layouts, body(): values = both[:, kv_cols:]  4.46 us
  transfers between devices with their start and end apart: 3, of which 2 were waited for; matrix products, arithmetic and copies ran while one was open for 15% of the time, Pallas kernels for 27%

profile of v8, /device:TPU:229, one launch (start us, length us, event | category | flops | bytes accessed | tf_op | source)
XLA Modules:
  0.0 174.8 jit_solution(12970789121927347426)
XLA Ops:
  7.2 0.0 copy-start
  7.2 0.0 all-gather.2.cloned.1.call-start
  7.2 1.6 pad_maximum_fusion.1
  8.8 0.0 all-gather.2.cloned.1.call-update
  8.8 0.7 convert_element_type.86
  9.5 0.6 slice.42
  10.1 2.0 %fusion.46 = s32[]{:T(128)} fusion(f32[]{:T(128)} %bitcast.2, s32[256]{0:T(256)} %param.17), kind=kLoop, calls=%fused_computation.68 | loop fusion | flops 1023 | bytes 1032 | tf_op jit(solution)/shard_map/reduce_sum | solution.py:167
  13.4 1.2 copy.42
  14.6 0.0 copy-start.1
  14.6 0.7 compare_select_fusion.1
  15.4 0.7 multiply_multiply_fusion
  16.0 1.3 compare_convert_fusion.1
  17.4 0.1 exponential_multiply_fusion
  17.4 1.4 convolution_add_fusion
  18.8 0.9 pad_maximum_fusion
  19.7 0.0 copy-done.1
  19.7 7.9 %all-to-all-start = ((f32[32,40,128]{2,1,0:T(8,128)}), f32[32,40,128]{2,1,0:T(8,128)S(1)}, u32[]{:S(2)}, u32[]{:S(2)}) async-start(f32[32,40,128]{2,1,0:T(8,128)} %pad_maximum_fusion), calls=%async_computation | async-start | bytes 1310720 | tf_op jit(solution)/shard_map/all_to_all | solution.py:173
  27.7 0.6 dynamic_slice.17
  29.0 0.2 convert_reduce_fusion
  29.2 0.1 fusion.26
  29.3 0.1 subtract_maximum_fusion
  29.4 15.8 %all-to-all-done = f32[32,40,128]{2,1,0:T(8,128)S(1)} async-done(((f32[32,40,128]{2,1,0:T(8,128)}), f32[32,40,128]{2,1,0:T(8,128)S(1)}, u32[]{:S(2)}, u32[]{:S(2)}) %all-to-all-start) | async-done | bytes 655392 | tf_op jit(solution)/shard_map/all_to_all | solution.py:173
  45.3 0.5 slice.54
  45.8 0.3 slice_reduce_fusion.2
  46.1 0.7 compare_select_fusion.2
  46.8 0.6 dynamic_slice.16
  47.4 0.6 slice_reduce_fusion.1
  48.0 1.2 fusion.49
  49.9 0.6 add_select_fusion
  50.5 0.6 fusion.56
  54.2 0.1 slice.60
  54.2 0.9 fusion.16
  55.1 1.1 copy.36
  56.2 10.5 %all-to-all-start.1 = ((f32[32,32,128]{2,1,0:T(8,128)}), f32[32,32,128]{2,1,0:T(8,128)S(1)}, u32[]{:S(2)}, u32[]{:S(2)}) async-start(f32[32,32,128]{2,1,0:T(8,128)} %copy.36), calls=%async_computation.1 | async-start | bytes 1048576 | tf_op jit(solution)/shard_map/all_to_all | solution.py:185
  66.8 0.8 copy.34.refs_4_
  67.6 0.7 stack.23.refs_0_
  68.2 0.6 fusion.54
  68.9 0.1 fusion.43
  68.9 0.6 fusion.5
  69.5 2.0 %fusion.2 = f32[256,8,128]{0,2,1:T(8,128)S(1)} fusion(f32[256,8,128]{0,2,1:T(8,128)S(1)} %fusion.5, bf16[256,8,128]{0,2,1:T(8,128)(2,1)} %bitcast.71, f32[256,256]{1,0:T(8,128)S(1)} %subtract_maximum_fusion, f32[8]{0:T(128)S(1)} %get-tuple-element.44, pred[256,256]{1,0:T(8,128)(4,1)S(1)} %fusion.26, bf16[256,1024]{1,0:T(8,128)(2,1)} %param.11, ...), kind=kOutput, calls=%fused_computation.3 | convolution fusion | flops 270794752 | bytes 3997728 | tf_op jit(solution)/shard_map/while/body/eval_jaxpr/hts,shd->thd/dot_general | solution.py:125
  71.6 27.4 %all-gather.2.cloned.1.call-done = bf16[8192,256]{1,0:T(8,128)(2,1)} async-done(((bf16[256,256]{1,0:T(8,128)(2,1)}), bf16[8192,256]{1,0:T(8,128)(2,1)}) %all-gather.2.cloned.1.call-update) | async-done | bytes 4194320 | tf_op jit(solution)/shard_map/all_gather | solution.py:192
  98.9 4.5 %fusion.55 = (bf16[8192,128]{1,0:T(8,128)(2,1)}, bf16[8192,128]{1,0:T(8,128)(2,1)}) fusion(bf16[8192,256]{1,0:T(8,128)(2,1)} %all-gather.2.cloned.1.call-done), kind=kLoop, calls=%fused_computation.83 | loop fusion | bytes 8388608 | tf_op jit(solution)/shard_map/slice | solution.py:195
  103.4 47.6 %shard_map.104 = bf16[256,1024]{1,0:T(8,128)(2,1)} custom-call(s32[5]{0:T(128)} %stack.23.refs_0_, bf16[256,1024]{1,0:T(8,128)(2,1)} %refs_1_.1, bf16[8192,128]{1,0:T(8,128)(2,1)} %get-tuple-element.36.refs_2_, bf16[8192,128]{1,0:T(8,128)(2,1)} %get-tuple-element.26.refs_3_, s32[256,1]{1,0:T(8,128)} %copy.34.refs_4_), custom_call_target="tpu_custom_call" | custom-call | flops 4294967296 | bytes 5242880 | tf_op jit(solution)/shard_map/pallas_call | solution.py:86
  151.0 0.0 all-to-all-done.1
  151.0 0.7 multiply_reduce_fusion
  151.8 14.9 %psum.7 = f32[256]{0:T(256)S(1)} all-reduce(f32[256]{0:T(256)S(1)} %get-tuple-element.45), channel_id=1, replica_groups=mesh['seq'=32,'heads'=8] {'heads'}, use_global_device_ids=true, to_apply=%region_4.5 | all-reduce | flops 256 | bytes 2048 | tf_op jit(solution)/shard_map/psum | solution.py:226
  166.6 0.3 copy.39
  167.0 0.9 multiply_convert_fusion
  (13 shorter events, 0.0 us)
Async XLA Ops:
  7.2 61.8 %copy-start = (bf16[256,1024]{1,0:T(8,128)(2,1)S(1)}, bf16[256,1024]{1,0:T(8,128)(2,1)}, u32[]{:S(2)}) copy-start(bf16[256,1024]{1,0:T(8,128)(2,1)} %param.9) | copy-start | bytes 1572868
  7.2 91.8 %all-gather.2.cloned.1.call-start = ((), (), s32[]{:S(2)}) async-start(), calls=%async_computation.2 | async-start | bytes 4325376 | tf_op jit(solution)/shard_map/all_gather | solution.py:192
  14.6 5.1 %copy-start.1 = (bf16[256,1024]{0,1:T(8,128)(2,1)}, bf16[256,1024]{0,1:T(8,128)(2,1)S(1)}, u32[]{:S(2)}) copy-start(bf16[256,1024]{0,1:T(8,128)(2,1)S(1)} %copy.42) | copy-start | bytes 1572868
  17.4 10.3 %copy-start.4 = (f32[8]{0:T(128)S(1)}, f32[8]{0:T(128)}, u32[]{:S(2)}) copy-start(f32[8]{0:T(128)} %param.12) | copy-start | bytes 100
  17.4 32.4 %copy-start.2 = (s32[256]{0:T(256)S(1)}, s32[256]{0:T(256)}, u32[]{:S(2)}) copy-start(s32[256]{0:T(256)} %param.17) | copy-start | bytes 3076
  19.7 25.5 %all-to-all-start = ((f32[32,40,128]{2,1,0:T(8,128)}), f32[32,40,128]{2,1,0:T(8,128)S(1)}, u32[]{:S(2)}, u32[]{:S(2)}) async-start(f32[32,40,128]{2,1,0:T(8,128)} %pad_maximum_fusion), calls=%async_computation | async-start | bytes 1310720 | tf_op jit(solution)/shard_map/all_to_all | solution.py:173
  56.2 94.8 %all-to-all-start.1 = ((f32[32,32,128]{2,1,0:T(8,128)}), f32[32,32,128]{2,1,0:T(8,128)S(1)}, u32[]{:S(2)}, u32[]{:S(2)}) async-start(f32[32,32,128]{2,1,0:T(8,128)} %copy.36), calls=%async_computation.1 | async-start | bytes 1048576 | tf_op jit(solution)/shard_map/all_to_all | solution.py:185
  151.0 15.9 %copy-start.3 = (f32[1024]{0:T(1024)S(1)}, f32[1024]{0:T(1024)}, u32[]{:S(2)}) copy-start(f32[1024]{0:T(1024)} %param.13) | copy-start | bytes 12292
Sparse Core Ops, SparseCore 0:
  10.6 88.2 all-gather.1

commit v9 on v7

--- a/solution.py
+++ b/solution.py
@@ -8,7 +8,7 @@
 from jax.sharding import PartitionSpec as P
 
 BLOCK = 256
-KEY_BLOCK = 512
+KEY_BLOCK = 1024
 
 
 def flash_body(sref, q_ref, k_ref, v_ref, st_ref, o_ref, m_ref, l_ref, acc_ref, *, heads, width, scale):
@@ -64,9 +64,10 @@
             o_ref[:, h * width:(h + 1) * width] = (acc_ref[h] / l_ref[h]).astype(o_ref.dtype)
 
 
-def flash_attention(q, keys, values, starts, q0):
+def flash_attention(q, both, starts, q0):
     rows, total = q.shape
-    length, width = keys.shape
+    length = both.shape[0]
+    width = both.shape[1] // 2
     heads = total // width
     kb = min(KEY_BLOCK, length)
     nk = length // kb
@@ -79,8 +80,11 @@
     fhi = (q0 + 1) // kb - 1
     sref = jnp.stack([lo, hi, flo, fhi, q0]).astype(jnp.int32)
 
-    def kv_map(j, s):
+    def k_map(j, s):
         return (jnp.minimum(jnp.maximum(j, s[0]), s[1]), 0)
+
+    def v_map(j, s):
+        return (jnp.minimum(jnp.maximum(j, s[0]), s[1]), 1)
 
     kernel = lambda *refs: flash_body(*refs, heads=heads, width=width, scale=scale)
     return pl.pallas_call(
@@ -91,8 +95,8 @@
             grid=(nk,),
             in_specs=[
                 pl.BlockSpec((rows, total), lambda j, s: (0, 0)),
-                pl.BlockSpec((kb, width), kv_map),
-                pl.BlockSpec((kb, width), kv_map),
+                pl.BlockSpec((kb, width), k_map),
+                pl.BlockSpec((kb, width), v_map),
                 pl.BlockSpec((rows, 1), lambda j, s: (0, 0)),
             ],
             out_specs=pl.BlockSpec((rows, total), lambda j, s: (0, 0)),
@@ -108,7 +112,7 @@
             transcendentals=rows * heads * length // 2,
             bytes_accessed=2 * length * width * 2 + 2 * rows * total * 2,
         ),
-    )(sref, q, keys, values, starts.reshape(rows, 1))
+    )(sref, q, both, both, starts.reshape(rows, 1))
 
 
 def light_block(carry, inputs, rates):
@@ -207,9 +211,6 @@
     shared_heads = soft_k.shape[1] // width
     group = heads // shared_heads
     both = lax.all_gather(jnp.concatenate([soft_k, soft_v], axis=1), "seq", axis=0, tiled=True)
-    kv_cols = soft_k.shape[1]
-    keys = both[:, :kv_cols]
-    values = both[:, kv_cols:]
     below = jnp.sum((seg_i[None, :] < seg_i[:, None]).astype(jnp.int32), axis=1)
     starts = jnp.where(
         seg_i == last_before, first_before.astype(jnp.int32), q0 + below
@@ -220,8 +221,7 @@
         pieces.append(
             flash_attention(
                 soft_q[:, cols],
-                keys[:, g * width:(g + 1) * width],
-                values[:, g * width:(g + 1) * width],
+                both,
                 starts,
                 q0,
             )

time: 164 us -> 147 us (0.90)
  the two profiles are of different devices: /device:TPU:166 before, /device:TPU:230 now
where the time goes in v9:
time: 147 us; the launch traced here: 146 us
  waiting for transfers between devices  34.3 us (23%)
  Pallas kernels  34.1 us (23%)
  between operations  20.2 us (14%)
  starting transfers between devices  17.1 us (12%)
  blocking collectives  13.4 us (9%)
  other arithmetic  12.5 us (9%)
  local copies, waits for them, and re-layouts  7.88 us (5%)
  matrix products  6.6 us (4%)
    pallas_call x1, Pallas kernels, flash_attention(): pl.pallas_call(kernel, out_shape=jax.ShapeDtypeStruct((rows, total), jnp....  34.1 us
    all_to_all x1, waiting for transfers between devices, body(): sent = lax.all_to_all(jnp.concatenate([chunks, info], axis=1), 'seq', 0, 0)  18.4 us
    all_to_all x1, waiting for transfers between devices, body(): state_in = lax.all_to_all(mixed, 'seq', 0, 0).reshape(heads, width, width)  15.8 us
    psum x1, blocking collectives, body(): total_sq = lax.psum(sums, 'heads')  13.4 us
    all_to_all x1, starting transfers between devices, body(): state_in = lax.all_to_all(mixed, 'seq', 0, 0).reshape(heads, width, width)  8.61 us
    all_to_all x1, starting transfers between devices, body(): sent = lax.all_to_all(jnp.concatenate([chunks, info], axis=1), 'seq', 0, 0)  8.47 us
  transfers between devices with their start and end apart: 3, of which 2 were waited for; matrix products, arithmetic and copies ran while one was open for 17% of the time, Pallas kernels for 0%

profile of v9, /device:TPU:230, one launch (start us, length us, event | category | flops | bytes accessed | tf_op | source)
XLA Modules:
  0.0 146.1 jit_solution(10023498585358062912)
XLA Ops:
  7.2 0.0 copy-start
  7.2 0.0 all-gather.2.cloned.1.call-start
  7.2 1.6 %pad_maximum_fusion.1 = bf16[256,256]{1,0:T(8,128)(2,1)} fusion(bf16[256,128]{1,0:T(8,128)(2,1)} %param.16, bf16[256,128]{1,0:T(8,128)(2,1)} %param.15), kind=kLoop, calls=%fused_computation.36 | loop fusion | flops 262144 | bytes 262144 | tf_op jit(solution)/shard_map/concatenate | solution.py:213
  8.8 0.0 all-gather.2.cloned.1.call-update
  8.8 0.7 convert_element_type.86
  9.5 0.6 slice.36
  10.1 2.0 %fusion.46 = s32[]{:T(128)} fusion(f32[]{:T(128)} %bitcast.2, s32[256]{0:T(256)} %param.17), kind=kLoop, calls=%fused_computation.68 | loop fusion | flops 1023 | bytes 1032 | tf_op jit(solution)/shard_map/reduce_sum | solution.py:171
  12.7 1.2 copy.42
  14.6 0.6 compare_select_fusion.1
  15.3 0.7 multiply_multiply_fusion
  15.9 1.3 compare_convert_fusion.1
  17.3 0.1 exponential_multiply_fusion
  17.3 1.4 convolution_add_fusion
  18.7 0.9 pad_maximum_fusion
  19.6 8.5 %all-to-all-start = ((f32[32,40,128]{2,1,0:T(8,128)}), f32[32,40,128]{2,1,0:T(8,128)S(1)}, u32[]{:S(2)}, u32[]{:S(2)}) async-start(f32[32,40,128]{2,1,0:T(8,128)} %pad_maximum_fusion), calls=%async_computation | async-start | bytes 1310720 | tf_op jit(solution)/shard_map/all_to_all | solution.py:177
  28.1 0.0 copy-done.3
  28.1 0.6 dynamic_slice.17
  29.4 0.2 convert_reduce_fusion
  29.6 0.2 fusion.26
  29.8 0.1 subtract_maximum_fusion
  29.9 18.4 %all-to-all-done = f32[32,40,128]{2,1,0:T(8,128)S(1)} async-done(((f32[32,40,128]{2,1,0:T(8,128)}), f32[32,40,128]{2,1,0:T(8,128)S(1)}, u32[]{:S(2)}, u32[]{:S(2)}) %all-to-all-start) | async-done | bytes 655392 | tf_op jit(solution)/shard_map/all_to_all | solution.py:177
  48.3 0.5 slice.46
  48.8 0.3 slice_reduce_fusion.2
  49.1 0.7 compare_select_fusion.2
  49.9 0.6 dynamic_slice.16
  50.4 0.6 slice_reduce_fusion
  51.0 1.2 fusion.49
  52.9 0.0 copy-done.1
  52.9 0.6 add_select_fusion
  53.5 0.6 fusion.55
  57.5 0.1 slice.49
  57.5 0.9 fusion.16
  58.4 0.0 copy-start.4
  58.4 1.1 copy.35
  59.5 8.6 %all-to-all-start.1 = ((f32[32,32,128]{2,1,0:T(8,128)}), f32[32,32,128]{2,1,0:T(8,128)S(1)}, u32[]{:S(2)}, u32[]{:S(2)}) async-start(f32[32,32,128]{2,1,0:T(8,128)} %copy.35), calls=%async_computation.1 | async-start | bytes 1048576 | tf_op jit(solution)/shard_map/all_to_all | solution.py:189
  68.2 0.8 copy.39.refs_4_
  69.0 0.6 stack.23.refs_0_
  69.5 0.6 fusion.54
  70.2 0.1 fusion.43
  70.2 0.0 copy-done
  70.2 0.6 fusion.5
  70.9 1.8 %fusion.2 = f32[256,8,128]{0,2,1:T(8,128)} fusion(f32[256,8,128]{0,2,1:T(8,128)S(1)} %fusion.5, bf16[256,8,128]{0,2,1:T(8,128)(2,1)S(1)} %bitcast.71, f32[256,256]{1,0:T(8,128)S(1)} %subtract_maximum_fusion, f32[8]{0:T(128)S(1)} %get-tuple-element.38, pred[256,256]{1,0:T(8,128)(4,1)S(1)} %fusion.26, bf16[256,1024]{1,0:T(8,128)(2,1)S(1)} %copy-done.4, ...), kind=kOutput, calls=%fused_computation.3 | convolution fusion | flops 270794752 | bytes 3997728 | tf_op jit(solution)/shard_map/while/body/eval_jaxpr/hts,shd->thd/dot_general | solution.py:129
  72.7 15.8 %all-to-all-done.1 = f32[32,32,128]{2,1,0:T(8,128)S(1)} async-done(((f32[32,32,128]{2,1,0:T(8,128)}), f32[32,32,128]{2,1,0:T(8,128)S(1)}, u32[]{:S(2)}, u32[]{:S(2)}) %all-to-all-start.1) | async-done | bytes 524320 | tf_op jit(solution)/shard_map/all_to_all | solution.py:189
  88.5 2.0 %multiply_reduce_fusion = (f32[256]{0:T(256)S(1)}, f32[256,8,128]{0,2,1:T(8,128)S(1)}) fusion(f32[256,8,128]{0,2,1:T(8,128)} %fusion.2, f32[8,128,128]{2,1,0:T(8,128)S(1)} %bitcast.69, f32[256,8]{0,1:T(8,128)S(1)} %get-tuple-element.22, bf16[256,1024]{1,0:T(8,128)(2,1)S(1)} %copy-done), kind=kOutput, calls=%fused_computation.11 | convolution fusion | flops 403701504 | bytes 3154944 | tf_op jit(solution)/shard_map/thd,hde->the/dot_general | solution.py:201
  90.4 0.3 copy.38
  90.8 13.4 %psum.7 = f32[256]{0:T(256)S(1)} all-reduce(f32[256]{0:T(256)S(1)} %get-tuple-element.39), channel_id=1, replica_groups=mesh['seq'=32,'heads'=8] {'heads'}, use_global_device_ids=true, to_apply=%region_2.3 | all-reduce | flops 256 | bytes 2048 | tf_op jit(solution)/shard_map/psum | solution.py:206
  104.2 1.0 multiply_convert_fusion
  105.1 34.1 %shard_map.104 = bf16[256,1024]{1,0:T(8,128)(2,1)} custom-call(s32[5]{0:T(128)} %stack.23.refs_0_, bf16[256,1024]{1,0:T(8,128)(2,1)} %refs_1_.1, bf16[8192,256]{1,0:T(8,128)(2,1)} %all-gather.2.cloned.1.call-done.refs_2_.refs_3_, bf16[8192,256]{1,0:T(8,128)(2,1)} %all-gather.2.cloned.1.call-done.refs_2_.refs_3_, s32[256,1]{1,0:T(8,128)} %copy.39.refs_4_), custom_call_target="tpu_custom_call" | custom-call | flops 4294967296 | bytes 5242880 | tf_op jit(solution)/shard_map/pallas_call | solution.py:90
  (12 shorter events, 0.0 us)
Async XLA Ops:
  7.2 63.1 %copy-start = (bf16[256,1024]{1,0:T(8,128)(2,1)S(1)}, bf16[256,1024]{1,0:T(8,128)(2,1)}, u32[]{:S(2)}) copy-start(bf16[256,1024]{1,0:T(8,128)(2,1)} %param.9) | copy-start | bytes 1572868
  7.2 98.0 %all-gather.2.cloned.1.call-start = ((), (), s32[]{:S(2)}) async-start(), calls=%async_computation.2 | async-start | bytes 4325376 | tf_op jit(solution)/shard_map/all_gather | solution.py:213
  17.3 10.8 %copy-start.3 = (f32[8]{0:T(128)S(1)}, f32[8]{0:T(128)}, u32[]{:S(2)}) copy-start(f32[8]{0:T(128)} %param.12) | copy-start | bytes 100
  17.3 35.5 %copy-start.1 = (s32[256]{0:T(256)S(1)}, s32[256]{0:T(256)}, u32[]{:S(2)}) copy-start(s32[256]{0:T(256)} %param.17) | copy-start | bytes 3076
  19.6 28.7 %all-to-all-start = ((f32[32,40,128]{2,1,0:T(8,128)}), f32[32,40,128]{2,1,0:T(8,128)S(1)}, u32[]{:S(2)}, u32[]{:S(2)}) async-start(f32[32,40,128]{2,1,0:T(8,128)} %pad_maximum_fusion), calls=%async_computation | async-start | bytes 1310720 | tf_op jit(solution)/shard_map/all_to_all | solution.py:177
  58.4 12.4 %copy-start.4 = (bf16[256,1024]{1,0:T(8,128)(2,1)S(1)}, bf16[256,1024]{1,0:T(8,128)(2,1)}, u32[]{:S(2)}) copy-start(bf16[256,1024]{1,0:T(8,128)(2,1)} %param.11) | copy-start | bytes 1572868
  59.5 28.9 %all-to-all-start.1 = ((f32[32,32,128]{2,1,0:T(8,128)}), f32[32,32,128]{2,1,0:T(8,128)S(1)}, u32[]{:S(2)}, u32[]{:S(2)}) async-start(f32[32,32,128]{2,1,0:T(8,128)} %copy.35), calls=%async_computation.1 | async-start | bytes 1048576 | tf_op jit(solution)/shard_map/all_to_all | solution.py:189
  88.5 15.7 %copy-start.2 = (f32[1024]{0:T(1024)S(1)}, f32[1024]{0:T(1024)}, u32[]{:S(2)}) copy-start(f32[1024]{0:T(1024)} %param.13) | copy-start | bytes 12292
Sparse Core Ops, SparseCore 0:
  10.6 90.3 all-gather.1

commit v10 on v9

--- a/solution.py
+++ b/solution.py
@@ -33,15 +33,12 @@
         for h in range(heads):
             q = q_ref[:, h * width:(h + 1) * width]
             s = lax.dot_general(q, k, (((1,), (1,)), ((), ())), preferred_element_type=jnp.float32) * scale
+            if masked:
+                s = jnp.where(valid, s, -jnp.inf)
             m_prev = m_ref[h]
-            if masked:
-                top = jnp.max(jnp.where(valid, s, -1e30), axis=1, keepdims=True)
-            else:
-                top = jnp.max(s, axis=1, keepdims=True)
-            m_new = jnp.maximum(m_prev, top)
-            corr = jnp.exp(m_prev - m_new)
-            e = jnp.exp(s - m_new)
-            p = jnp.where(valid, e, 0.0) if masked else e
+            m_new = jnp.maximum(m_prev, jnp.max(s, axis=1, keepdims=True))
+            corr = jnp.exp2(m_prev - m_new)
+            p = jnp.exp2(s - m_new)
             l_ref[h] = l_ref[h] * corr + jnp.sum(p, axis=1, keepdims=True)
             pv = jnp.dot(p.astype(jnp.bfloat16), v, preferred_element_type=jnp.float32)
             acc_ref[h] = acc_ref[h] * corr + pv
@@ -71,7 +68,7 @@
     heads = total // width
     kb = min(KEY_BLOCK, length)
     nk = length // kb
-    scale = 1.0 / math.sqrt(width)
+    scale = math.log2(math.e) / math.sqrt(width)
     first = starts[0]
     last_start = starts[rows - 1]
     lo = first // kb

time: 147 us -> 145 us (0.986)
  the two profiles are of different devices: /device:TPU:230 before, /device:TPU:166 now
where the time goes in v10:
time: 145 us; the launch traced here: 143 us
  Pallas kernels  32.8 us (23%)
  waiting for transfers between devices  31.3 us (22%)
  between operations  20.2 us (14%)
  starting transfers between devices  19.1 us (13%)
  blocking collectives  13.1 us (9%)
  other arithmetic  12.5 us (9%)
  local copies, waits for them, and re-layouts  7.89 us (5%)
  matrix products  6.62 us (5%)
    pallas_call x1, Pallas kernels, flash_attention(): pl.pallas_call(kernel, out_shape=jax.ShapeDtypeStruct((rows, total), jnp....  32.8 us
    all_to_all x1, waiting for transfers between devices, body(): sent = lax.all_to_all(jnp.concatenate([chunks, info], axis=1), 'seq', 0, 0)  17.3 us
    all_to_all x1, waiting for transfers between devices, body(): state_in = lax.all_to_all(mixed, 'seq', 0, 0).reshape(heads, width, width)  13.9 us
    psum x1, blocking collectives, body(): total_sq = lax.psum(sums, 'heads')  13.1 us
    all_to_all x1, starting transfers between devices, body(): state_in = lax.all_to_all(mixed, 'seq', 0, 0).reshape(heads, width, width)  9.74 us
    all_to_all x1, starting transfers between devices, body(): sent = lax.all_to_all(jnp.concatenate([chunks, info], axis=1), 'seq', 0, 0)  9.32 us
  transfers between devices with their start and end apart: 3, of which 2 were waited for; matrix products, arithmetic and copies ran while one was open for 18% of the time, Pallas kernels for 0%

profile of v10, /device:TPU:166, one launch (start us, length us, event | category | flops | bytes accessed | tf_op | source)
XLA Modules:
  0.0 143.5 jit_solution(17172494272419967770)
XLA Ops:
  7.2 0.0 copy-start
  7.2 0.0 all-gather.2.cloned.1.call-start
  7.2 1.6 %pad_maximum_fusion.1 = bf16[256,256]{1,0:T(8,128)(2,1)} fusion(bf16[256,128]{1,0:T(8,128)(2,1)} %param.16, bf16[256,128]{1,0:T(8,128)(2,1)} %param.15), kind=kLoop, calls=%fused_computation.36 | loop fusion | flops 262144 | bytes 262144 | tf_op jit(solution)/shard_map/concatenate | solution.py:210
  8.8 0.0 all-gather.2.cloned.1.call-update
  8.8 0.7 convert_element_type.86
  9.5 0.6 slice.36
  10.1 2.0 %fusion.46 = s32[]{:T(128)} fusion(f32[]{:T(128)} %bitcast.2, s32[256]{0:T(256)} %param.17), kind=kLoop, calls=%fused_computation.68 | loop fusion | flops 1023 | bytes 1032 | tf_op jit(solution)/shard_map/reduce_sum | solution.py:168
  12.7 1.2 copy.42
  14.6 0.6 compare_select_fusion.1
  15.3 0.7 multiply_multiply_fusion
  15.9 1.3 compare_convert_fusion.1
  17.3 0.1 exponential_multiply_fusion
  17.3 1.4 convolution_add_fusion
  18.7 0.9 pad_maximum_fusion
  19.6 9.3 %all-to-all-start = ((f32[32,40,128]{2,1,0:T(8,128)}), f32[32,40,128]{2,1,0:T(8,128)S(1)}, u32[]{:S(2)}, u32[]{:S(2)}) async-start(f32[32,40,128]{2,1,0:T(8,128)} %pad_maximum_fusion), calls=%async_computation | async-start | bytes 1310720 | tf_op jit(solution)/shard_map/all_to_all | solution.py:174
  29.0 0.0 copy-done.3
  29.0 0.6 dynamic_slice.17
  30.3 0.2 convert_reduce_fusion
  30.4 0.1 fusion.26
  30.6 0.1 subtract_maximum_fusion
  30.7 17.3 %all-to-all-done = f32[32,40,128]{2,1,0:T(8,128)S(1)} async-done(((f32[32,40,128]{2,1,0:T(8,128)}), f32[32,40,128]{2,1,0:T(8,128)S(1)}, u32[]{:S(2)}, u32[]{:S(2)}) %all-to-all-start) | async-done | bytes 655392 | tf_op jit(solution)/shard_map/all_to_all | solution.py:174
  48.0 0.5 slice.46
  48.5 0.3 slice_reduce_fusion.2
  48.9 0.7 compare_select_fusion.2
  49.6 0.6 dynamic_slice.16
  50.2 0.6 slice_reduce_fusion
  50.7 1.2 fusion.49
  52.6 0.0 copy-done.1
  52.6 0.6 add_select_fusion
  53.2 0.6 fusion.55
  57.2 0.1 slice.49
  57.2 0.9 fusion.16
  58.1 0.0 copy-start.4
  58.1 1.1 copy.35
  59.2 9.7 %all-to-all-start.1 = ((f32[32,32,128]{2,1,0:T(8,128)}), f32[32,32,128]{2,1,0:T(8,128)S(1)}, u32[]{:S(2)}, u32[]{:S(2)}) async-start(f32[32,32,128]{2,1,0:T(8,128)} %copy.35), calls=%async_computation.1 | async-start | bytes 1048576 | tf_op jit(solution)/shard_map/all_to_all | solution.py:186
  69.0 0.8 copy.39.refs_4_
  69.8 0.6 stack.23.refs_0_
  70.4 0.6 fusion.54
  71.0 0.1 fusion.43
  71.1 0.0 copy-done
  71.1 0.6 fusion.5
  71.7 1.8 %fusion.2 = f32[256,8,128]{0,2,1:T(8,128)} fusion(f32[256,8,128]{0,2,1:T(8,128)S(1)} %fusion.5, bf16[256,8,128]{0,2,1:T(8,128)(2,1)S(1)} %bitcast.71, f32[256,256]{1,0:T(8,128)S(1)} %subtract_maximum_fusion, f32[8]{0:T(128)S(1)} %get-tuple-element.38, pred[256,256]{1,0:T(8,128)(4,1)S(1)} %fusion.26, bf16[256,1024]{1,0:T(8,128)(2,1)S(1)} %copy-done.4, ...), kind=kOutput, calls=%fused_computation.3 | convolution fusion | flops 270794752 | bytes 3997728 | tf_op jit(solution)/shard_map/while/body/eval_jaxpr/hts,shd->thd/dot_general | solution.py:126
  73.5 13.9 %all-to-all-done.1 = f32[32,32,128]{2,1,0:T(8,128)S(1)} async-done(((f32[32,32,128]{2,1,0:T(8,128)}), f32[32,32,128]{2,1,0:T(8,128)S(1)}, u32[]{:S(2)}, u32[]{:S(2)}) %all-to-all-start.1) | async-done | bytes 524320 | tf_op jit(solution)/shard_map/all_to_all | solution.py:186
  87.5 2.0 %multiply_reduce_fusion = (f32[256]{0:T(256)S(1)}, f32[256,8,128]{0,2,1:T(8,128)S(1)}) fusion(f32[256,8,128]{0,2,1:T(8,128)} %fusion.2, f32[8,128,128]{2,1,0:T(8,128)S(1)} %bitcast.69, f32[256,8]{0,1:T(8,128)S(1)} %get-tuple-element.22, bf16[256,1024]{1,0:T(8,128)(2,1)S(1)} %copy-done), kind=kOutput, calls=%fused_computation.11 | convolution fusion | flops 403701504 | bytes 3154944 | tf_op jit(solution)/shard_map/thd,hde->the/dot_general | solution.py:198
  89.4 0.3 copy.38
  89.8 13.1 %psum.7 = f32[256]{0:T(256)S(1)} all-reduce(f32[256]{0:T(256)S(1)} %get-tuple-element.39), channel_id=1, replica_groups=mesh['seq'=32,'heads'=8] {'heads'}, use_global_device_ids=true, to_apply=%region_2.3 | all-reduce | flops 256 | bytes 2048 | tf_op jit(solution)/shard_map/psum | solution.py:203
  102.9 1.0 multiply_convert_fusion
  103.8 32.8 %shard_map.104 = bf16[256,1024]{1,0:T(8,128)(2,1)} custom-call(s32[5]{0:T(128)} %stack.23.refs_0_, bf16[256,1024]{1,0:T(8,128)(2,1)} %refs_1_.1, bf16[8192,256]{1,0:T(8,128)(2,1)} %all-gather.2.cloned.1.call-done.refs_2_.refs_3_, bf16[8192,256]{1,0:T(8,128)(2,1)} %all-gather.2.cloned.1.call-done.refs_2_.refs_3_, s32[256,1]{1,0:T(8,128)} %copy.39.refs_4_), custom_call_target="tpu_custom_call" | custom-call | flops 4294967296 | bytes 5242880 | tf_op jit(solution)/shard_map/pallas_call | solution.py:87
  (12 shorter events, 0.0 us)
Async XLA Ops:
  7.2 63.9 %copy-start = (bf16[256,1024]{1,0:T(8,128)(2,1)S(1)}, bf16[256,1024]{1,0:T(8,128)(2,1)}, u32[]{:S(2)}) copy-start(bf16[256,1024]{1,0:T(8,128)(2,1)} %param.9) | copy-start | bytes 1572868
  7.2 96.6 %all-gather.2.cloned.1.call-start = ((), (), s32[]{:S(2)}) async-start(), calls=%async_computation.2 | async-start | bytes 4325376 | tf_op jit(solution)/shard_map/all_gather | solution.py:210
  17.3 11.6 %copy-start.3 = (f32[8]{0:T(128)S(1)}, f32[8]{0:T(128)}, u32[]{:S(2)}) copy-start(f32[8]{0:T(128)} %param.12) | copy-start | bytes 100
  17.3 35.3 %copy-start.1 = (s32[256]{0:T(256)S(1)}, s32[256]{0:T(256)}, u32[]{:S(2)}) copy-start(s32[256]{0:T(256)} %param.17) | copy-start | bytes 3076
  19.6 28.4 %all-to-all-start = ((f32[32,40,128]{2,1,0:T(8,128)}), f32[32,40,128]{2,1,0:T(8,128)S(1)}, u32[]{:S(2)}, u32[]{:S(2)}) async-start(f32[32,40,128]{2,1,0:T(8,128)} %pad_maximum_fusion), calls=%async_computation | async-start | bytes 1310720 | tf_op jit(solution)/shard_map/all_to_all | solution.py:174
  58.1 13.6 %copy-start.4 = (bf16[256,1024]{1,0:T(8,128)(2,1)S(1)}, bf16[256,1024]{1,0:T(8,128)(2,1)}, u32[]{:S(2)}) copy-start(bf16[256,1024]{1,0:T(8,128)(2,1)} %param.11) | copy-start | bytes 1572868
  59.2 28.2 %all-to-all-start.1 = ((f32[32,32,128]{2,1,0:T(8,128)}), f32[32,32,128]{2,1,0:T(8,128)S(1)}, u32[]{:S(2)}, u32[]{:S(2)}) async-start(f32[32,32,128]{2,1,0:T(8,128)} %copy.35), calls=%async_computation.1 | async-start | bytes 1048576 | tf_op jit(solution)/shard_map/all_to_all | solution.py:186
  87.5 15.4 %copy-start.2 = (f32[1024]{0:T(1024)S(1)}, f32[1024]{0:T(1024)}, u32[]{:S(2)}) copy-start(f32[1024]{0:T(1024)} %param.13) | copy-start | bytes 12292
Sparse Core Ops, SparseCore 0:
  10.6 89.9 all-gather.1

commit v11 on v10

--- a/solution.py
+++ b/solution.py
@@ -11,7 +11,7 @@
 KEY_BLOCK = 1024
 
 
-def flash_body(sref, q_ref, k_ref, v_ref, st_ref, o_ref, m_ref, l_ref, acc_ref, *, heads, width, scale):
+def flash_body(sref, q_ref, k_ref, v_ref, st_ref, o_ref, m_ref, l_ref, acc_ref, vx_ref, *, heads, width, scale):
     j = pl.program_id(0)
     lo, hi, flo, fhi, q0 = sref[0], sref[1], sref[2], sref[3], sref[4]
     rows = q_ref.shape[0]
@@ -22,10 +22,12 @@
         m_ref[...] = jnp.full(m_ref.shape, -1e30, jnp.float32)
         l_ref[...] = jnp.zeros(l_ref.shape, jnp.float32)
         acc_ref[...] = jnp.zeros(acc_ref.shape, jnp.float32)
+        vx_ref[:, width:] = jnp.ones((vx_ref.shape[0], width), vx_ref.dtype)
 
     def step(masked):
         k = k_ref[...]
-        v = v_ref[...]
+        vx_ref[:, :width] = v_ref[...]
+        vx = vx_ref[...]
         if masked:
             kpos = j * kb + lax.broadcasted_iota(jnp.int32, (rows, kb), 1)
             qpos = q0 + lax.broadcasted_iota(jnp.int32, (rows, kb), 0)
@@ -39,9 +41,9 @@
             m_new = jnp.maximum(m_prev, jnp.max(s, axis=1, keepdims=True))
             corr = jnp.exp2(m_prev - m_new)
             p = jnp.exp2(s - m_new)
-            l_ref[h] = l_ref[h] * corr + jnp.sum(p, axis=1, keepdims=True)
-            pv = jnp.dot(p.astype(jnp.bfloat16), v, preferred_element_type=jnp.float32)
-            acc_ref[h] = acc_ref[h] * corr + pv
+            pv = jnp.dot(p.astype(jnp.bfloat16), vx, preferred_element_type=jnp.float32)
+            l_ref[h] = l_ref[h] * corr + pv[:, width:width + 1]
+            acc_ref[h] = acc_ref[h] * corr + pv[:, :width]
             m_ref[h] = m_new
 
     inside = (j >= lo) & (j <= hi)
@@ -101,6 +103,7 @@
                 pltpu.VMEM((heads, rows, 1), jnp.float32),
                 pltpu.VMEM((heads, rows, 1), jnp.float32),
                 pltpu.VMEM((heads, rows, width), jnp.float32),
+                pltpu.VMEM((kb, 2 * width), jnp.bfloat16),
             ],
         ),
         compiler_params=pltpu.CompilerParams(dimension_semantics=("arbitrary",)),

time: 145 us -> 136 us (0.938)
  the two profiles are of different devices: /device:TPU:166 before, /device:TPU:230 now
where the time goes in v11:
time: 136 us; the launch traced here: 135 us
  waiting for transfers between devices  34.3 us (25%)
  Pallas kernels  23.5 us (17%)
  between operations  20.2 us (15%)
  starting transfers between devices  17.1 us (13%)
  blocking collectives  13.4 us (10%)
  other arithmetic  12.5 us (9%)
  local copies, waits for them, and re-layouts  7.88 us (6%)
  matrix products  6.6 us (5%)
    pallas_call x1, Pallas kernels, flash_attention(): pl.pallas_call(kernel, out_shape=jax.ShapeDtypeStruct((rows, total), jnp....  23.5 us
    all_to_all x1, waiting for transfers between devices, body(): sent = lax.all_to_all(jnp.concatenate([chunks, info], axis=1), 'seq', 0, 0)  18.4 us
    all_to_all x1, waiting for transfers between devices, body(): state_in = lax.all_to_all(mixed, 'seq', 0, 0).reshape(heads, width, width)  15.8 us
    psum x1, blocking collectives, body(): total_sq = lax.psum(sums, 'heads')  13.4 us
    all_to_all x1, starting transfers between devices, body(): state_in = lax.all_to_all(mixed, 'seq', 0, 0).reshape(heads, width, width)  8.61 us
    all_to_all x1, starting transfers between devices, body(): sent = lax.all_to_all(jnp.concatenate([chunks, info], axis=1), 'seq', 0, 0)  8.47 us
  transfers between devices with their start and end apart: 3, of which 2 were waited for; matrix products, arithmetic and copies ran while one was open for 19% of the time, Pallas kernels for 0%

profile of v11, /device:TPU:230, one launch (start us, length us, event | category | flops | bytes accessed | tf_op | source)
XLA Modules:
  0.0 135.5 jit_solution(16199252566210392922)
XLA Ops:
  7.2 0.0 copy-start
  7.2 0.0 all-gather.2.cloned.1.call-start
  7.2 1.6 %pad_maximum_fusion.1 = bf16[256,256]{1,0:T(8,128)(2,1)} fusion(bf16[256,128]{1,0:T(8,128)(2,1)} %param.16, bf16[256,128]{1,0:T(8,128)(2,1)} %param.15), kind=kLoop, calls=%fused_computation.36 | loop fusion | flops 262144 | bytes 262144 | tf_op jit(solution)/shard_map/concatenate | solution.py:213
  8.8 0.0 all-gather.2.cloned.1.call-update
  8.8 0.7 convert_element_type.86
  9.5 0.6 slice.36
  10.1 2.0 %fusion.46 = s32[]{:T(128)} fusion(f32[]{:T(128)} %bitcast.2, s32[256]{0:T(256)} %param.17), kind=kLoop, calls=%fused_computation.68 | loop fusion | flops 1023 | bytes 1032 | tf_op jit(solution)/shard_map/reduce_sum | solution.py:171
  12.7 1.2 copy.42
  14.6 0.6 compare_select_fusion.1
  15.3 0.7 multiply_multiply_fusion
  15.9 1.3 compare_convert_fusion.1
  17.3 0.1 exponential_multiply_fusion
  17.3 1.4 %convolution_add_fusion = f32[8,128,128]{2,1,0:T(8,128)S(1)} fusion(bf16[256,8,128]{0,2,1:T(8,128)(2,1)S(1)} %bitcast.70, f32[256,8]{0,1:T(8,128)S(1)} %exponential_multiply_fusion, f32[8]{0:T(128)S(1)} %get-tuple-element.37, bf16[256,1024]{1,0:T(8,128)(2,1)} %param.11), kind=kOutput, calls=%fused_computation.9 | convolution fusion | flops 68026368 | bytes 1581088 | tf_op jit(solution)/shard_map/while/body/eval_jaxpr/shd,she->hde/dot_general | solution.py:142
  18.7 0.9 pad_maximum_fusion
  19.6 8.5 %all-to-all-start = ((f32[32,40,128]{2,1,0:T(8,128)}), f32[32,40,128]{2,1,0:T(8,128)S(1)}, u32[]{:S(2)}, u32[]{:S(2)}) async-start(f32[32,40,128]{2,1,0:T(8,128)} %pad_maximum_fusion), calls=%async_computation | async-start | bytes 1310720 | tf_op jit(solution)/shard_map/all_to_all | solution.py:177
  28.1 0.0 copy-done.3
  28.1 0.6 dynamic_slice.17
  29.4 0.2 convert_reduce_fusion
  29.6 0.2 fusion.26
  29.8 0.1 subtract_maximum_fusion
  29.9 18.4 %all-to-all-done = f32[32,40,128]{2,1,0:T(8,128)S(1)} async-done(((f32[32,40,128]{2,1,0:T(8,128)}), f32[32,40,128]{2,1,0:T(8,128)S(1)}, u32[]{:S(2)}, u32[]{:S(2)}) %all-to-all-start) | async-done | bytes 655392 | tf_op jit(solution)/shard_map/all_to_all | solution.py:177
  48.3 0.5 slice.46
  48.8 0.3 slice_reduce_fusion.2
  49.1 0.7 compare_select_fusion.2
  49.9 0.6 dynamic_slice.16
  50.4 0.6 slice_reduce_fusion
  51.0 1.2 fusion.49
  52.9 0.0 copy-done.1
  52.9 0.6 add_select_fusion
  53.5 0.6 fusion.55
  57.5 0.1 slice.49
  57.5 0.9 fusion.16
  58.4 0.0 copy-start.4
  58.4 1.1 copy.35
  59.5 8.6 %all-to-all-start.1 = ((f32[32,32,128]{2,1,0:T(8,128)}), f32[32,32,128]{2,1,0:T(8,128)S(1)}, u32[]{:S(2)}, u32[]{:S(2)}) async-start(f32[32,32,128]{2,1,0:T(8,128)} %copy.35), calls=%async_computation.1 | async-start | bytes 1048576 | tf_op jit(solution)/shard_map/all_to_all | solution.py:189
  68.2 0.8 copy.39.refs_4_
  69.0 0.6 stack.23.refs_0_
  69.5 0.6 fusion.54
  70.2 0.1 fusion.43
  70.2 0.0 copy-done
  70.2 0.6 fusion.5
  70.9 1.8 %fusion.2 = f32[256,8,128]{0,2,1:T(8,128)} fusion(f32[256,8,128]{0,2,1:T(8,128)S(1)} %fusion.5, bf16[256,8,128]{0,2,1:T(8,128)(2,1)S(1)} %bitcast.71, f32[256,256]{1,0:T(8,128)S(1)} %subtract_maximum_fusion, f32[8]{0:T(128)S(1)} %get-tuple-element.38, pred[256,256]{1,0:T(8,128)(4,1)S(1)} %fusion.26, bf16[256,1024]{1,0:T(8,128)(2,1)S(1)} %copy-done.4, ...), kind=kOutput, calls=%fused_computation.3 | convolution fusion | flops 270794752 | bytes 3997728 | tf_op jit(solution)/shard_map/while/body/eval_jaxpr/hts,shd->thd/dot_general | solution.py:129
  72.7 15.8 %all-to-all-done.1 = f32[32,32,128]{2,1,0:T(8,128)S(1)} async-done(((f32[32,32,128]{2,1,0:T(8,128)}), f32[32,32,128]{2,1,0:T(8,128)S(1)}, u32[]{:S(2)}, u32[]{:S(2)}) %all-to-all-start.1) | async-done | bytes 524320 | tf_op jit(solution)/shard_map/all_to_all | solution.py:189
  88.5 2.0 %multiply_reduce_fusion = (f32[256]{0:T(256)S(1)}, f32[256,8,128]{0,2,1:T(8,128)S(1)}) fusion(f32[256,8,128]{0,2,1:T(8,128)} %fusion.2, f32[8,128,128]{2,1,0:T(8,128)S(1)} %bitcast.69, f32[256,8]{0,1:T(8,128)S(1)} %get-tuple-element.22, bf16[256,1024]{1,0:T(8,128)(2,1)S(1)} %copy-done), kind=kOutput, calls=%fused_computation.11 | convolution fusion | flops 403701504 | bytes 3154944 | tf_op jit(solution)/shard_map/thd,hde->the/dot_general | solution.py:201
  90.4 0.3 copy.38
  90.8 13.4 %psum.7 = f32[256]{0:T(256)S(1)} all-reduce(f32[256]{0:T(256)S(1)} %get-tuple-element.39), channel_id=1, replica_groups=mesh['seq'=32,'heads'=8] {'heads'}, use_global_device_ids=true, to_apply=%region_2.3 | all-reduce | flops 256 | bytes 2048 | tf_op jit(solution)/shard_map/psum | solution.py:206
  104.2 1.0 multiply_convert_fusion
  105.1 23.5 %shard_map.104 = bf16[256,1024]{1,0:T(8,128)(2,1)} custom-call(s32[5]{0:T(128)} %stack.23.refs_0_, bf16[256,1024]{1,0:T(8,128)(2,1)} %refs_1_.1, bf16[8192,256]{1,0:T(8,128)(2,1)} %all-gather.2.cloned.1.call-done.refs_2_.refs_3_, bf16[8192,256]{1,0:T(8,128)(2,1)} %all-gather.2.cloned.1.call-done.refs_2_.refs_3_, s32[256,1]{1,0:T(8,128)} %copy.39.refs_4_), custom_call_target="tpu_custom_call" | custom-call | flops 4294967296 | bytes 5242880 | tf_op jit(solution)/shard_map/pallas_call | solution.py:89
  (12 shorter events, 0.0 us)
Async XLA Ops:
  7.2 63.1 %copy-start = (bf16[256,1024]{1,0:T(8,128)(2,1)S(1)}, bf16[256,1024]{1,0:T(8,128)(2,1)}, u32[]{:S(2)}) copy-start(bf16[256,1024]{1,0:T(8,128)(2,1)} %param.9) | copy-start | bytes 1572868
  7.2 98.0 %all-gather.2.cloned.1.call-start = ((), (), s32[]{:S(2)}) async-start(), calls=%async_computation.2 | async-start | bytes 4325376 | tf_op jit(solution)/shard_map/all_gather | solution.py:213
  17.3 10.8 %copy-start.3 = (f32[8]{0:T(128)S(1)}, f32[8]{0:T(128)}, u32[]{:S(2)}) copy-start(f32[8]{0:T(128)} %param.12) | copy-start | bytes 100
  17.3 35.5 %copy-start.1 = (s32[256]{0:T(256)S(1)}, s32[256]{0:T(256)}, u32[]{:S(2)}) copy-start(s32[256]{0:T(256)} %param.17) | copy-start | bytes 3076
  19.6 28.7 %all-to-all-start = ((f32[32,40,128]{2,1,0:T(8,128)}), f32[32,40,128]{2,1,0:T(8,128)S(1)}, u32[]{:S(2)}, u32[]{:S(2)}) async-start(f32[32,40,128]{2,1,0:T(8,128)} %pad_maximum_fusion), calls=%async_computation | async-start | bytes 1310720 | tf_op jit(solution)/shard_map/all_to_all | solution.py:177
  58.4 12.4 %copy-start.4 = (bf16[256,1024]{1,0:T(8,128)(2,1)S(1)}, bf16[256,1024]{1,0:T(8,128)(2,1)}, u32[]{:S(2)}) copy-start(bf16[256,1024]{1,0:T(8,128)(2,1)} %param.11) | copy-start | bytes 1572868
  59.5 28.9 %all-to-all-start.1 = ((f32[32,32,128]{2,1,0:T(8,128)}), f32[32,32,128]{2,1,0:T(8,128)S(1)}, u32[]{:S(2)}, u32[]{:S(2)}) async-start(f32[32,32,128]{2,1,0:T(8,128)} %copy.35), calls=%async_computation.1 | async-start | bytes 1048576 | tf_op jit(solution)/shard_map/all_to_all | solution.py:189
  88.5 15.7 %copy-start.2 = (f32[1024]{0:T(1024)S(1)}, f32[1024]{0:T(1024)}, u32[]{:S(2)}) copy-start(f32[1024]{0:T(1024)} %param.13) | copy-start | bytes 12292
Sparse Core Ops, SparseCore 0:
  10.6 90.3 all-gather.1

commit v12 on v11

--- a/solution.py
+++ b/solution.py
@@ -146,6 +146,10 @@
 
 def body(lin_q, lin_k, lin_v, decay_rates, norm_gain, soft_q, soft_k, soft_v, segment_ids):
     tok = lin_q.shape[0]
+    kv_here, lin_q, lin_k, lin_v = lax.optimization_barrier(
+        (jnp.concatenate([soft_k, soft_v], axis=1), lin_q, lin_k, lin_v)
+    )
+    both = lax.all_gather(kv_here, "seq", axis=0, tiled=True)
     heads = decay_rates.shape[0]
     width = lin_q.shape[1] // heads
     blocks = tok // BLOCK
@@ -210,7 +214,6 @@
     )
     shared_heads = soft_k.shape[1] // width
     group = heads // shared_heads
-    both = lax.all_gather(jnp.concatenate([soft_k, soft_v], axis=1), "seq", axis=0, tiled=True)
     below = jnp.sum((seg_i[None, :] < seg_i[:, None]).astype(jnp.int32), axis=1)
     starts = jnp.where(
         seg_i == last_before, first_before.astype(jnp.int32), q0 + below

time: 136 us -> 136 us (level)
  the two profiles are of different devices: /device:TPU:230 before, /device:TPU:166 now
where the time goes in v12:
time: 136 us; the launch traced here: 134 us
  waiting for transfers between devices  31.3 us (23%)
  Pallas kernels  23.5 us (17%)
  between operations  20.2 us (15%)
  starting transfers between devices  19.1 us (14%)
  blocking collectives  13.1 us (10%)
  other arithmetic  12.5 us (9%)
  local copies, waits for them, and re-layouts  7.89 us (6%)
  matrix products  6.62 us (5%)
    pallas_call x1, Pallas kernels, flash_attention(): pl.pallas_call(kernel, out_shape=jax.ShapeDtypeStruct((rows, total), jnp....  23.5 us
    all_to_all x1, waiting for transfers between devices, body(): sent = lax.all_to_all(jnp.concatenate([chunks, info], axis=1), 'seq', 0, 0)  17.3 us
    all_to_all x1, waiting for transfers between devices, body(): state_in = lax.all_to_all(mixed, 'seq', 0, 0).reshape(heads, width, width)  13.9 us
    psum x1, blocking collectives, body(): total_sq = lax.psum(sums, 'heads')  13.1 us
    all_to_all x1, starting transfers between devices, body(): state_in = lax.all_to_all(mixed, 'seq', 0, 0).reshape(heads, width, width)  9.74 us
    all_to_all x1, starting transfers between devices, body(): sent = lax.all_to_all(jnp.concatenate([chunks, info], axis=1), 'seq', 0, 0)  9.32 us
  transfers between devices with their start and end apart: 3, of which 2 were waited for; matrix products, arithmetic and copies ran while one was open for 19% of the time, Pallas kernels for 0%

profile of v12, /device:TPU:166, one launch (start us, length us, event | category | flops | bytes accessed | tf_op | source)
XLA Modules:
  0.0 134.2 jit_solution(1248027023292727824)
XLA Ops:
  7.2 0.0 copy-start
  7.2 0.0 all-gather.2.cloned.1.call-start
  7.2 1.6 %pad_maximum_fusion.1 = bf16[256,256]{1,0:T(8,128)(2,1)} fusion(bf16[256,128]{1,0:T(8,128)(2,1)} %param.16, bf16[256,128]{1,0:T(8,128)(2,1)} %param.15), kind=kLoop, calls=%fused_computation.36 | loop fusion | flops 262144 | bytes 262144 | tf_op jit(solution)/shard_map/concatenate | solution.py:150
  8.8 0.0 all-gather.2.cloned.1.call-update
  8.8 0.7 convert_element_type.86
  9.5 0.6 slice.36
  10.1 2.0 %fusion.46 = s32[]{:T(128)} fusion(f32[]{:T(128)} %bitcast.2, s32[256]{0:T(256)} %param.17), kind=kLoop, calls=%fused_computation.68 | loop fusion | flops 1023 | bytes 1032 | tf_op jit(solution)/shard_map/reduce_sum | solution.py:175
  12.7 1.2 copy.42
  14.6 0.6 compare_select_fusion.1
  15.3 0.7 multiply_multiply_fusion
  15.9 1.3 compare_convert_fusion.1
  17.3 0.1 exponential_multiply_fusion
  17.3 1.4 %convolution_add_fusion = f32[8,128,128]{2,1,0:T(8,128)S(1)} fusion(bf16[256,8,128]{0,2,1:T(8,128)(2,1)S(1)} %bitcast.70, f32[256,8]{0,1:T(8,128)S(1)} %exponential_multiply_fusion, f32[8]{0:T(128)S(1)} %get-tuple-element.45, bf16[256,1024]{1,0:T(8,128)(2,1)} %param.11), kind=kOutput, calls=%fused_computation.9 | convolution fusion | flops 68026368 | bytes 1581088 | tf_op jit(solution)/shard_map/while/body/eval_jaxpr/shd,she->hde/dot_general | solution.py:142
  18.7 0.9 pad_maximum_fusion
  19.6 9.3 %all-to-all-start = ((f32[32,40,128]{2,1,0:T(8,128)}), f32[32,40,128]{2,1,0:T(8,128)S(1)}, u32[]{:S(2)}, u32[]{:S(2)}) async-start(f32[32,40,128]{2,1,0:T(8,128)} %pad_maximum_fusion), calls=%async_computation | async-start | bytes 1310720 | tf_op jit(solution)/shard_map/all_to_all | solution.py:181
  29.0 0.0 copy-done.3
  29.0 0.6 dynamic_slice.17
  30.3 0.2 convert_reduce_fusion
  30.4 0.1 fusion.26
  30.6 0.1 subtract_maximum_fusion
  30.7 17.3 %all-to-all-done = f32[32,40,128]{2,1,0:T(8,128)S(1)} async-done(((f32[32,40,128]{2,1,0:T(8,128)}), f32[32,40,128]{2,1,0:T(8,128)S(1)}, u32[]{:S(2)}, u32[]{:S(2)}) %all-to-all-start) | async-done | bytes 655392 | tf_op jit(solution)/shard_map/all_to_all | solution.py:181
  48.0 0.5 slice.46
  48.5 0.3 slice_reduce_fusion.2
  48.9 0.7 compare_select_fusion.2
  49.6 0.6 dynamic_slice.16
  50.2 0.6 slice_reduce_fusion
  50.7 1.2 fusion.49
  52.6 0.0 copy-done.1
  52.6 0.6 add_select_fusion
  53.2 0.6 fusion.55
  57.2 0.1 slice.49
  57.2 0.9 fusion.16
  58.1 0.0 copy-start.4
  58.1 1.1 copy.35
  59.2 9.7 %all-to-all-start.1 = ((f32[32,32,128]{2,1,0:T(8,128)}), f32[32,32,128]{2,1,0:T(8,128)S(1)}, u32[]{:S(2)}, u32[]{:S(2)}) async-start(f32[32,32,128]{2,1,0:T(8,128)} %copy.35), calls=%async_computation.1 | async-start | bytes 1048576 | tf_op jit(solution)/shard_map/all_to_all | solution.py:193
  69.0 0.8 copy.39.refs_4_
  69.8 0.6 stack.23.refs_0_
  70.4 0.6 fusion.54
  71.0 0.1 fusion.43
  71.1 0.0 copy-done
  71.1 0.6 fusion.5
  71.7 1.8 %fusion.2 = f32[256,8,128]{0,2,1:T(8,128)} fusion(f32[256,8,128]{0,2,1:T(8,128)S(1)} %fusion.5, bf16[256,8,128]{0,2,1:T(8,128)(2,1)S(1)} %bitcast.71, f32[256,256]{1,0:T(8,128)S(1)} %subtract_maximum_fusion, f32[8]{0:T(128)S(1)} %get-tuple-element.46, pred[256,256]{1,0:T(8,128)(4,1)S(1)} %fusion.26, bf16[256,1024]{1,0:T(8,128)(2,1)S(1)} %copy-done, ...), kind=kOutput, calls=%fused_computation.3 | convolution fusion | flops 270794752 | bytes 3997728 | tf_op jit(solution)/shard_map/while/body/eval_jaxpr/hts,shd->thd/dot_general | solution.py:129
  73.5 13.9 %all-to-all-done.1 = f32[32,32,128]{2,1,0:T(8,128)S(1)} async-done(((f32[32,32,128]{2,1,0:T(8,128)}), f32[32,32,128]{2,1,0:T(8,128)S(1)}, u32[]{:S(2)}, u32[]{:S(2)}) %all-to-all-start.1) | async-done | bytes 524320 | tf_op jit(solution)/shard_map/all_to_all | solution.py:193
  87.5 2.0 %multiply_reduce_fusion = (f32[256]{0:T(256)S(1)}, f32[256,8,128]{0,2,1:T(8,128)S(1)}) fusion(f32[256,8,128]{0,2,1:T(8,128)} %fusion.2, f32[8,128,128]{2,1,0:T(8,128)S(1)} %bitcast.69, f32[256,8]{0,1:T(8,128)S(1)} %get-tuple-element.39, bf16[256,1024]{1,0:T(8,128)(2,1)S(1)} %copy-done), kind=kOutput, calls=%fused_computation.11 | convolution fusion | flops 403701504 | bytes 3154944 | tf_op jit(solution)/shard_map/thd,hde->the/dot_general | solution.py:205
  89.4 0.3 copy.38
  89.8 13.1 %psum.7 = f32[256]{0:T(256)S(1)} all-reduce(f32[256]{0:T(256)S(1)} %get-tuple-element.47), channel_id=1, replica_groups=mesh['seq'=32,'heads'=8] {'heads'}, use_global_device_ids=true, to_apply=%region_2.3 | all-reduce | flops 256 | bytes 2048 | tf_op jit(solution)/shard_map/psum | solution.py:210
  102.9 1.0 multiply_convert_fusion
  103.8 23.5 %shard_map.104 = bf16[256,1024]{1,0:T(8,128)(2,1)} custom-call(s32[5]{0:T(128)} %stack.23.refs_0_, bf16[256,1024]{1,0:T(8,128)(2,1)} %refs_1_.1, bf16[8192,256]{1,0:T(8,128)(2,1)} %all-gather.2.cloned.1.call-done.refs_2_.refs_3_, bf16[8192,256]{1,0:T(8,128)(2,1)} %all-gather.2.cloned.1.call-done.refs_2_.refs_3_, s32[256,1]{1,0:T(8,128)} %copy.39.refs_4_), custom_call_target="tpu_custom_call" | custom-call | flops 4294967296 | bytes 5242880 | tf_op jit(solution)/shard_map/pallas_call | solution.py:89
  (12 shorter events, 0.0 us)
Async XLA Ops:
  7.2 63.9 %copy-start = (bf16[256,1024]{1,0:T(8,128)(2,1)S(1)}, bf16[256,1024]{1,0:T(8,128)(2,1)}, u32[]{:S(2)}) copy-start(bf16[256,1024]{1,0:T(8,128)(2,1)} %param.9) | copy-start | bytes 1572868
  7.2 96.6 %all-gather.2.cloned.1.call-start = ((), (), s32[]{:S(2)}) async-start(), calls=%async_computation.2 | async-start | bytes 4325376 | tf_op jit(solution)/shard_map/all_gather | solution.py:152
  17.3 11.6 %copy-start.3 = (f32[8]{0:T(128)S(1)}, f32[8]{0:T(128)}, u32[]{:S(2)}) copy-start(f32[8]{0:T(128)} %param.12) | copy-start | bytes 100
  17.3 35.3 %copy-start.1 = (s32[256]{0:T(256)S(1)}, s32[256]{0:T(256)}, u32[]{:S(2)}) copy-start(s32[256]{0:T(256)} %param.17) | copy-start | bytes 3076
  19.6 28.4 %all-to-all-start = ((f32[32,40,128]{2,1,0:T(8,128)}), f32[32,40,128]{2,1,0:T(8,128)S(1)}, u32[]{:S(2)}, u32[]{:S(2)}) async-start(f32[32,40,128]{2,1,0:T(8,128)} %pad_maximum_fusion), calls=%async_computation | async-start | bytes 1310720 | tf_op jit(solution)/shard_map/all_to_all | solution.py:181
  58.1 13.6 %copy-start.4 = (bf16[256,1024]{1,0:T(8,128)(2,1)S(1)}, bf16[256,1024]{1,0:T(8,128)(2,1)}, u32[]{:S(2)}) copy-start(bf16[256,1024]{1,0:T(8,128)(2,1)} %param.11) | copy-start | bytes 1572868
  59.2 28.2 %all-to-all-start.1 = ((f32[32,32,128]{2,1,0:T(8,128)}), f32[32,32,128]{2,1,0:T(8,128)S(1)}, u32[]{:S(2)}, u32[]{:S(2)}) async-start(f32[32,32,128]{2,1,0:T(8,128)} %copy.35), calls=%async_computation.1 | async-start | bytes 1048576 | tf_op jit(solution)/shard_map/all_to_all | solution.py:193
  87.5 15.4 %copy-start.2 = (f32[1024]{0:T(1024)S(1)}, f32[1024]{0:T(1024)}, u32[]{:S(2)}) copy-start(f32[1024]{0:T(1024)} %param.13) | copy-start | bytes 12292
Sparse Core Ops, SparseCore 0:
  10.6 89.9 all-gather.1

commit v13 on v12

--- a/solution.py
+++ b/solution.py
@@ -8,6 +8,7 @@
 from jax.sharding import PartitionSpec as P
 
 BLOCK = 256
+SEQ = ("z", "x")
 KEY_BLOCK = 1024
 
 
@@ -149,7 +150,8 @@
     kv_here, lin_q, lin_k, lin_v = lax.optimization_barrier(
         (jnp.concatenate([soft_k, soft_v], axis=1), lin_q, lin_k, lin_v)
     )
-    both = lax.all_gather(kv_here, "seq", axis=0, tiled=True)
+    both = lax.all_gather(kv_here, "x", axis=0, tiled=True)
+    both = lax.all_gather(both, "z", axis=0, tiled=True)
     heads = decay_rates.shape[0]
     width = lin_q.shape[1] // heads
     blocks = tok // BLOCK
@@ -167,8 +169,8 @@
         ),
     )
     local_out = outs.reshape(tok, heads, width)
-    mine = lax.axis_index("seq")
-    parts = lax.axis_size("seq")
+    mine = lax.axis_index(SEQ)
+    parts = lax.axis_size(SEQ)
     q0 = (mine * tok).astype(jnp.int32)
     seg_i = segment_ids.astype(jnp.float32)
     last_here = seg_i[tok - 1]
@@ -178,7 +180,7 @@
     lane = jnp.arange(width)
     info = jnp.where(lane == 0, last_here, jnp.where(lane == 1, first_here, 0.0))
     info = jnp.broadcast_to(info[None, None, :], (parts, 8, width))
-    sent = lax.all_to_all(jnp.concatenate([chunks, info], axis=1), "seq", 0, 0)
+    sent = lax.all_to_all(jnp.concatenate([chunks, info], axis=1), SEQ, 0, 0)
     lasts = sent[:, rows_per, 0]
     firsts = sent[:, rows_per, 1]
     idx = jnp.arange(parts)
@@ -190,7 +192,7 @@
     mixed = jnp.einsum(
         "pj,jrc->prc", weight, sent[:, :rows_per, :], precision=lax.Precision.HIGHEST
     )
-    state_in = lax.all_to_all(mixed, "seq", 0, 0).reshape(heads, width, width)
+    state_in = lax.all_to_all(mixed, SEQ, 0, 0).reshape(heads, width, width)
     last_before = last_prev[mine]
     same_doc = (idx < mine) & (lasts == last_before)
     first_before = jnp.min(jnp.where(same_doc, firsts, jnp.float32(tok * parts)))
@@ -235,20 +237,24 @@
 
 def solution(mesh):
     placed = (
-        P("seq", "heads"),
-        P("seq", "heads"),
-        P("seq", "heads"),
+        P(SEQ, "heads"),
+        P(SEQ, "heads"),
+        P(SEQ, "heads"),
         P("heads"),
         P("heads"),
-        P("seq", "heads"),
-        P("seq", "heads"),
-        P("seq", "heads"),
-        P("seq"),
+        P(SEQ, "heads"),
+        P(SEQ, "heads"),
+        P(SEQ, "heads"),
+        P(SEQ),
+    )
+    devices = mesh.devices
+    split = jax.sharding.Mesh(
+        devices.reshape(devices.shape[0] // 4, 4, devices.shape[1]), ("z", "x", "heads")
     )
     return jax.shard_map(
         body,
-        mesh=mesh,
+        mesh=split,
         in_specs=placed,
-        out_specs=(P("seq", "heads"), P("seq", "heads")),
+        out_specs=(P(SEQ, "heads"), P(SEQ, "heads")),
         check_vma=False,
     )

time: 136 us -> 146 us (1.074)
  blocking collectives: 13.1 us -> 26.8 us
  other arithmetic: 12.5 us -> 10.6 us
    all_gather x0 -> x1, blocking collectives: none -> 14.2 us  [body(): both = lax.all_gather(kv_here, 'x', axis=0, tiled=True)]
  transfers between devices with their start and end apart: 3 -> 3, of which waited for: 2 -> 2; matrix products, arithmetic and copies ran while one was open for 19% -> 16% of each run, Pallas kernels for 0% -> 0%
where the time goes in v13:
time: 146 us; the launch traced here: 145 us
  waiting for transfers between devices  32 us (22%)
  blocking collectives  26.8 us (18%)
  Pallas kernels  23.5 us (16%)
  between operations  20.2 us (14%)
  starting transfers between devices  18.2 us (12%)
  other arithmetic  10.6 us (7%)
  local copies, waits for them, and re-layouts  7.99 us (5%)
  matrix products  5.54 us (4%)
    pallas_call x1, Pallas kernels, flash_attention(): pl.pallas_call(kernel, out_shape=jax.ShapeDtypeStruct((rows, total), jnp....  23.5 us
    all_to_all x1, waiting for transfers between devices, body(): sent = lax.all_to_all(jnp.concatenate([chunks, info], axis=1), SEQ, 0, 0)  19.6 us
    all_gather x1, blocking collectives, body(): both = lax.all_gather(kv_here, 'x', axis=0, tiled=True)  14.2 us
    psum x1, blocking collectives, body(): total_sq = lax.psum(sums, 'heads')  12.6 us
    all_to_all x1, waiting for transfers between devices, body(): state_in = lax.all_to_all(mixed, SEQ, 0, 0).reshape(heads, width, width)  12.4 us
    all_to_all x1, starting transfers between devices, body(): state_in = lax.all_to_all(mixed, SEQ, 0, 0).reshape(heads, width, width)  9.15 us
    all_to_all x1, starting transfers between devices, body(): sent = lax.all_to_all(jnp.concatenate([chunks, info], axis=1), SEQ, 0, 0)  9.05 us
  transfers between devices with their start and end apart: 3, of which 2 were waited for; matrix products, arithmetic and copies ran while one was open for 16% of the time, Pallas kernels for 0%

profile of v13, /device:TPU:166, one launch (start us, length us, event | category | flops | bytes accessed | tf_op | source)
XLA Modules:
  0.0 144.9 jit_solution(2872631433191687446)
XLA Ops:
  7.2 0.0 copy-start
  7.2 0.0 copy-start.4
  7.2 0.0 copy-start.1
  7.2 0.0 copy-start.3
  7.2 0.0 all-gather.2.cloned.1.call-start
  7.3 1.0 pad_maximum_fusion.1
  8.2 14.2 %all_gather.6 = bf16[1024,256]{1,0:T(8,128)(2,1)} all-gather(bf16[256,256]{1,0:T(8,128)(2,1)S(1)} %pad_maximum_fusion.1), channel_id=1, replica_groups=mesh['z'=8,'x'=4,'heads'=8] {'x'}, dimensions={0}, use_global_device_ids=true | all-gather | bytes 655360 | tf_op jit(solution)/shard_map/all_gather | solution.py:153
  22.4 0.0 all-gather.2.cloned.1.call-update
  22.5 0.7 convert_element_type.86
  23.1 0.6 slice.36
  23.7 2.0 %fusion.46 = s32[]{:T(128)} fusion(f32[]{:T(128)} %bitcast.2, s32[256]{0:T(256)} %param.17), kind=kLoop, calls=%fused_computation.68 | loop fusion | flops 1023 | bytes 1032 | tf_op jit(solution)/shard_map/reduce_sum | solution.py:177
  26.3 1.2 copy.42
  28.2 0.6 compare_select_fusion.1
  28.9 0.0 copy-done.1
  28.9 0.7 compare_convert_fusion.1
  29.6 0.1 exponential_multiply_fusion
  29.7 0.3 convolution_add_fusion
  30.0 0.9 pad_maximum_fusion
  30.9 9.1 %all-to-all-start = ((f32[32,40,128]{2,1,0:T(8,128)}), f32[32,40,128]{2,1,0:T(8,128)S(1)}, u32[]{:S(2)}, u32[]{:S(2)}) async-start(f32[32,40,128]{2,1,0:T(8,128)} %pad_maximum_fusion), calls=%async_computation | async-start | bytes 1310720 | tf_op jit(solution)/shard_map/all_to_all | solution.py:183
  40.0 0.6 dynamic_slice.17
  41.3 0.2 convert_reduce_fusion
  41.4 0.1 fusion.26
  41.6 0.1 subtract_maximum_fusion
  41.7 19.6 %all-to-all-done = f32[32,40,128]{2,1,0:T(8,128)S(1)} async-done(((f32[32,40,128]{2,1,0:T(8,128)}), f32[32,40,128]{2,1,0:T(8,128)S(1)}, u32[]{:S(2)}, u32[]{:S(2)}) %all-to-all-start) | async-done | bytes 655392 | tf_op jit(solution)/shard_map/all_to_all | solution.py:183
  61.3 0.5 slice.46
  61.8 0.3 slice_reduce_fusion.2
  62.1 0.7 compare_select_fusion.2
  62.9 0.6 dynamic_slice.16
  63.4 0.6 slice_reduce_fusion
  64.0 1.2 fusion.49
  65.9 0.6 add_select_fusion
  66.5 0.6 fusion.55
  70.4 0.1 slice.49
  70.5 0.9 fusion.16
  71.4 1.1 copy.35
  72.5 9.1 %all-to-all-start.1 = ((f32[32,32,128]{2,1,0:T(8,128)}), f32[32,32,128]{2,1,0:T(8,128)S(1)}, u32[]{:S(2)}, u32[]{:S(2)}) async-start(f32[32,32,128]{2,1,0:T(8,128)} %copy.35), calls=%async_computation.1 | async-start | bytes 1048576 | tf_op jit(solution)/shard_map/all_to_all | solution.py:195
  81.7 0.8 copy.39.refs_4_
  82.5 0.7 stack.23.refs_0_
  83.2 0.6 fusion.54
  83.8 0.1 fusion.43
  83.9 0.6 fusion.5
  84.5 1.8 %fusion.2 = f32[256,8,128]{0,2,1:T(8,128)} fusion(f32[256,8,128]{0,2,1:T(8,128)S(1)} %fusion.5, bf16[256,8,128]{0,2,1:T(8,128)(2,1)S(1)} %bitcast.71, f32[256,256]{1,0:T(8,128)S(1)} %subtract_maximum_fusion, f32[8]{0:T(128)S(1)} %get-tuple-element.46, pred[256,256]{1,0:T(8,128)(4,1)S(1)} %fusion.26, bf16[256,1024]{1,0:T(8,128)(2,1)S(1)} %copy-done, ...), kind=kOutput, calls=%fused_computation.3 | convolution fusion | flops 270794752 | bytes 3997728 | tf_op jit(solution)/shard_map/while/body/eval_jaxpr/hts,shd->thd/dot_general | solution.py:130
  86.3 12.4 %all-to-all-done.1 = f32[32,32,128]{2,1,0:T(8,128)S(1)} async-done(((f32[32,32,128]{2,1,0:T(8,128)}), f32[32,32,128]{2,1,0:T(8,128)S(1)}, u32[]{:S(2)}, u32[]{:S(2)}) %all-to-all-start.1) | async-done | bytes 524320 | tf_op jit(solution)/shard_map/all_to_all | solution.py:195
  98.6 2.0 %multiply_reduce_fusion = (f32[256]{0:T(256)S(1)}, f32[256,8,128]{0,2,1:T(8,128)S(1)}) fusion(f32[256,8,128]{0,2,1:T(8,128)} %fusion.2, f32[8,128,128]{2,1,0:T(8,128)S(1)} %bitcast.69, f32[256,8]{0,1:T(8,128)S(1)} %get-tuple-element.39, bf16[256,1024]{1,0:T(8,128)(2,1)S(1)} %copy-done), kind=kOutput, calls=%fused_computation.11 | convolution fusion | flops 403701504 | bytes 3154944 | tf_op jit(solution)/shard_map/thd,hde->the/dot_general | solution.py:207
  100.6 0.3 copy.38
  100.9 12.6 %psum.7 = f32[256]{0:T(256)S(1)} all-reduce(f32[256]{0:T(256)S(1)} %get-tuple-element.47), channel_id=1, replica_groups=mesh['z'=8,'x'=4,'heads'=8] {'heads'}, use_global_device_ids=true, to_apply=%region_2.3 | all-reduce | flops 256 | bytes 2048 | tf_op jit(solution)/shard_map/psum | solution.py:212
  113.6 1.0 multiply_convert_fusion
  114.5 23.5 %shard_map.104 = bf16[256,1024]{1,0:T(8,128)(2,1)} custom-call(s32[5]{0:T(128)} %stack.23.refs_0_, bf16[256,1024]{1,0:T(8,128)(2,1)} %refs_1_.1, bf16[8192,256]{1,0:T(8,128)(2,1)} %all-gather.2.cloned.1.call-done.refs_2_.refs_3_, bf16[8192,256]{1,0:T(8,128)(2,1)} %all-gather.2.cloned.1.call-done.refs_2_.refs_3_, s32[256,1]{1,0:T(8,128)} %copy.39.refs_4_), custom_call_target="tpu_custom_call" | custom-call | flops 4294967296 | bytes 5242880 | tf_op jit(solution)/shard_map/pallas_call | solution.py:90
  (13 shorter events, 0.1 us)
Async XLA Ops:
  7.2 76.7 %copy-start = (bf16[256,1024]{1,0:T(8,128)(2,1)S(1)}, bf16[256,1024]{1,0:T(8,128)(2,1)}, u32[]{:S(2)}) copy-start(bf16[256,1024]{1,0:T(8,128)(2,1)} %param.9) | copy-start | bytes 1572868
  7.2 22.5 %copy-start.4 = (bf16[256,1024]{1,0:T(8,128)(2,1)S(1)}, bf16[256,1024]{1,0:T(8,128)(2,1)}, u32[]{:S(2)}) copy-start(bf16[256,1024]{1,0:T(8,128)(2,1)} %param.11) | copy-start | bytes 1572868
  7.2 21.7 %copy-start.1 = (s32[256]{0:T(256)S(1)}, s32[256]{0:T(256)}, u32[]{:S(2)}) copy-start(s32[256]{0:T(256)} %param.17) | copy-start | bytes 3076
  7.2 21.7 %copy-start.3 = (f32[8]{0:T(128)S(1)}, f32[8]{0:T(128)}, u32[]{:S(2)}) copy-start(f32[8]{0:T(128)} %param.12) | copy-start | bytes 100
  7.2 107.3 %all-gather.2.cloned.1.call-start = ((), (), s32[]{:S(2)}) async-start(), calls=%async_computation.2 | async-start | bytes 4718592 | tf_op jit(solution)/shard_map/all_gather | solution.py:154
  30.9 30.4 %all-to-all-start = ((f32[32,40,128]{2,1,0:T(8,128)}), f32[32,40,128]{2,1,0:T(8,128)S(1)}, u32[]{:S(2)}, u32[]{:S(2)}) async-start(f32[32,40,128]{2,1,0:T(8,128)} %pad_maximum_fusion), calls=%async_computation | async-start | bytes 1310720 | tf_op jit(solution)/shard_map/all_to_all | solution.py:183
  72.5 26.1 %all-to-all-start.1 = ((f32[32,32,128]{2,1,0:T(8,128)}), f32[32,32,128]{2,1,0:T(8,128)S(1)}, u32[]{:S(2)}, u32[]{:S(2)}) async-start(f32[32,32,128]{2,1,0:T(8,128)} %copy.35), calls=%async_computation.1 | async-start | bytes 1048576 | tf_op jit(solution)/shard_map/all_to_all | solution.py:195
  98.6 14.9 %copy-start.2 = (f32[1024]{0:T(1024)S(1)}, f32[1024]{0:T(1024)}, u32[]{:S(2)}) copy-start(f32[1024]{0:T(1024)} %param.13) | copy-start | bytes 12292
Sparse Core Ops, SparseCore 0:
  22.6 78.9 all-gather.1

commit v14 on v12

--- a/solution.py
+++ b/solution.py
@@ -25,7 +25,7 @@
         vx_ref[:, width:] = jnp.ones((vx_ref.shape[0], width), vx_ref.dtype)
 
     def step(masked):
-        k = k_ref[...]
+        kt = k_ref[...].T
         vx_ref[:, :width] = v_ref[...]
         vx = vx_ref[...]
         if masked:
@@ -34,7 +34,7 @@
             valid = (kpos <= qpos) & (kpos >= st_ref[...])
         for h in range(heads):
             q = q_ref[:, h * width:(h + 1) * width]
-            s = lax.dot_general(q, k, (((1,), (1,)), ((), ())), preferred_element_type=jnp.float32) * scale
+            s = jnp.dot(q, kt, preferred_element_type=jnp.float32) * scale
             if masked:
                 s = jnp.where(valid, s, -jnp.inf)
             m_prev = m_ref[h]

time: 136 us -> 141 us (1.037)
  the two profiles are of different devices: /device:TPU:166 before, /device:TPU:228 now
where the time goes in v14:
time: 141 us; the launch traced here: 140 us
  waiting for transfers between devices  33.6 us (24%)
  Pallas kernels  28.9 us (20%)
  between operations  20.2 us (14%)
  starting transfers between devices  17.8 us (13%)
  blocking collectives  13 us (9%)
  other arithmetic  12.5 us (9%)
  local copies, waits for them, and re-layouts  7.89 us (6%)
  matrix products  6.6 us (5%)
    pallas_call x1, Pallas kernels, flash_attention(): pl.pallas_call(kernel, out_shape=jax.ShapeDtypeStruct((rows, total), jnp....  28.9 us
    all_to_all x1, waiting for transfers between devices, body(): sent = lax.all_to_all(jnp.concatenate([chunks, info], axis=1), 'seq', 0, 0)  17.8 us
    all_to_all x1, waiting for transfers between devices, body(): state_in = lax.all_to_all(mixed, 'seq', 0, 0).reshape(heads, width, width)  15.8 us
    psum x1, blocking collectives, body(): total_sq = lax.psum(sums, 'heads')  13 us
    all_to_all x1, starting transfers between devices, body(): state_in = lax.all_to_all(mixed, 'seq', 0, 0).reshape(heads, width, width)  9.27 us
    all_to_all x1, starting transfers between devices, body(): sent = lax.all_to_all(jnp.concatenate([chunks, info], axis=1), 'seq', 0, 0)  8.49 us
  transfers between devices with their start and end apart: 3, of which 2 were waited for; matrix products, arithmetic and copies ran while one was open for 18% of the time, Pallas kernels for 0%

profile of v14, /device:TPU:228, one launch (start us, length us, event | category | flops | bytes accessed | tf_op | source)
XLA Modules:
  0.0 140.4 jit_solution(1248027023292727824)
XLA Ops:
  7.2 0.0 copy-start
  7.2 0.0 all-gather.2.cloned.1.call-start
  7.2 1.6 %pad_maximum_fusion.1 = bf16[256,256]{1,0:T(8,128)(2,1)} fusion(bf16[256,128]{1,0:T(8,128)(2,1)} %param.16, bf16[256,128]{1,0:T(8,128)(2,1)} %param.15), kind=kLoop, calls=%fused_computation.36 | loop fusion | flops 262144 | bytes 262144 | tf_op jit(solution)/shard_map/concatenate | solution.py:150
  8.8 0.0 all-gather.2.cloned.1.call-update
  8.8 0.7 convert_element_type.86
  9.5 0.6 slice.36
  10.1 2.0 %fusion.46 = s32[]{:T(128)} fusion(f32[]{:T(128)} %bitcast.2, s32[256]{0:T(256)} %param.17), kind=kLoop, calls=%fused_computation.68 | loop fusion | flops 1023 | bytes 1032 | tf_op jit(solution)/shard_map/reduce_sum | solution.py:175
  12.7 1.2 copy.42
  14.6 0.6 compare_select_fusion.1
  15.3 0.7 multiply_multiply_fusion
  15.9 1.3 compare_convert_fusion.1
  17.3 0.1 exponential_multiply_fusion
  17.3 1.4 convolution_add_fusion
  18.7 0.9 pad_maximum_fusion
  19.6 8.5 %all-to-all-start = ((f32[32,40,128]{2,1,0:T(8,128)}), f32[32,40,128]{2,1,0:T(8,128)S(1)}, u32[]{:S(2)}, u32[]{:S(2)}) async-start(f32[32,40,128]{2,1,0:T(8,128)} %pad_maximum_fusion), calls=%async_computation | async-start | bytes 1310720 | tf_op jit(solution)/shard_map/all_to_all | solution.py:181
  28.2 0.0 copy-done.3
  28.2 0.6 dynamic_slice.17
  29.4 0.2 convert_reduce_fusion
  29.6 0.1 fusion.26
  29.8 0.1 subtract_maximum_fusion
  29.9 17.8 %all-to-all-done = f32[32,40,128]{2,1,0:T(8,128)S(1)} async-done(((f32[32,40,128]{2,1,0:T(8,128)}), f32[32,40,128]{2,1,0:T(8,128)S(1)}, u32[]{:S(2)}, u32[]{:S(2)}) %all-to-all-start) | async-done | bytes 655392 | tf_op jit(solution)/shard_map/all_to_all | solution.py:181
  47.7 0.5 slice.46
  48.2 0.3 slice_reduce_fusion.2
  48.5 0.7 compare_select_fusion.2
  49.2 0.6 dynamic_slice.16
  49.8 0.6 slice_reduce_fusion
  50.4 1.2 fusion.49
  52.2 0.0 copy-done.1
  52.3 0.6 add_select_fusion
  52.9 0.6 fusion.55
  56.8 0.1 slice.49
  56.9 0.9 fusion.16
  57.8 0.0 copy-start.4
  57.8 1.1 copy.35
  58.9 9.3 %all-to-all-start.1 = ((f32[32,32,128]{2,1,0:T(8,128)}), f32[32,32,128]{2,1,0:T(8,128)S(1)}, u32[]{:S(2)}, u32[]{:S(2)}) async-start(f32[32,32,128]{2,1,0:T(8,128)} %copy.35), calls=%async_computation.1 | async-start | bytes 1048576 | tf_op jit(solution)/shard_map/all_to_all | solution.py:193
  68.2 0.8 copy.39.refs_4_
  69.0 0.6 stack.23.refs_0_
  69.6 0.6 fusion.54
  70.2 0.1 fusion.43
  70.3 0.0 copy-done
  70.3 0.6 fusion.5
  70.9 1.8 %fusion.2 = f32[256,8,128]{0,2,1:T(8,128)} fusion(f32[256,8,128]{0,2,1:T(8,128)S(1)} %fusion.5, bf16[256,8,128]{0,2,1:T(8,128)(2,1)S(1)} %bitcast.71, f32[256,256]{1,0:T(8,128)S(1)} %subtract_maximum_fusion, f32[8]{0:T(128)S(1)} %get-tuple-element.46, pred[256,256]{1,0:T(8,128)(4,1)S(1)} %fusion.26, bf16[256,1024]{1,0:T(8,128)(2,1)S(1)} %copy-done, ...), kind=kOutput, calls=%fused_computation.3 | convolution fusion | flops 270794752 | bytes 3997728 | tf_op jit(solution)/shard_map/while/body/eval_jaxpr/hts,shd->thd/dot_general | solution.py:129
  72.7 15.8 %all-to-all-done.1 = f32[32,32,128]{2,1,0:T(8,128)S(1)} async-done(((f32[32,32,128]{2,1,0:T(8,128)}), f32[32,32,128]{2,1,0:T(8,128)S(1)}, u32[]{:S(2)}, u32[]{:S(2)}) %all-to-all-start.1) | async-done | bytes 524320 | tf_op jit(solution)/shard_map/all_to_all | solution.py:193
  88.5 2.0 %multiply_reduce_fusion = (f32[256]{0:T(256)S(1)}, f32[256,8,128]{0,2,1:T(8,128)S(1)}) fusion(f32[256,8,128]{0,2,1:T(8,128)} %fusion.2, f32[8,128,128]{2,1,0:T(8,128)S(1)} %bitcast.69, f32[256,8]{0,1:T(8,128)S(1)} %get-tuple-element.39, bf16[256,1024]{1,0:T(8,128)(2,1)S(1)} %copy-done), kind=kOutput, calls=%fused_computation.11 | convolution fusion | flops 403701504 | bytes 3154944 | tf_op jit(solution)/shard_map/thd,hde->the/dot_general | solution.py:205
  90.4 0.3 copy.38
  90.8 13.0 %psum.7 = f32[256]{0:T(256)S(1)} all-reduce(f32[256]{0:T(256)S(1)} %get-tuple-element.47), channel_id=1, replica_groups=mesh['seq'=32,'heads'=8] {'heads'}, use_global_device_ids=true, to_apply=%region_2.3 | all-reduce | flops 256 | bytes 2048 | tf_op jit(solution)/shard_map/psum | solution.py:210
  103.8 1.0 multiply_convert_fusion
  104.7 28.9 %shard_map.104 = bf16[256,1024]{1,0:T(8,128)(2,1)} custom-call(s32[5]{0:T(128)} %stack.23.refs_0_, bf16[256,1024]{1,0:T(8,128)(2,1)} %refs_1_.1, bf16[8192,256]{1,0:T(8,128)(2,1)} %all-gather.2.cloned.1.call-done.refs_2_.refs_3_, bf16[8192,256]{1,0:T(8,128)(2,1)} %all-gather.2.cloned.1.call-done.refs_2_.refs_3_, s32[256,1]{1,0:T(8,128)} %copy.39.refs_4_), custom_call_target="tpu_custom_call" | custom-call | flops 4294967296 | bytes 5242880 | tf_op jit(solution)/shard_map/pallas_call | solution.py:89
  (12 shorter events, 0.0 us)
Async XLA Ops:
  7.2 63.1 %copy-start = (bf16[256,1024]{1,0:T(8,128)(2,1)S(1)}, bf16[256,1024]{1,0:T(8,128)(2,1)}, u32[]{:S(2)}) copy-start(bf16[256,1024]{1,0:T(8,128)(2,1)} %param.9) | copy-start | bytes 1572868
  7.2 97.5 %all-gather.2.cloned.1.call-start = ((), (), s32[]{:S(2)}) async-start(), calls=%async_computation.2 | async-start | bytes 4325376 | tf_op jit(solution)/shard_map/all_gather | solution.py:152
  17.3 10.8 %copy-start.3 = (f32[8]{0:T(128)S(1)}, f32[8]{0:T(128)}, u32[]{:S(2)}) copy-start(f32[8]{0:T(128)} %param.12) | copy-start | bytes 100
  17.3 34.9 %copy-start.1 = (s32[256]{0:T(256)S(1)}, s32[256]{0:T(256)}, u32[]{:S(2)}) copy-start(s32[256]{0:T(256)} %param.17) | copy-start | bytes 3076
  19.6 28.0 %all-to-all-start = ((f32[32,40,128]{2,1,0:T(8,128)}), f32[32,40,128]{2,1,0:T(8,128)S(1)}, u32[]{:S(2)}, u32[]{:S(2)}) async-start(f32[32,40,128]{2,1,0:T(8,128)} %pad_maximum_fusion), calls=%async_computation | async-start | bytes 1310720 | tf_op jit(solution)/shard_map/all_to_all | solution.py:181
  57.8 13.1 %copy-start.4 = (bf16[256,1024]{1,0:T(8,128)(2,1)S(1)}, bf16[256,1024]{1,0:T(8,128)(2,1)}, u32[]{:S(2)}) copy-start(bf16[256,1024]{1,0:T(8,128)(2,1)} %param.11) | copy-start | bytes 1572868
  58.9 29.6 %all-to-all-start.1 = ((f32[32,32,128]{2,1,0:T(8,128)}), f32[32,32,128]{2,1,0:T(8,128)S(1)}, u32[]{:S(2)}, u32[]{:S(2)}) async-start(f32[32,32,128]{2,1,0:T(8,128)} %copy.35), calls=%async_computation.1 | async-start | bytes 1048576 | tf_op jit(solution)/shard_map/all_to_all | solution.py:193
  88.5 15.3 %copy-start.2 = (f32[1024]{0:T(1024)S(1)}, f32[1024]{0:T(1024)}, u32[]{:S(2)}) copy-start(f32[1024]{0:T(1024)} %param.13) | copy-start | bytes 12292
Sparse Core Ops, SparseCore 0:
  10.6 90.4 all-gather.1

commit v15 on v14

--- a/solution.py
+++ b/solution.py
@@ -9,13 +9,15 @@
 
 BLOCK = 256
 KEY_BLOCK = 1024
-
-
-def flash_body(sref, q_ref, k_ref, v_ref, st_ref, o_ref, m_ref, l_ref, acc_ref, vx_ref, *, heads, width, scale):
+HEAD_PACK = 2
+
+
+def flash_body(sref, q_ref, k_ref, v_ref, st_ref, o_ref, qs_ref, m_ref, l_ref, acc_ref, vx_ref, *, heads, width, scale, pack):
     j = pl.program_id(0)
     lo, hi, flo, fhi, q0 = sref[0], sref[1], sref[2], sref[3], sref[4]
     rows = q_ref.shape[0]
     kb = k_ref.shape[0]
+    sets = heads // pack
 
     @pl.when(j == 0)
     def _():
@@ -23,28 +25,31 @@
         l_ref[...] = jnp.zeros(l_ref.shape, jnp.float32)
         acc_ref[...] = jnp.zeros(acc_ref.shape, jnp.float32)
         vx_ref[:, width:] = jnp.ones((vx_ref.shape[0], width), vx_ref.dtype)
+        for g in range(sets):
+            for i in range(pack):
+                h = g * pack + i
+                qs_ref[g, i * rows:(i + 1) * rows, :] = q_ref[:, h * width:(h + 1) * width]
 
     def step(masked):
         kt = k_ref[...].T
         vx_ref[:, :width] = v_ref[...]
         vx = vx_ref[...]
         if masked:
-            kpos = j * kb + lax.broadcasted_iota(jnp.int32, (rows, kb), 1)
-            qpos = q0 + lax.broadcasted_iota(jnp.int32, (rows, kb), 0)
+            kpos = j * kb + lax.broadcasted_iota(jnp.int32, (pack * rows, kb), 1)
+            qpos = q0 + lax.rem(lax.broadcasted_iota(jnp.int32, (pack * rows, kb), 0), rows)
             valid = (kpos <= qpos) & (kpos >= st_ref[...])
-        for h in range(heads):
-            q = q_ref[:, h * width:(h + 1) * width]
-            s = jnp.dot(q, kt, preferred_element_type=jnp.float32) * scale
+        for g in range(sets):
+            s = jnp.dot(qs_ref[g], kt, preferred_element_type=jnp.float32) * scale
             if masked:
                 s = jnp.where(valid, s, -jnp.inf)
-            m_prev = m_ref[h]
+            m_prev = m_ref[g]
             m_new = jnp.maximum(m_prev, jnp.max(s, axis=1, keepdims=True))
             corr = jnp.exp2(m_prev - m_new)
             p = jnp.exp2(s - m_new)
             pv = jnp.dot(p.astype(jnp.bfloat16), vx, preferred_element_type=jnp.float32)
-            l_ref[h] = l_ref[h] * corr + pv[:, width:width + 1]
-            acc_ref[h] = acc_ref[h] * corr + pv[:, :width]
-            m_ref[h] = m_new
+            l_ref[g] = l_ref[g] * corr + pv[:, width:width + 1]
+            acc_ref[g] = acc_ref[g] * corr + pv[:, :width]
+            m_ref[g] = m_new
 
     inside = (j >= lo) & (j <= hi)
     full = (j >= flo) & (j <= fhi)
@@ -59,8 +64,13 @@
 
     @pl.when(j == pl.num_programs(0) - 1)
     def _():
-        for h in range(heads):
-            o_ref[:, h * width:(h + 1) * width] = (acc_ref[h] / l_ref[h]).astype(o_ref.dtype)
+        for g in range(sets):
+            for i in range(pack):
+                h = g * pack + i
+                part = slice(i * rows, (i + 1) * rows)
+                o_ref[:, h * width:(h + 1) * width] = (
+                    acc_ref[g, part, :] / l_ref[g, part, :]
+                ).astype(o_ref.dtype)
 
 
 def flash_attention(q, both, starts, q0):
@@ -85,7 +95,8 @@
     def v_map(j, s):
         return (jnp.minimum(jnp.maximum(j, s[0]), s[1]), 1)
 
-    kernel = lambda *refs: flash_body(*refs, heads=heads, width=width, scale=scale)
+    pack = HEAD_PACK if heads % HEAD_PACK == 0 else 1
+    kernel = lambda *refs: flash_body(*refs, heads=heads, width=width, scale=scale, pack=pack)
     return pl.pallas_call(
         kernel,
         out_shape=jax.ShapeDtypeStruct((rows, total), jnp.bfloat16),
@@ -96,13 +107,14 @@
                 pl.BlockSpec((rows, total), lambda j, s: (0, 0)),
                 pl.BlockSpec((kb, width), k_map),
                 pl.BlockSpec((kb, width), v_map),
-                pl.BlockSpec((rows, 1), lambda j, s: (0, 0)),
+                pl.BlockSpec((pack * rows, 1), lambda j, s: (0, 0)),
             ],
             out_specs=pl.BlockSpec((rows, total), lambda j, s: (0, 0)),
             scratch_shapes=[
-                pltpu.VMEM((heads, rows, 1), jnp.float32),
-                pltpu.VMEM((heads, rows, 1), jnp.float32),
-                pltpu.VMEM((heads, rows, width), jnp.float32),
+                pltpu.VMEM((heads // pack, pack * rows, width), q.dtype),
+                pltpu.VMEM((heads // pack, pack * rows, 1), jnp.float32),
+                pltpu.VMEM((heads // pack, pack * rows, 1), jnp.float32),
+                pltpu.VMEM((heads // pack, pack * rows, width), jnp.float32),
                 pltpu.VMEM((kb, 2 * width), jnp.bfloat16),
             ],
         ),
@@ -112,7 +124,7 @@
             transcendentals=rows * heads * length // 2,
             bytes_accessed=2 * length * width * 2 + 2 * rows * total * 2,
         ),
-    )(sref, q, both, both, starts.reshape(rows, 1))
+    )(sref, q, both, both, jnp.tile(starts, pack).reshape(pack * rows, 1))
 
 
 def light_block(carry, inputs, rates):

time: 141 us -> 145 us (1.028)
  the two profiles are of different devices: /device:TPU:228 before, /device:TPU:194 now
where the time goes in v15:
time: 145 us; the launch traced here: 144 us
  waiting for transfers between devices  32.4 us (22%)
  Pallas kernels  32 us (22%)
  between operations  20.2 us (14%)
  starting transfers between devices  18.4 us (13%)
  blocking collectives  14.1 us (10%)
  other arithmetic  12.5 us (9%)
  local copies, waits for them, and re-layouts  8.07 us (6%)
  matrix products  6.6 us (5%)
    pallas_call x1, Pallas kernels, flash_attention(): pl.pallas_call(kernel, out_shape=jax.ShapeDtypeStruct((rows, total), jnp....  32 us
    all_to_all x1, waiting for transfers between devices, body(): sent = lax.all_to_all(jnp.concatenate([chunks, info], axis=1), 'seq', 0, 0)  17.6 us
    all_to_all x1, waiting for transfers between devices, body(): state_in = lax.all_to_all(mixed, 'seq', 0, 0).reshape(heads, width, width)  14.8 us
    psum x1, blocking collectives, body(): total_sq = lax.psum(sums, 'heads')  14.1 us
    all_to_all x1, starting transfers between devices, body(): state_in = lax.all_to_all(mixed, 'seq', 0, 0).reshape(heads, width, width)  9.38 us
    all_to_all x1, starting transfers between devices, body(): sent = lax.all_to_all(jnp.concatenate([chunks, info], axis=1), 'seq', 0, 0)  8.94 us
  transfers between devices with their start and end apart: 3, of which 2 were waited for; matrix products, arithmetic and copies ran while one was open for 18% of the time, Pallas kernels for 0%

profile of v15, /device:TPU:194, one launch (start us, length us, event | category | flops | bytes accessed | tf_op | source)
XLA Modules:
  0.0 144.3 jit_solution(9825771059924683906)
XLA Ops:
  7.2 0.0 copy-start
  7.2 0.0 all-gather.2.cloned.1.call-start
  7.2 1.6 %pad_maximum_fusion.1 = bf16[256,256]{1,0:T(8,128)(2,1)} fusion(bf16[256,128]{1,0:T(8,128)(2,1)} %param.16, bf16[256,128]{1,0:T(8,128)(2,1)} %param.15), kind=kLoop, calls=%fused_computation.36 | loop fusion | flops 262144 | bytes 262144 | tf_op jit(solution)/shard_map/concatenate | solution.py:162
  8.8 0.0 all-gather.2.cloned.1.call-update
  8.9 0.7 convert_element_type.86
  9.5 0.6 slice.36
  10.1 2.0 %fusion.46 = s32[]{:T(128)} fusion(f32[]{:T(128)} %bitcast.2, s32[256]{0:T(256)} %param.17), kind=kLoop, calls=%fused_computation.68 | loop fusion | flops 1023 | bytes 1032 | tf_op jit(solution)/shard_map/reduce_sum | solution.py:187
  12.7 1.2 copy.42
  14.6 0.6 compare_select_fusion.1
  15.3 0.7 multiply_multiply_fusion
  16.0 1.3 compare_convert_fusion.1
  17.3 0.1 exponential_multiply_fusion
  17.4 1.4 convolution_add_fusion
  18.8 0.9 pad_maximum_fusion
  19.7 8.9 %all-to-all-start = ((f32[32,40,128]{2,1,0:T(8,128)}), f32[32,40,128]{2,1,0:T(8,128)S(1)}, u32[]{:S(2)}, u32[]{:S(2)}) async-start(f32[32,40,128]{2,1,0:T(8,128)} %pad_maximum_fusion), calls=%async_computation | async-start | bytes 1310720 | tf_op jit(solution)/shard_map/all_to_all | solution.py:193
  28.6 0.0 copy-done.3
  28.6 0.6 dynamic_slice.17
  29.9 0.2 convert_reduce_fusion
  30.1 0.1 fusion.26
  30.2 0.1 subtract_maximum_fusion
  30.4 17.6 %all-to-all-done = f32[32,40,128]{2,1,0:T(8,128)S(1)} async-done(((f32[32,40,128]{2,1,0:T(8,128)}), f32[32,40,128]{2,1,0:T(8,128)S(1)}, u32[]{:S(2)}, u32[]{:S(2)}) %all-to-all-start) | async-done | bytes 655392 | tf_op jit(solution)/shard_map/all_to_all | solution.py:193
  47.9 0.5 slice.46
  48.5 0.3 slice_reduce_fusion.2
  48.8 0.7 compare_select_fusion.2
  49.5 0.6 dynamic_slice.16
  50.1 0.6 slice_reduce_fusion
  50.7 1.2 fusion.49
  52.5 0.0 copy-done.1
  52.5 0.6 add_select_fusion
  53.2 0.6 fusion.55
  57.1 0.1 slice.49
  57.2 0.9 fusion.16
  58.0 0.0 copy-start.4
  58.1 1.1 copy.35
  59.2 9.4 %all-to-all-start.1 = ((f32[32,32,128]{2,1,0:T(8,128)}), f32[32,32,128]{2,1,0:T(8,128)S(1)}, u32[]{:S(2)}, u32[]{:S(2)}) async-start(f32[32,32,128]{2,1,0:T(8,128)} %copy.35), calls=%async_computation.1 | async-start | bytes 1048576 | tf_op jit(solution)/shard_map/all_to_all | solution.py:205
  68.6 0.9 copy.46
  69.5 0.7 stack.23.refs_0_
  70.2 0.6 fusion.54
  70.8 0.1 fusion.43
  70.9 0.6 fusion.5
  71.5 1.8 %fusion.2 = f32[256,8,128]{0,2,1:T(8,128)} fusion(f32[256,8,128]{0,2,1:T(8,128)S(1)} %fusion.5, bf16[256,8,128]{0,2,1:T(8,128)(2,1)S(1)} %bitcast.75, f32[256,256]{1,0:T(8,128)S(1)} %subtract_maximum_fusion, f32[8]{0:T(128)S(1)} %get-tuple-element.46, pred[256,256]{1,0:T(8,128)(4,1)S(1)} %fusion.26, bf16[256,1024]{1,0:T(8,128)(2,1)S(1)} %copy-done, ...), kind=kOutput, calls=%fused_computation.3 | convolution fusion | flops 270794752 | bytes 3997728 | tf_op jit(solution)/shard_map/while/body/eval_jaxpr/hts,shd->thd/dot_general | solution.py:141
  73.3 14.8 %all-to-all-done.1 = f32[32,32,128]{2,1,0:T(8,128)S(1)} async-done(((f32[32,32,128]{2,1,0:T(8,128)}), f32[32,32,128]{2,1,0:T(8,128)S(1)}, u32[]{:S(2)}, u32[]{:S(2)}) %all-to-all-start.1) | async-done | bytes 524320 | tf_op jit(solution)/shard_map/all_to_all | solution.py:205
  88.1 2.0 %multiply_reduce_fusion = (f32[256]{0:T(256)S(1)}, f32[256,8,128]{0,2,1:T(8,128)S(1)}) fusion(f32[256,8,128]{0,2,1:T(8,128)} %fusion.2, f32[8,128,128]{2,1,0:T(8,128)S(1)} %bitcast.73, f32[256,8]{0,1:T(8,128)S(1)} %get-tuple-element.39, bf16[256,1024]{1,0:T(8,128)(2,1)S(1)} %copy-done), kind=kOutput, calls=%fused_computation.11 | convolution fusion | flops 403701504 | bytes 3154944 | tf_op jit(solution)/shard_map/thd,hde->the/dot_general | solution.py:217
  90.1 0.3 copy.38
  90.4 14.1 %psum.7 = f32[256]{0:T(256)S(1)} all-reduce(f32[256]{0:T(256)S(1)} %get-tuple-element.47), channel_id=1, replica_groups=mesh['seq'=32,'heads'=8] {'heads'}, use_global_device_ids=true, to_apply=%region_2.3 | all-reduce | flops 256 | bytes 2048 | tf_op jit(solution)/shard_map/psum | solution.py:222
  104.5 0.0 copy-done.2
  104.5 1.0 multiply_convert_fusion
  105.4 32.0 %shard_map.104 = bf16[256,1024]{1,0:T(8,128)(2,1)} custom-call(s32[5]{0:T(128)} %stack.23.refs_0_, bf16[256,1024]{1,0:T(8,128)(2,1)} %refs_1_.1, bf16[8192,256]{1,0:T(8,128)(2,1)} %all-gather.2.cloned.1.call-done.refs_2_.refs_3_, bf16[8192,256]{1,0:T(8,128)(2,1)} %all-gather.2.cloned.1.call-done.refs_2_.refs_3_, s32[512,1]{1,0:T(8,128)} %bitcast.77), custom_call_target="tpu_custom_call" | custom-call | flops 4294967296 | bytes 5242880 | tf_op jit(solution)/shard_map/pallas_call | solution.py:100
  (14 shorter events, 0.1 us)
Async XLA Ops:
  7.2 63.7 %copy-start = (bf16[256,1024]{1,0:T(8,128)(2,1)S(1)}, bf16[256,1024]{1,0:T(8,128)(2,1)}, u32[]{:S(2)}) copy-start(bf16[256,1024]{1,0:T(8,128)(2,1)} %param.9) | copy-start | bytes 1572868
  7.2 98.3 %all-gather.2.cloned.1.call-start = ((), (), s32[]{:S(2)}) async-start(), calls=%async_computation.2 | async-start | bytes 4325376 | tf_op jit(solution)/shard_map/all_gather | solution.py:164
  17.4 11.3 %copy-start.3 = (f32[8]{0:T(128)S(1)}, f32[8]{0:T(128)}, u32[]{:S(2)}) copy-start(f32[8]{0:T(128)} %param.12) | copy-start | bytes 100
  17.4 35.2 %copy-start.1 = (s32[256]{0:T(256)S(1)}, s32[256]{0:T(256)}, u32[]{:S(2)}) copy-start(s32[256]{0:T(256)} %param.17) | copy-start | bytes 3076
  19.7 28.3 %all-to-all-start = ((f32[32,40,128]{2,1,0:T(8,128)}), f32[32,40,128]{2,1,0:T(8,128)S(1)}, u32[]{:S(2)}, u32[]{:S(2)}) async-start(f32[32,40,128]{2,1,0:T(8,128)} %pad_maximum_fusion), calls=%async_computation | async-start | bytes 1310720 | tf_op jit(solution)/shard_map/all_to_all | solution.py:193
  58.0 13.4 %copy-start.4 = (bf16[256,1024]{1,0:T(8,128)(2,1)S(1)}, bf16[256,1024]{1,0:T(8,128)(2,1)}, u32[]{:S(2)}) copy-start(bf16[256,1024]{1,0:T(8,128)(2,1)} %param.11) | copy-start | bytes 1572868
  59.2 28.9 %all-to-all-start.1 = ((f32[32,32,128]{2,1,0:T(8,128)}), f32[32,32,128]{2,1,0:T(8,128)S(1)}, u32[]{:S(2)}, u32[]{:S(2)}) async-start(f32[32,32,128]{2,1,0:T(8,128)} %copy.35), calls=%async_computation.1 | async-start | bytes 1048576 | tf_op jit(solution)/shard_map/all_to_all | solution.py:205
  88.1 16.4 %copy-start.2 = (f32[1024]{0:T(1024)S(1)}, f32[1024]{0:T(1024)}, u32[]{:S(2)}) copy-start(f32[1024]{0:T(1024)} %param.13) | copy-start | bytes 12292
Sparse Core Ops, SparseCore 0:
  10.6 90.3 all-gather.1

commit v16 on v14

--- a/solution.py
+++ b/solution.py
@@ -9,6 +9,7 @@
 
 BLOCK = 256
 KEY_BLOCK = 1024
+SUB_BLOCK = 512
 
 
 def flash_body(sref, q_ref, k_ref, v_ref, st_ref, o_ref, m_ref, l_ref, acc_ref, vx_ref, *, heads, width, scale):
@@ -32,19 +33,22 @@
             kpos = j * kb + lax.broadcasted_iota(jnp.int32, (rows, kb), 1)
             qpos = q0 + lax.broadcasted_iota(jnp.int32, (rows, kb), 0)
             valid = (kpos <= qpos) & (kpos >= st_ref[...])
+        sub = min(SUB_BLOCK, kb)
         for h in range(heads):
             q = q_ref[:, h * width:(h + 1) * width]
-            s = jnp.dot(q, kt, preferred_element_type=jnp.float32) * scale
-            if masked:
-                s = jnp.where(valid, s, -jnp.inf)
-            m_prev = m_ref[h]
-            m_new = jnp.maximum(m_prev, jnp.max(s, axis=1, keepdims=True))
-            corr = jnp.exp2(m_prev - m_new)
-            p = jnp.exp2(s - m_new)
-            pv = jnp.dot(p.astype(jnp.bfloat16), vx, preferred_element_type=jnp.float32)
-            l_ref[h] = l_ref[h] * corr + pv[:, width:width + 1]
-            acc_ref[h] = acc_ref[h] * corr + pv[:, :width]
-            m_ref[h] = m_new
+            for c in range(kb // sub):
+                cols = slice(c * sub, (c + 1) * sub)
+                s = jnp.dot(q, kt[:, cols], preferred_element_type=jnp.float32) * scale
+                if masked:
+                    s = jnp.where(valid[:, cols], s, -jnp.inf)
+                m_prev = m_ref[h]
+                m_new = jnp.maximum(m_prev, jnp.max(s, axis=1, keepdims=True))
+                corr = jnp.exp2(m_prev - m_new)
+                p = jnp.exp2(s - m_new)
+                pv = jnp.dot(p.astype(jnp.bfloat16), vx[cols, :], preferred_element_type=jnp.float32)
+                l_ref[h] = l_ref[h] * corr + pv[:, width:width + 1]
+                acc_ref[h] = acc_ref[h] * corr + pv[:, :width]
+                m_ref[h] = m_new
 
     inside = (j >= lo) & (j <= hi)
     full = (j >= flo) & (j <= fhi)

time: 141 us -> 143 us (1.014)
  the two profiles are of different devices: /device:TPU:228 before, /device:TPU:166 now
where the time goes in v16:
time: 143 us; the launch traced here: 141 us
  waiting for transfers between devices  31.3 us (22%)
  Pallas kernels  30.4 us (21%)
  between operations  20.2 us (14%)
  starting transfers between devices  19.1 us (13%)
  blocking collectives  13.1 us (9%)
  other arithmetic  12.5 us (9%)
  local copies, waits for them, and re-layouts  7.89 us (6%)
  matrix products  6.62 us (5%)
    pallas_call x1, Pallas kernels, flash_attention(): pl.pallas_call(kernel, out_shape=jax.ShapeDtypeStruct((rows, total), jnp....  30.4 us
    all_to_all x1, waiting for transfers between devices, body(): sent = lax.all_to_all(jnp.concatenate([chunks, info], axis=1), 'seq', 0, 0)  17.3 us
    all_to_all x1, waiting for transfers between devices, body(): state_in = lax.all_to_all(mixed, 'seq', 0, 0).reshape(heads, width, width)  13.9 us
    psum x1, blocking collectives, body(): total_sq = lax.psum(sums, 'heads')  13.1 us
    all_to_all x1, starting transfers between devices, body(): state_in = lax.all_to_all(mixed, 'seq', 0, 0).reshape(heads, width, width)  9.74 us
    all_to_all x1, starting transfers between devices, body(): sent = lax.all_to_all(jnp.concatenate([chunks, info], axis=1), 'seq', 0, 0)  9.32 us
  transfers between devices with their start and end apart: 3, of which 2 were waited for; matrix products, arithmetic and copies ran while one was open for 18% of the time, Pallas kernels for 0%

profile of v16, /device:TPU:166, one launch (start us, length us, event | category | flops | bytes accessed | tf_op | source)
XLA Modules:
  0.0 141.0 jit_solution(17314453939158411784)
XLA Ops:
  7.2 0.0 copy-start
  7.2 0.0 all-gather.2.cloned.1.call-start
  7.2 1.6 %pad_maximum_fusion.1 = bf16[256,256]{1,0:T(8,128)(2,1)} fusion(bf16[256,128]{1,0:T(8,128)(2,1)} %param.16, bf16[256,128]{1,0:T(8,128)(2,1)} %param.15), kind=kLoop, calls=%fused_computation.36 | loop fusion | flops 262144 | bytes 262144 | tf_op jit(solution)/shard_map/concatenate | solution.py:154
  8.8 0.0 all-gather.2.cloned.1.call-update
  8.8 0.7 convert_element_type.86
  9.5 0.6 slice.36
  10.1 2.0 %fusion.46 = s32[]{:T(128)} fusion(f32[]{:T(128)} %bitcast.2, s32[256]{0:T(256)} %param.17), kind=kLoop, calls=%fused_computation.68 | loop fusion | flops 1023 | bytes 1032 | tf_op jit(solution)/shard_map/reduce_sum | solution.py:179
  12.7 1.2 copy.42
  14.6 0.6 compare_select_fusion.1
  15.3 0.7 multiply_multiply_fusion
  15.9 1.3 compare_convert_fusion.1
  17.3 0.1 exponential_multiply_fusion
  17.3 1.4 convolution_add_fusion
  18.7 0.9 pad_maximum_fusion
  19.6 9.3 %all-to-all-start = ((f32[32,40,128]{2,1,0:T(8,128)}), f32[32,40,128]{2,1,0:T(8,128)S(1)}, u32[]{:S(2)}, u32[]{:S(2)}) async-start(f32[32,40,128]{2,1,0:T(8,128)} %pad_maximum_fusion), calls=%async_computation | async-start | bytes 1310720 | tf_op jit(solution)/shard_map/all_to_all | solution.py:185
  29.0 0.0 copy-done.3
  29.0 0.6 dynamic_slice.17
  30.3 0.2 convert_reduce_fusion
  30.4 0.1 fusion.26
  30.6 0.1 subtract_maximum_fusion
  30.7 17.3 %all-to-all-done = f32[32,40,128]{2,1,0:T(8,128)S(1)} async-done(((f32[32,40,128]{2,1,0:T(8,128)}), f32[32,40,128]{2,1,0:T(8,128)S(1)}, u32[]{:S(2)}, u32[]{:S(2)}) %all-to-all-start) | async-done | bytes 655392 | tf_op jit(solution)/shard_map/all_to_all | solution.py:185
  48.0 0.5 slice.46
  48.5 0.3 slice_reduce_fusion.2
  48.9 0.7 compare_select_fusion.2
  49.6 0.6 dynamic_slice.16
  50.2 0.6 slice_reduce_fusion
  50.7 1.2 fusion.49
  52.6 0.0 copy-done.1
  52.6 0.6 add_select_fusion
  53.2 0.6 fusion.55
  57.2 0.1 slice.49
  57.2 0.9 fusion.16
  58.1 0.0 copy-start.4
  58.1 1.1 copy.35
  59.2 9.7 %all-to-all-start.1 = ((f32[32,32,128]{2,1,0:T(8,128)}), f32[32,32,128]{2,1,0:T(8,128)S(1)}, u32[]{:S(2)}, u32[]{:S(2)}) async-start(f32[32,32,128]{2,1,0:T(8,128)} %copy.35), calls=%async_computation.1 | async-start | bytes 1048576 | tf_op jit(solution)/shard_map/all_to_all | solution.py:197
  69.0 0.8 copy.39.refs_4_
  69.8 0.6 stack.23.refs_0_
  70.4 0.6 fusion.54
  71.0 0.1 fusion.43
  71.1 0.0 copy-done
  71.1 0.6 fusion.5
  71.7 1.8 %fusion.2 = f32[256,8,128]{0,2,1:T(8,128)} fusion(f32[256,8,128]{0,2,1:T(8,128)S(1)} %fusion.5, bf16[256,8,128]{0,2,1:T(8,128)(2,1)S(1)} %bitcast.71, f32[256,256]{1,0:T(8,128)S(1)} %subtract_maximum_fusion, f32[8]{0:T(128)S(1)} %get-tuple-element.46, pred[256,256]{1,0:T(8,128)(4,1)S(1)} %fusion.26, bf16[256,1024]{1,0:T(8,128)(2,1)S(1)} %copy-done, ...), kind=kOutput, calls=%fused_computation.3 | convolution fusion | flops 270794752 | bytes 3997728 | tf_op jit(solution)/shard_map/while/body/eval_jaxpr/hts,shd->thd/dot_general | solution.py:133
  73.5 13.9 %all-to-all-done.1 = f32[32,32,128]{2,1,0:T(8,128)S(1)} async-done(((f32[32,32,128]{2,1,0:T(8,128)}), f32[32,32,128]{2,1,0:T(8,128)S(1)}, u32[]{:S(2)}, u32[]{:S(2)}) %all-to-all-start.1) | async-done | bytes 524320 | tf_op jit(solution)/shard_map/all_to_all | solution.py:197
  87.5 2.0 %multiply_reduce_fusion = (f32[256]{0:T(256)S(1)}, f32[256,8,128]{0,2,1:T(8,128)S(1)}) fusion(f32[256,8,128]{0,2,1:T(8,128)} %fusion.2, f32[8,128,128]{2,1,0:T(8,128)S(1)} %bitcast.69, f32[256,8]{0,1:T(8,128)S(1)} %get-tuple-element.39, bf16[256,1024]{1,0:T(8,128)(2,1)S(1)} %copy-done), kind=kOutput, calls=%fused_computation.11 | convolution fusion | flops 403701504 | bytes 3154944 | tf_op jit(solution)/shard_map/thd,hde->the/dot_general | solution.py:209
  89.4 0.3 copy.38
  89.8 13.1 %psum.7 = f32[256]{0:T(256)S(1)} all-reduce(f32[256]{0:T(256)S(1)} %get-tuple-element.47), channel_id=1, replica_groups=mesh['seq'=32,'heads'=8] {'heads'}, use_global_device_ids=true, to_apply=%region_2.3 | all-reduce | flops 256 | bytes 2048 | tf_op jit(solution)/shard_map/psum | solution.py:214
  102.9 1.0 multiply_convert_fusion
  103.8 30.4 %shard_map.104 = bf16[256,1024]{1,0:T(8,128)(2,1)} custom-call(s32[5]{0:T(128)} %stack.23.refs_0_, bf16[256,1024]{1,0:T(8,128)(2,1)} %refs_1_.1, bf16[8192,256]{1,0:T(8,128)(2,1)} %all-gather.2.cloned.1.call-done.refs_2_.refs_3_, bf16[8192,256]{1,0:T(8,128)(2,1)} %all-gather.2.cloned.1.call-done.refs_2_.refs_3_, s32[256,1]{1,0:T(8,128)} %copy.39.refs_4_), custom_call_target="tpu_custom_call" | custom-call | flops 4294967296 | bytes 5242880 | tf_op jit(solution)/shard_map/pallas_call | solution.py:93
  (12 shorter events, 0.0 us)
Async XLA Ops:
  7.2 63.9 %copy-start = (bf16[256,1024]{1,0:T(8,128)(2,1)S(1)}, bf16[256,1024]{1,0:T(8,128)(2,1)}, u32[]{:S(2)}) copy-start(bf16[256,1024]{1,0:T(8,128)(2,1)} %param.9) | copy-start | bytes 1572868
  7.2 96.6 %all-gather.2.cloned.1.call-start = ((), (), s32[]{:S(2)}) async-start(), calls=%async_computation.2 | async-start | bytes 4325376 | tf_op jit(solution)/shard_map/all_gather | solution.py:156
  17.3 11.6 %copy-start.3 = (f32[8]{0:T(128)S(1)}, f32[8]{0:T(128)}, u32[]{:S(2)}) copy-start(f32[8]{0:T(128)} %param.12) | copy-start | bytes 100
  17.3 35.3 %copy-start.1 = (s32[256]{0:T(256)S(1)}, s32[256]{0:T(256)}, u32[]{:S(2)}) copy-start(s32[256]{0:T(256)} %param.17) | copy-start | bytes 3076
  19.6 28.4 %all-to-all-start = ((f32[32,40,128]{2,1,0:T(8,128)}), f32[32,40,128]{2,1,0:T(8,128)S(1)}, u32[]{:S(2)}, u32[]{:S(2)}) async-start(f32[32,40,128]{2,1,0:T(8,128)} %pad_maximum_fusion), calls=%async_computation | async-start | bytes 1310720 | tf_op jit(solution)/shard_map/all_to_all | solution.py:185
  58.1 13.6 %copy-start.4 = (bf16[256,1024]{1,0:T(8,128)(2,1)S(1)}, bf16[256,1024]{1,0:T(8,128)(2,1)}, u32[]{:S(2)}) copy-start(bf16[256,1024]{1,0:T(8,128)(2,1)} %param.11) | copy-start | bytes 1572868
  59.2 28.2 %all-to-all-start.1 = ((f32[32,32,128]{2,1,0:T(8,128)}), f32[32,32,128]{2,1,0:T(8,128)S(1)}, u32[]{:S(2)}, u32[]{:S(2)}) async-start(f32[32,32,128]{2,1,0:T(8,128)} %copy.35), calls=%async_computation.1 | async-start | bytes 1048576 | tf_op jit(solution)/shard_map/all_to_all | solution.py:197
  87.5 15.4 %copy-start.2 = (f32[1024]{0:T(1024)S(1)}, f32[1024]{0:T(1024)}, u32[]{:S(2)}) copy-start(f32[1024]{0:T(1024)} %param.13) | copy-start | bytes 12292
Sparse Core Ops, SparseCore 0:
  10.6 89.9 all-gather.1

commit v17 on v14

--- a/solution.py
+++ b/solution.py
@@ -30,8 +30,13 @@
         vx = vx_ref[...]
         if masked:
             kpos = j * kb + lax.broadcasted_iota(jnp.int32, (rows, kb), 1)
-            qpos = q0 + lax.broadcasted_iota(jnp.int32, (rows, kb), 0)
-            valid = (kpos <= qpos) & (kpos >= st_ref[...])
+            if masked == "causal":
+                valid = kpos <= q0 + lax.broadcasted_iota(jnp.int32, (rows, kb), 0)
+            elif masked == "start":
+                valid = kpos >= st_ref[...]
+            else:
+                qpos = q0 + lax.broadcasted_iota(jnp.int32, (rows, kb), 0)
+                valid = (kpos <= qpos) & (kpos >= st_ref[...])
         for h in range(heads):
             q = q_ref[:, h * width:(h + 1) * width]
             s = jnp.dot(q, kt, preferred_element_type=jnp.float32) * scale
@@ -53,9 +58,20 @@
     def _():
         step(False)
 
-    @pl.when(inside & jnp.logical_not(full))
-    def _():
-        step(True)
+    late = (j + 1) * kb - 1 > q0
+    early = j < flo
+
+    @pl.when(inside & jnp.logical_not(full) & late & early)
+    def _():
+        step("both")
+
+    @pl.when(inside & jnp.logical_not(full) & late & jnp.logical_not(early))
+    def _():
+        step("causal")
+
+    @pl.when(inside & jnp.logical_not(full) & jnp.logical_not(late))
+    def _():
+        step("start")
 
     @pl.when(j == pl.num_programs(0) - 1)
     def _():

time: 141 us -> 141 us (level)
  the two profiles are of different devices: /device:TPU:228 before, /device:TPU:230 now
where the time goes in v17:
time: 141 us
  waiting for transfers between devices  34.3 us (24%)
  Pallas kernels  28.9 us (20%)
  between operations  20.2 us (14%)
  starting transfers between devices  17.1 us (12%)
  blocking collectives  13.2 us (9%)
  other arithmetic  12.5 us (9%)
  local copies, waits for them, and re-layouts  7.88 us (6%)
  matrix products  6.6 us (5%)
    pallas_call x1, Pallas kernels, flash_attention(): pl.pallas_call(kernel, out_shape=jax.ShapeDtypeStruct((rows, total), jnp....  28.9 us
    all_to_all x1, waiting for transfers between devices, body(): sent = lax.all_to_all(jnp.concatenate([chunks, info], axis=1), 'seq', 0, 0)  18.4 us
    all_to_all x1, waiting for transfers between devices, body(): state_in = lax.all_to_all(mixed, 'seq', 0, 0).reshape(heads, width, width)  15.8 us
    psum x1, blocking collectives, body(): total_sq = lax.psum(sums, 'heads')  13.2 us
    all_to_all x1, starting transfers between devices, body(): state_in = lax.all_to_all(mixed, 'seq', 0, 0).reshape(heads, width, width)  8.61 us
    all_to_all x1, starting transfers between devices, body(): sent = lax.all_to_all(jnp.concatenate([chunks, info], axis=1), 'seq', 0, 0)  8.47 us
  transfers between devices with their start and end apart: 3, of which 2 were waited for; matrix products, arithmetic and copies ran while one was open for 18% of the time, Pallas kernels for 0%

profile of v17, /device:TPU:230, one launch (start us, length us, event | category | flops | bytes accessed | tf_op | source)
XLA Modules:
  0.0 140.7 jit_solution(5391309958033275872)
XLA Ops:
  7.2 0.0 copy-start
  7.2 0.0 all-gather.2.cloned.1.call-start
  7.2 1.6 %pad_maximum_fusion.1 = bf16[256,256]{1,0:T(8,128)(2,1)} fusion(bf16[256,128]{1,0:T(8,128)(2,1)} %param.16, bf16[256,128]{1,0:T(8,128)(2,1)} %param.15), kind=kLoop, calls=%fused_computation.36 | loop fusion | flops 262144 | bytes 262144 | tf_op jit(solution)/shard_map/concatenate | solution.py:166
  8.8 0.0 all-gather.2.cloned.1.call-update
  8.8 0.7 convert_element_type.86
  9.5 0.6 slice.36
  10.1 2.0 %fusion.46 = s32[]{:T(128)} fusion(f32[]{:T(128)} %bitcast.2, s32[256]{0:T(256)} %param.17), kind=kLoop, calls=%fused_computation.68 | loop fusion | flops 1023 | bytes 1032 | tf_op jit(solution)/shard_map/reduce_sum | solution.py:191
  12.7 1.2 copy.42
  14.6 0.6 compare_select_fusion.1
  15.3 0.7 multiply_multiply_fusion
  15.9 1.3 compare_convert_fusion.1
  17.3 0.1 exponential_multiply_fusion
  17.3 1.4 convolution_add_fusion
  18.7 0.9 pad_maximum_fusion
  19.6 8.5 %all-to-all-start = ((f32[32,40,128]{2,1,0:T(8,128)}), f32[32,40,128]{2,1,0:T(8,128)S(1)}, u32[]{:S(2)}, u32[]{:S(2)}) async-start(f32[32,40,128]{2,1,0:T(8,128)} %pad_maximum_fusion), calls=%async_computation | async-start | bytes 1310720 | tf_op jit(solution)/shard_map/all_to_all | solution.py:197
  28.1 0.0 copy-done.3
  28.1 0.6 dynamic_slice.17
  29.4 0.2 convert_reduce_fusion
  29.6 0.2 fusion.26
  29.8 0.1 subtract_maximum_fusion
  29.9 18.4 %all-to-all-done = f32[32,40,128]{2,1,0:T(8,128)S(1)} async-done(((f32[32,40,128]{2,1,0:T(8,128)}), f32[32,40,128]{2,1,0:T(8,128)S(1)}, u32[]{:S(2)}, u32[]{:S(2)}) %all-to-all-start) | async-done | bytes 655392 | tf_op jit(solution)/shard_map/all_to_all | solution.py:197
  48.3 0.5 slice.46
  48.8 0.3 slice_reduce_fusion.2
  49.1 0.7 compare_select_fusion.2
  49.9 0.6 dynamic_slice.16
  50.4 0.6 slice_reduce_fusion
  51.0 1.2 fusion.49
  52.9 0.0 copy-done.1
  52.9 0.6 add_select_fusion
  53.5 0.6 fusion.55
  57.5 0.1 slice.49
  57.5 0.9 fusion.16
  58.4 0.0 copy-start.4
  58.4 1.1 copy.35
  59.5 8.6 %all-to-all-start.1 = ((f32[32,32,128]{2,1,0:T(8,128)}), f32[32,32,128]{2,1,0:T(8,128)S(1)}, u32[]{:S(2)}, u32[]{:S(2)}) async-start(f32[32,32,128]{2,1,0:T(8,128)} %copy.35), calls=%async_computation.1 | async-start | bytes 1048576 | tf_op jit(solution)/shard_map/all_to_all | solution.py:209
  68.2 0.8 copy.39.refs_4_
  69.0 0.6 stack.23.refs_0_
  69.5 0.6 fusion.54
  70.2 0.1 fusion.43
  70.2 0.0 copy-done
  70.2 0.6 fusion.5
  70.9 1.8 %fusion.2 = f32[256,8,128]{0,2,1:T(8,128)} fusion(f32[256,8,128]{0,2,1:T(8,128)S(1)} %fusion.5, bf16[256,8,128]{0,2,1:T(8,128)(2,1)S(1)} %bitcast.71, f32[256,256]{1,0:T(8,128)S(1)} %subtract_maximum_fusion, f32[8]{0:T(128)S(1)} %get-tuple-element.46, pred[256,256]{1,0:T(8,128)(4,1)S(1)} %fusion.26, bf16[256,1024]{1,0:T(8,128)(2,1)S(1)} %copy-done, ...), kind=kOutput, calls=%fused_computation.3 | convolution fusion | flops 270794752 | bytes 3997728 | tf_op jit(solution)/shard_map/while/body/eval_jaxpr/hts,shd->thd/dot_general | solution.py:145
  72.7 15.8 %all-to-all-done.1 = f32[32,32,128]{2,1,0:T(8,128)S(1)} async-done(((f32[32,32,128]{2,1,0:T(8,128)}), f32[32,32,128]{2,1,0:T(8,128)S(1)}, u32[]{:S(2)}, u32[]{:S(2)}) %all-to-all-start.1) | async-done | bytes 524320 | tf_op jit(solution)/shard_map/all_to_all | solution.py:209
  88.5 2.0 %multiply_reduce_fusion = (f32[256]{0:T(256)S(1)}, f32[256,8,128]{0,2,1:T(8,128)S(1)}) fusion(f32[256,8,128]{0,2,1:T(8,128)} %fusion.2, f32[8,128,128]{2,1,0:T(8,128)S(1)} %bitcast.69, f32[256,8]{0,1:T(8,128)S(1)} %get-tuple-element.39, bf16[256,1024]{1,0:T(8,128)(2,1)S(1)} %copy-done), kind=kOutput, calls=%fused_computation.11 | convolution fusion | flops 403701504 | bytes 3154944 | tf_op jit(solution)/shard_map/thd,hde->the/dot_general | solution.py:221
  90.4 0.3 copy.38
  90.8 13.2 %psum.7 = f32[256]{0:T(256)S(1)} all-reduce(f32[256]{0:T(256)S(1)} %get-tuple-element.47), channel_id=1, replica_groups=mesh['seq'=32,'heads'=8] {'heads'}, use_global_device_ids=true, to_apply=%region_2.3 | all-reduce | flops 256 | bytes 2048 | tf_op jit(solution)/shard_map/psum | solution.py:226
  104.0 1.0 multiply_convert_fusion
  105.0 28.9 %shard_map.104 = bf16[256,1024]{1,0:T(8,128)(2,1)} custom-call(s32[5]{0:T(128)} %stack.23.refs_0_, bf16[256,1024]{1,0:T(8,128)(2,1)} %refs_1_.1, bf16[8192,256]{1,0:T(8,128)(2,1)} %all-gather.2.cloned.1.call-done.refs_2_.refs_3_, bf16[8192,256]{1,0:T(8,128)(2,1)} %all-gather.2.cloned.1.call-done.refs_2_.refs_3_, s32[256,1]{1,0:T(8,128)} %copy.39.refs_4_), custom_call_target="tpu_custom_call" | custom-call | flops 4294967296 | bytes 5242880 | tf_op jit(solution)/shard_map/pallas_call | solution.py:105
  (12 shorter events, 0.0 us)
Async XLA Ops:
  7.2 63.1 %copy-start = (bf16[256,1024]{1,0:T(8,128)(2,1)S(1)}, bf16[256,1024]{1,0:T(8,128)(2,1)}, u32[]{:S(2)}) copy-start(bf16[256,1024]{1,0:T(8,128)(2,1)} %param.9) | copy-start | bytes 1572868
  7.2 97.8 %all-gather.2.cloned.1.call-start = ((), (), s32[]{:S(2)}) async-start(), calls=%async_computation.2 | async-start | bytes 4325376 | tf_op jit(solution)/shard_map/all_gather | solution.py:168
  17.3 10.8 %copy-start.3 = (f32[8]{0:T(128)S(1)}, f32[8]{0:T(128)}, u32[]{:S(2)}) copy-start(f32[8]{0:T(128)} %param.12) | copy-start | bytes 100
  17.3 35.5 %copy-start.1 = (s32[256]{0:T(256)S(1)}, s32[256]{0:T(256)}, u32[]{:S(2)}) copy-start(s32[256]{0:T(256)} %param.17) | copy-start | bytes 3076
  19.6 28.7 %all-to-all-start = ((f32[32,40,128]{2,1,0:T(8,128)}), f32[32,40,128]{2,1,0:T(8,128)S(1)}, u32[]{:S(2)}, u32[]{:S(2)}) async-start(f32[32,40,128]{2,1,0:T(8,128)} %pad_maximum_fusion), calls=%async_computation | async-start | bytes 1310720 | tf_op jit(solution)/shard_map/all_to_all | solution.py:197
  58.4 12.4 %copy-start.4 = (bf16[256,1024]{1,0:T(8,128)(2,1)S(1)}, bf16[256,1024]{1,0:T(8,128)(2,1)}, u32[]{:S(2)}) copy-start(bf16[256,1024]{1,0:T(8,128)(2,1)} %param.11) | copy-start | bytes 1572868
  59.5 28.9 %all-to-all-start.1 = ((f32[32,32,128]{2,1,0:T(8,128)}), f32[32,32,128]{2,1,0:T(8,128)S(1)}, u32[]{:S(2)}, u32[]{:S(2)}) async-start(f32[32,32,128]{2,1,0:T(8,128)} %copy.35), calls=%async_computation.1 | async-start | bytes 1048576 | tf_op jit(solution)/shard_map/all_to_all | solution.py:209
  88.5 15.5 %copy-start.2 = (f32[1024]{0:T(1024)S(1)}, f32[1024]{0:T(1024)}, u32[]{:S(2)}) copy-start(f32[1024]{0:T(1024)} %param.13) | copy-start | bytes 12292
Sparse Core Ops, SparseCore 0:
  10.6 90.3 all-gather.1

commit v18 on v14

--- a/solution.py
+++ b/solution.py
@@ -8,7 +8,7 @@
 from jax.sharding import PartitionSpec as P
 
 BLOCK = 256
-KEY_BLOCK = 1024
+KEY_BLOCK = 2048
 
 
 def flash_body(sref, q_ref, k_ref, v_ref, st_ref, o_ref, m_ref, l_ref, acc_ref, vx_ref, *, heads, width, scale):

time: 141 us -> 143 us (1.014)
  the two profiles are of different devices: /device:TPU:228 before, /device:TPU:196 now
where the time goes in v18:
time: 143 us; the launch traced here: 142 us
  waiting for transfers between devices  32.6 us (23%)
  Pallas kernels  30.7 us (21%)
  between operations  20.2 us (14%)
  starting transfers between devices  18.2 us (13%)
  blocking collectives  13.6 us (10%)
  other arithmetic  12.5 us (9%)
  local copies, waits for them, and re-layouts  7.89 us (6%)
  matrix products  6.61 us (5%)
    pallas_call x1, Pallas kernels, flash_attention(): pl.pallas_call(kernel, out_shape=jax.ShapeDtypeStruct((rows, total), jnp....  30.7 us
    all_to_all x1, waiting for transfers between devices, body(): sent = lax.all_to_all(jnp.concatenate([chunks, info], axis=1), 'seq', 0, 0)  17.8 us
    all_to_all x1, waiting for transfers between devices, body(): state_in = lax.all_to_all(mixed, 'seq', 0, 0).reshape(heads, width, width)  14.9 us
    psum x1, blocking collectives, body(): total_sq = lax.psum(sums, 'heads')  13.6 us
    all_to_all x1, starting transfers between devices, body(): state_in = lax.all_to_all(mixed, 'seq', 0, 0).reshape(heads, width, width)  9.28 us
    all_to_all x1, starting transfers between devices, body(): sent = lax.all_to_all(jnp.concatenate([chunks, info], axis=1), 'seq', 0, 0)  8.91 us
  transfers between devices with their start and end apart: 3, of which 2 were waited for; matrix products, arithmetic and copies ran while one was open for 18% of the time, Pallas kernels for 0%

profile of v18, /device:TPU:196, one launch (start us, length us, event | category | flops | bytes accessed | tf_op | source)
XLA Modules:
  0.0 142.3 jit_solution(11286241102533988497)
XLA Ops:
  7.2 0.0 copy-start
  7.2 0.0 all-gather.2.cloned.1.call-start
  7.2 1.6 %pad_maximum_fusion.1 = bf16[256,256]{1,0:T(8,128)(2,1)} fusion(bf16[256,128]{1,0:T(8,128)(2,1)} %param.16, bf16[256,128]{1,0:T(8,128)(2,1)} %param.15), kind=kLoop, calls=%fused_computation.36 | loop fusion | flops 262144 | bytes 262144 | tf_op jit(solution)/shard_map/concatenate | solution.py:150
  8.8 0.0 all-gather.2.cloned.1.call-update
  8.8 0.7 convert_element_type.86
  9.5 0.6 slice.36
  10.1 2.0 %fusion.46 = s32[]{:T(128)} fusion(f32[]{:T(128)} %bitcast.2, s32[256]{0:T(256)} %param.17), kind=kLoop, calls=%fused_computation.68 | loop fusion | flops 1023 | bytes 1032 | tf_op jit(solution)/shard_map/reduce_sum | solution.py:175
  12.7 1.2 copy.42
  14.6 0.6 compare_select_fusion.1
  15.3 0.7 multiply_multiply_fusion
  15.9 1.3 compare_convert_fusion.1
  17.3 0.1 exponential_multiply_fusion
  17.3 1.4 convolution_add_fusion
  18.7 0.9 pad_maximum_fusion
  19.6 8.9 %all-to-all-start = ((f32[32,40,128]{2,1,0:T(8,128)}), f32[32,40,128]{2,1,0:T(8,128)S(1)}, u32[]{:S(2)}, u32[]{:S(2)}) async-start(f32[32,40,128]{2,1,0:T(8,128)} %pad_maximum_fusion), calls=%async_computation | async-start | bytes 1310720 | tf_op jit(solution)/shard_map/all_to_all | solution.py:181
  28.6 0.0 copy-done.3
  28.6 0.6 dynamic_slice.17
  29.9 0.2 convert_reduce_fusion
  30.0 0.2 fusion.26
  30.2 0.1 subtract_maximum_fusion
  30.3 17.8 %all-to-all-done = f32[32,40,128]{2,1,0:T(8,128)S(1)} async-done(((f32[32,40,128]{2,1,0:T(8,128)}), f32[32,40,128]{2,1,0:T(8,128)S(1)}, u32[]{:S(2)}, u32[]{:S(2)}) %all-to-all-start) | async-done | bytes 655392 | tf_op jit(solution)/shard_map/all_to_all | solution.py:181
  48.1 0.5 slice.46
  48.6 0.3 slice_reduce_fusion.2
  48.9 0.7 compare_select_fusion.2
  49.6 0.6 dynamic_slice.16
  50.2 0.6 slice_reduce_fusion
  50.8 1.2 fusion.49
  52.7 0.0 copy-done.1
  52.7 0.6 add_select_fusion
  53.3 0.6 fusion.55
  57.2 0.1 slice.49
  57.3 0.9 fusion.16
  58.2 0.0 copy-start.4
  58.2 1.1 copy.35
  59.3 9.3 %all-to-all-start.1 = ((f32[32,32,128]{2,1,0:T(8,128)}), f32[32,32,128]{2,1,0:T(8,128)S(1)}, u32[]{:S(2)}, u32[]{:S(2)}) async-start(f32[32,32,128]{2,1,0:T(8,128)} %copy.35), calls=%async_computation.1 | async-start | bytes 1048576 | tf_op jit(solution)/shard_map/all_to_all | solution.py:193
  68.6 0.8 copy.39.refs_4_
  69.4 0.6 stack.23.refs_0_
  70.0 0.6 fusion.54
  70.6 0.1 fusion.43
  70.7 0.0 copy-done
  70.7 0.6 fusion.5
  71.3 1.8 %fusion.2 = f32[256,8,128]{0,2,1:T(8,128)} fusion(f32[256,8,128]{0,2,1:T(8,128)S(1)} %fusion.5, bf16[256,8,128]{0,2,1:T(8,128)(2,1)S(1)} %bitcast.71, f32[256,256]{1,0:T(8,128)S(1)} %subtract_maximum_fusion, f32[8]{0:T(128)S(1)} %get-tuple-element.46, pred[256,256]{1,0:T(8,128)(4,1)S(1)} %fusion.26, bf16[256,1024]{1,0:T(8,128)(2,1)S(1)} %copy-done, ...), kind=kOutput, calls=%fused_computation.3 | convolution fusion | flops 270794752 | bytes 3997728 | tf_op jit(solution)/shard_map/while/body/eval_jaxpr/hts,shd->thd/dot_general | solution.py:129
  73.1 14.9 %all-to-all-done.1 = f32[32,32,128]{2,1,0:T(8,128)S(1)} async-done(((f32[32,32,128]{2,1,0:T(8,128)}), f32[32,32,128]{2,1,0:T(8,128)S(1)}, u32[]{:S(2)}, u32[]{:S(2)}) %all-to-all-start.1) | async-done | bytes 524320 | tf_op jit(solution)/shard_map/all_to_all | solution.py:193
  88.0 2.0 %multiply_reduce_fusion = (f32[256]{0:T(256)S(1)}, f32[256,8,128]{0,2,1:T(8,128)S(1)}) fusion(f32[256,8,128]{0,2,1:T(8,128)} %fusion.2, f32[8,128,128]{2,1,0:T(8,128)S(1)} %bitcast.69, f32[256,8]{0,1:T(8,128)S(1)} %get-tuple-element.39, bf16[256,1024]{1,0:T(8,128)(2,1)S(1)} %copy-done), kind=kOutput, calls=%fused_computation.11 | convolution fusion | flops 403701504 | bytes 3154944 | tf_op jit(solution)/shard_map/thd,hde->the/dot_general | solution.py:205
  89.9 0.3 copy.38
  90.3 13.6 %psum.7 = f32[256]{0:T(256)S(1)} all-reduce(f32[256]{0:T(256)S(1)} %get-tuple-element.47), channel_id=1, replica_groups=mesh['seq'=32,'heads'=8] {'heads'}, use_global_device_ids=true, to_apply=%region_2.3 | all-reduce | flops 256 | bytes 2048 | tf_op jit(solution)/shard_map/psum | solution.py:210
  103.8 1.0 multiply_convert_fusion
  104.8 30.7 %shard_map.104 = bf16[256,1024]{1,0:T(8,128)(2,1)} custom-call(s32[5]{0:T(128)} %stack.23.refs_0_, bf16[256,1024]{1,0:T(8,128)(2,1)} %refs_1_.1, bf16[8192,256]{1,0:T(8,128)(2,1)} %all-gather.2.cloned.1.call-done.refs_2_.refs_3_, bf16[8192,256]{1,0:T(8,128)(2,1)} %all-gather.2.cloned.1.call-done.refs_2_.refs_3_, s32[256,1]{1,0:T(8,128)} %copy.39.refs_4_), custom_call_target="tpu_custom_call" | custom-call | flops 4294967296 | bytes 5242880 | tf_op jit(solution)/shard_map/pallas_call | solution.py:89
  (12 shorter events, 0.0 us)
Async XLA Ops:
  7.2 63.5 %copy-start = (bf16[256,1024]{1,0:T(8,128)(2,1)S(1)}, bf16[256,1024]{1,0:T(8,128)(2,1)}, u32[]{:S(2)}) copy-start(bf16[256,1024]{1,0:T(8,128)(2,1)} %param.9) | copy-start | bytes 1572868
  7.2 97.6 %all-gather.2.cloned.1.call-start = ((), (), s32[]{:S(2)}) async-start(), calls=%async_computation.2 | async-start | bytes 4325376 | tf_op jit(solution)/shard_map/all_gather | solution.py:152
  17.3 11.2 %copy-start.3 = (f32[8]{0:T(128)S(1)}, f32[8]{0:T(128)}, u32[]{:S(2)}) copy-start(f32[8]{0:T(128)} %param.12) | copy-start | bytes 100
  17.3 35.3 %copy-start.1 = (s32[256]{0:T(256)S(1)}, s32[256]{0:T(256)}, u32[]{:S(2)}) copy-start(s32[256]{0:T(256)} %param.17) | copy-start | bytes 3076
  19.6 28.4 %all-to-all-start = ((f32[32,40,128]{2,1,0:T(8,128)}), f32[32,40,128]{2,1,0:T(8,128)S(1)}, u32[]{:S(2)}, u32[]{:S(2)}) async-start(f32[32,40,128]{2,1,0:T(8,128)} %pad_maximum_fusion), calls=%async_computation | async-start | bytes 1310720 | tf_op jit(solution)/shard_map/all_to_all | solution.py:181
  58.2 13.1 %copy-start.4 = (bf16[256,1024]{1,0:T(8,128)(2,1)S(1)}, bf16[256,1024]{1,0:T(8,128)(2,1)}, u32[]{:S(2)}) copy-start(bf16[256,1024]{1,0:T(8,128)(2,1)} %param.11) | copy-start | bytes 1572868
  59.3 28.7 %all-to-all-start.1 = ((f32[32,32,128]{2,1,0:T(8,128)}), f32[32,32,128]{2,1,0:T(8,128)S(1)}, u32[]{:S(2)}, u32[]{:S(2)}) async-start(f32[32,32,128]{2,1,0:T(8,128)} %copy.35), calls=%async_computation.1 | async-start | bytes 1048576 | tf_op jit(solution)/shard_map/all_to_all | solution.py:193
  88.0 15.9 %copy-start.2 = (f32[1024]{0:T(1024)S(1)}, f32[1024]{0:T(1024)}, u32[]{:S(2)}) copy-start(f32[1024]{0:T(1024)} %param.13) | copy-start | bytes 12292
Sparse Core Ops, SparseCore 0:
  10.6 90.1 all-gather.1

commit v19 on v18

--- a/solution.py
+++ b/solution.py
@@ -8,7 +8,7 @@
 from jax.sharding import PartitionSpec as P
 
 BLOCK = 256
-KEY_BLOCK = 2048
+KEY_BLOCK = 4096
 
 
 def flash_body(sref, q_ref, k_ref, v_ref, st_ref, o_ref, m_ref, l_ref, acc_ref, vx_ref, *, heads, width, scale):

time: 143 us -> 142 us (level)
  the two profiles are of different devices: /device:TPU:196 before, /device:TPU:128 now
where the time goes in v19:
time: 142 us; the launch traced here: 141 us
  waiting for transfers between devices  32.8 us (23%)
  Pallas kernels  28.7 us (20%)
  between operations  20.2 us (14%)
  starting transfers between devices  18.6 us (13%)
  blocking collectives  13.3 us (9%)
  other arithmetic  12.5 us (9%)
  local copies, waits for them, and re-layouts  7.88 us (6%)
  matrix products  6.62 us (5%)
    pallas_call x1, Pallas kernels, flash_attention(): pl.pallas_call(kernel, out_shape=jax.ShapeDtypeStruct((rows, total), jnp....  28.7 us
    all_to_all x1, waiting for transfers between devices, body(): sent = lax.all_to_all(jnp.concatenate([chunks, info], axis=1), 'seq', 0, 0)  18.3 us
    all_to_all x1, waiting for transfers between devices, body(): state_in = lax.all_to_all(mixed, 'seq', 0, 0).reshape(heads, width, width)  14.4 us
    psum x1, blocking collectives, body(): total_sq = lax.psum(sums, 'heads')  13.3 us
    all_to_all x1, starting transfers between devices, body(): sent = lax.all_to_all(jnp.concatenate([chunks, info], axis=1), 'seq', 0, 0)  9.83 us
    all_to_all x1, starting transfers between devices, body(): state_in = lax.all_to_all(mixed, 'seq', 0, 0).reshape(heads, width, width)  8.71 us
  transfers between devices with their start and end apart: 3, of which 2 were waited for; matrix products, arithmetic and copies ran while one was open for 18% of the time, Pallas kernels for 0%

profile of v19, /device:TPU:128, one launch (start us, length us, event | category | flops | bytes accessed | tf_op | source)
XLA Modules:
  0.0 140.6 jit_solution(8158484321098490242)
XLA Ops:
  7.2 0.0 copy-start
  7.2 0.0 all-gather.2.cloned.1.call-start
  7.2 1.6 %pad_maximum_fusion.1 = bf16[256,256]{1,0:T(8,128)(2,1)} fusion(bf16[256,128]{1,0:T(8,128)(2,1)} %param.16, bf16[256,128]{1,0:T(8,128)(2,1)} %param.15), kind=kLoop, calls=%fused_computation.36 | loop fusion | flops 262144 | bytes 262144 | tf_op jit(solution)/shard_map/concatenate | solution.py:150
  8.8 0.0 all-gather.2.cloned.1.call-update
  8.8 0.7 convert_element_type.86
  9.5 0.6 slice.36
  10.1 2.0 %fusion.46 = s32[]{:T(128)} fusion(f32[]{:T(128)} %bitcast.2, s32[256]{0:T(256)} %param.17), kind=kLoop, calls=%fused_computation.68 | loop fusion | flops 1023 | bytes 1032 | tf_op jit(solution)/shard_map/reduce_sum | solution.py:175
  12.7 1.2 copy.42
  14.6 0.6 compare_select_fusion.1
  15.3 0.7 multiply_multiply_fusion
  15.9 1.3 compare_convert_fusion.1
  17.3 0.1 exponential_multiply_fusion
  17.3 1.4 convolution_add_fusion
  18.7 0.9 pad_maximum_fusion
  19.6 9.8 %all-to-all-start = ((f32[32,40,128]{2,1,0:T(8,128)}), f32[32,40,128]{2,1,0:T(8,128)S(1)}, u32[]{:S(2)}, u32[]{:S(2)}) async-start(f32[32,40,128]{2,1,0:T(8,128)} %pad_maximum_fusion), calls=%async_computation | async-start | bytes 1310720 | tf_op jit(solution)/shard_map/all_to_all | solution.py:181
  29.5 0.0 copy-done.3
  29.5 0.6 dynamic_slice.17
  30.8 0.2 convert_reduce_fusion
  31.0 0.1 fusion.26
  31.1 0.1 subtract_maximum_fusion
  31.2 18.3 %all-to-all-done = f32[32,40,128]{2,1,0:T(8,128)S(1)} async-done(((f32[32,40,128]{2,1,0:T(8,128)}), f32[32,40,128]{2,1,0:T(8,128)S(1)}, u32[]{:S(2)}, u32[]{:S(2)}) %all-to-all-start) | async-done | bytes 655392 | tf_op jit(solution)/shard_map/all_to_all | solution.py:181
  49.6 0.5 slice.46
  50.1 0.3 slice_reduce_fusion.2
  50.4 0.7 compare_select_fusion.2
  51.1 0.6 dynamic_slice.16
  51.7 0.6 slice_reduce_fusion
  52.3 1.2 fusion.49
  54.2 0.6 add_select_fusion
  54.8 0.6 fusion.55
  58.7 0.1 slice.49
  58.8 0.9 fusion.16
  59.7 0.0 copy-start.4
  59.7 1.1 copy.35
  60.8 8.7 %all-to-all-start.1 = ((f32[32,32,128]{2,1,0:T(8,128)}), f32[32,32,128]{2,1,0:T(8,128)S(1)}, u32[]{:S(2)}, u32[]{:S(2)}) async-start(f32[32,32,128]{2,1,0:T(8,128)} %copy.35), calls=%async_computation.1 | async-start | bytes 1048576 | tf_op jit(solution)/shard_map/all_to_all | solution.py:193
  69.5 0.8 copy.39.refs_4_
  70.3 0.6 stack.23.refs_0_
  70.9 0.6 fusion.54
  71.5 0.1 fusion.43
  71.6 0.0 copy-done
  71.6 0.6 fusion.5
  72.2 1.8 %fusion.2 = f32[256,8,128]{0,2,1:T(8,128)} fusion(f32[256,8,128]{0,2,1:T(8,128)S(1)} %fusion.5, bf16[256,8,128]{0,2,1:T(8,128)(2,1)S(1)} %bitcast.71, f32[256,256]{1,0:T(8,128)S(1)} %subtract_maximum_fusion, f32[8]{0:T(128)S(1)} %get-tuple-element.46, pred[256,256]{1,0:T(8,128)(4,1)S(1)} %fusion.26, bf16[256,1024]{1,0:T(8,128)(2,1)S(1)} %copy-done, ...), kind=kOutput, calls=%fused_computation.3 | convolution fusion | flops 270794752 | bytes 3997728 | tf_op jit(solution)/shard_map/while/body/eval_jaxpr/hts,shd->thd/dot_general | solution.py:129
  74.0 14.4 %all-to-all-done.1 = f32[32,32,128]{2,1,0:T(8,128)S(1)} async-done(((f32[32,32,128]{2,1,0:T(8,128)}), f32[32,32,128]{2,1,0:T(8,128)S(1)}, u32[]{:S(2)}, u32[]{:S(2)}) %all-to-all-start.1) | async-done | bytes 524320 | tf_op jit(solution)/shard_map/all_to_all | solution.py:193
  88.5 2.0 %multiply_reduce_fusion = (f32[256]{0:T(256)S(1)}, f32[256,8,128]{0,2,1:T(8,128)S(1)}) fusion(f32[256,8,128]{0,2,1:T(8,128)} %fusion.2, f32[8,128,128]{2,1,0:T(8,128)S(1)} %bitcast.69, f32[256,8]{0,1:T(8,128)S(1)} %get-tuple-element.39, bf16[256,1024]{1,0:T(8,128)(2,1)S(1)} %copy-done), kind=kOutput, calls=%fused_computation.11 | convolution fusion | flops 403701504 | bytes 3154944 | tf_op jit(solution)/shard_map/thd,hde->the/dot_general | solution.py:205
  90.4 0.3 copy.38
  90.8 13.3 %psum.7 = f32[256]{0:T(256)S(1)} all-reduce(f32[256]{0:T(256)S(1)} %get-tuple-element.47), channel_id=1, replica_groups=mesh['seq'=32,'heads'=8] {'heads'}, use_global_device_ids=true, to_apply=%region_2.3 | all-reduce | flops 256 | bytes 2048 | tf_op jit(solution)/shard_map/psum | solution.py:210
  104.1 0.0 copy-done.2
  104.1 1.0 multiply_convert_fusion
  105.0 28.7 %shard_map.104 = bf16[256,1024]{1,0:T(8,128)(2,1)} custom-call(s32[5]{0:T(128)} %stack.23.refs_0_, bf16[256,1024]{1,0:T(8,128)(2,1)} %refs_1_.1, bf16[8192,256]{1,0:T(8,128)(2,1)} %all-gather.2.cloned.1.call-done.refs_2_.refs_3_, bf16[8192,256]{1,0:T(8,128)(2,1)} %all-gather.2.cloned.1.call-done.refs_2_.refs_3_, s32[256,1]{1,0:T(8,128)} %copy.39.refs_4_), custom_call_target="tpu_custom_call" | custom-call | flops 4294967296 | bytes 5242880 | tf_op jit(solution)/shard_map/pallas_call | solution.py:89
  (12 shorter events, 0.0 us)
Async XLA Ops:
  7.2 64.4 %copy-start = (bf16[256,1024]{1,0:T(8,128)(2,1)S(1)}, bf16[256,1024]{1,0:T(8,128)(2,1)}, u32[]{:S(2)}) copy-start(bf16[256,1024]{1,0:T(8,128)(2,1)} %param.9) | copy-start | bytes 1572868
  7.2 97.8 %all-gather.2.cloned.1.call-start = ((), (), s32[]{:S(2)}) async-start(), calls=%async_computation.2 | async-start | bytes 4325376 | tf_op jit(solution)/shard_map/all_gather | solution.py:152
  17.3 12.2 %copy-start.3 = (f32[8]{0:T(128)S(1)}, f32[8]{0:T(128)}, u32[]{:S(2)}) copy-start(f32[8]{0:T(128)} %param.12) | copy-start | bytes 100
  17.3 36.8 %copy-start.1 = (s32[256]{0:T(256)S(1)}, s32[256]{0:T(256)}, u32[]{:S(2)}) copy-start(s32[256]{0:T(256)} %param.17) | copy-start | bytes 3076
  19.6 29.9 %all-to-all-start = ((f32[32,40,128]{2,1,0:T(8,128)}), f32[32,40,128]{2,1,0:T(8,128)S(1)}, u32[]{:S(2)}, u32[]{:S(2)}) async-start(f32[32,40,128]{2,1,0:T(8,128)} %pad_maximum_fusion), calls=%async_computation | async-start | bytes 1310720 | tf_op jit(solution)/shard_map/all_to_all | solution.py:181
  59.7 12.5 %copy-start.4 = (bf16[256,1024]{1,0:T(8,128)(2,1)S(1)}, bf16[256,1024]{1,0:T(8,128)(2,1)}, u32[]{:S(2)}) copy-start(bf16[256,1024]{1,0:T(8,128)(2,1)} %param.11) | copy-start | bytes 1572868
  60.8 27.7 %all-to-all-start.1 = ((f32[32,32,128]{2,1,0:T(8,128)}), f32[32,32,128]{2,1,0:T(8,128)S(1)}, u32[]{:S(2)}, u32[]{:S(2)}) async-start(f32[32,32,128]{2,1,0:T(8,128)} %copy.35), calls=%async_computation.1 | async-start | bytes 1048576 | tf_op jit(solution)/shard_map/all_to_all | solution.py:193
  88.4 15.6 %copy-start.2 = (f32[1024]{0:T(1024)S(1)}, f32[1024]{0:T(1024)}, u32[]{:S(2)}) copy-start(f32[1024]{0:T(1024)} %param.13) | copy-start | bytes 12292
Sparse Core Ops, SparseCore 0:
  10.6 91.0 all-gather.1
